TPU v7x, 32 devices: a whole 2x2x4 slice. The times are simulated.
32 devices in a mesh: grp: 2 (over y), ex: 4 (over z), col: 4 (over x, core).
Axes of the slice: x: 2, y: 2, z: 4, core: 2. Of those that a mesh axis runs over, the one named last changes fastest.
Arguments:
- hidden_input: bfloat16 [8, 2, 256, 5120], P(('grp', 'ex'), None, None, 'col'), parts along dimension 0, may hold values from -6 to 6
- output_gradient: bfloat16 [8, 2, 256, 5120], P(('grp', 'ex'), None, None, 'col'), parts along dimension 0, may hold values from -11 to 11
- lengths: int32 [8], P(('grp', 'ex')), parts along dimension 0, may hold values from 64 to 256
- adapter_down: bfloat16 [2, 128, 5120], P(None, None, 'col'), may hold values from -0.078125 to 0.078125
- adapter_up: bfloat16 [2, 5120, 128], P(None, 'col'), may hold values from -0.078125 to 0.078125
- left_sign_words: int32 [2, 2, 32, 5120], P(None, None, None, 'col'), may hold values from 0 to 65535
- right_sign_words: int32 [2, 2, 128, 4], replicated, may hold values from 0 to 1
- targets: float32 [512, 8192], P(('grp', 'ex'), 'col'), parts along dimension 0, may hold values from -40 to 40
Outputs:
- gradient_features: float32 [8, 8192], P(('grp', 'ex'), 'col'), parts along dimension 0
- scores: float32 [8, 256], P(('grp', 'ex'), 'col'), parts along dimension 0
There are 2 independent parts, one for each index of `grp`. A program takes and returns all parts, laid end to end along the dimension named above; an argument that names none is the same for every part. Nothing has to cross between parts.
Inputs may be any that keep to these rules, and one draw needn't show every extreme that they name: `left_sign_words`: each word holds 16 independent bits.
All inputs are finite; a program needn't handle non-finite values.
Results may differ from a plain program's by a relative error of at most 0.0003.
Values sent between devices are 32-bit elements; how exact they have to be, the bound alone decides.
No kernel may reach another device: no remote copies, remote signals or barrier semaphores. Data moves between devices by JAX's collectives and lax.ppermute only.
A program may use at most 64 MiB of HBM per device.

v0:
```python
import math

import jax
import jax.numpy as jnp
from jax import lax
from jax.sharding import PartitionSpec as P

ADAPTED_LAYERS = 2
K_LEFT = 512
COLS = 8192


epsilon = 1e-06
highest_precision = lax.Precision.HIGHEST


def unpack(packed):
    shifts = jnp.arange(16, dtype=jnp.int32)
    bit_values = jnp.right_shift(packed[..., :, None, :], shifts[:, None]) & 1
    shape_out = packed.shape[:-2] + (packed.shape[-2] * 16, packed.shape[-1])
    return (2 * bit_values - 1).reshape(shape_out)


def on_device(
    hidden_input,
    output_gradient,
    lengths,
    adapter_down,
    adapter_up,
    left_sign_words,
    right_sign_words,
    targets,
):
    examples = hidden_input.shape[0]
    positions = jnp.arange(hidden_input.shape[2], dtype=jnp.int32)
    token_weights = jnp.where(positions[None, :] < lengths[:, None], 1.0, 0.0).astype(
        jnp.float32
    ) / lengths[:, None].astype(jnp.float32)
    left_signs = unpack(left_sign_words).astype(jnp.bfloat16)
    right_signs = (2 * right_sign_words - 1).astype(jnp.float32)
    blocks = []
    for index_of_layer in range(ADAPTED_LAYERS):
        input_rows = hidden_input[:, index_of_layer]
        gradient_value = output_gradient[:, index_of_layer]
        shrunk_input = jnp.einsum(
            "aom,cm->aoc",
            input_rows,
            adapter_down[index_of_layer],
            preferred_element_type=jnp.float32,
        )
        shrunk_gradient = jnp.einsum(
            "wvl,lz->wvz",
            gradient_value,
            adapter_up[index_of_layer],
            preferred_element_type=jnp.float32,
        )
        shrunk_input, shrunk_gradient = lax.psum((shrunk_input, shrunk_gradient), "col")
        mixed_b = (
            jnp.einsum(
                "esr,rm->esm",
                shrunk_input,
                right_signs[index_of_layer, 0],
                precision=highest_precision,
            )
            * token_weights[:, :, None]
        )
        mixed_a = (
            jnp.einsum(
                "esr,rm->esm",
                shrunk_gradient,
                right_signs[index_of_layer, 1],
                precision=highest_precision,
            )
            * token_weights[:, :, None]
        )
        signed_grad = jnp.einsum(
            "esd,kd->esk",
            gradient_value,
            left_signs[index_of_layer, 0],
            preferred_element_type=jnp.float32,
        )
        signed_input = jnp.einsum(
            "esd,kd->esk",
            input_rows,
            left_signs[index_of_layer, 1],
            preferred_element_type=jnp.float32,
        )
        block_b = jnp.einsum("esm,esk->emk", mixed_b, signed_grad, precision=highest_precision)
        block_a = jnp.einsum("esm,esk->emk", mixed_a, signed_input, precision=highest_precision)
        blocks.append(jnp.stack([block_b, block_a], axis=1))
    sketch_part = jnp.stack(blocks, axis=1).reshape(examples, -1, K_LEFT)
    own_columns = lax.psum_scatter(sketch_part, "col", scatter_dimension=1, tiled=True)
    cand_squares = lax.psum(jnp.sum(own_columns * own_columns, axis=(1, 2)), "col")
    gradient_features = (
        own_columns * lax.rsqrt(cand_squares / COLS + epsilon)[:, None, None]
    ).reshape(examples, -1)
    target_squares = lax.psum(jnp.sum(targets * targets, axis=1), "col")
    target_units = targets * lax.rsqrt(target_squares / COLS + epsilon)[:, None]
    by_target = jnp.dot(
        lax.all_gather(gradient_features, "ex", axis=0, tiled=True),
        target_units.T,
        precision=highest_precision,
    )
    partial_scores = lax.all_to_all(by_target, "ex", split_axis=0, concat_axis=1, tiled=True)
    scores = lax.psum_scatter(partial_scores, "col", scatter_dimension=1, tiled=True) / math.sqrt(
        COLS
    )
    return (gradient_features, scores)


def solution(mesh):
    return jax.shard_map(
        on_device,
        mesh=mesh,
        in_specs=(
            P(("grp", "ex"), None, None, "col"),
            P(("grp", "ex"), None, None, "col"),
            P(("grp", "ex")),
            P(None, None, "col"),
            P(None, "col", None),
            P(None, None, None, "col"),
            P(),
            P(("grp", "ex"), "col"),
        ),
        out_specs=(P(("grp", "ex"), "col"), P(("grp", "ex"), "col")),
        check_vma=False,
    )
```

profile of v0, /device:TPU:0, one launch (start us, length us, event | category | flops | bytes accessed | tf_op | source)
XLA Modules:
  0.0 127.5 jit_solution(15626251608258976946)
XLA Ops:
  7.2 0.0 copy-start.5
  7.2 0.0 copy-start.4
  7.2 0.0 all-reduce.5.cloned.1.call-start
  7.2 2.3 %fusion.12 = f32[256,128]{1,0:T(8,128)} fusion(bf16[1,2,256,1280]{3,2,1,0:T(8,128)(2,1)} %param.8, bf16[2,128,1280]{2,1,0:T(8,128)(2,1)} %param.11), kind=kOutput, calls=%fused_computation.25 | convolution fusion | flops 83886080 | bytes 1114112 | tf_op jit(solution)/shard_map/aom,cm->aoc/dot_general | solution.py:45
  9.5 0.0 copy-done.5
  9.5 0.0 copy-start.7
  9.5 2.0 %fusion.18 = f32[256,128]{1,0:T(8,128)} fusion(bf16[1,2,256,1280]{3,2,1,0:T(8,128)(2,1)S(1)} %copy-done.5, bf16[2,128,1280]{2,1,0:T(8,128)(2,1)} %param.11), kind=kOutput, calls=%fused_computation.31 | convolution fusion | flops 83886080 | bytes 1114112 | tf_op jit(solution)/shard_map/aom,cm->aoc/dot_general | solution.py:45
  11.6 0.0 copy-done.4
  11.6 0.0 copy-start.2
  11.6 2.0 %fusion.14 = f32[256,128]{1,0:T(8,128)} fusion(bf16[1,2,256,1280]{3,2,1,0:T(8,128)(2,1)S(1)} %copy-done.4, bf16[2,1280,128]{2,1,0:T(8,128)(2,1)} %param.12), kind=kOutput, calls=%fused_computation.27 | convolution fusion | flops 83886080 | bytes 1114112 | tf_op jit(solution)/shard_map/wvl,lz->wvz/dot_general | solution.py:51
  13.6 0.0 copy-done.7
  13.6 1.0 fusion.8
  14.6 0.0 all-reduce.5.cloned.1.call-update
  14.6 0.0 reduce-scatter.5.cloned.1.call-start
  14.7 0.1 shift_right_arithmetic.23
  14.7 0.0 copy-done.2
  14.7 0.0 copy-start.6
  14.7 2.5 %fusion.3 = bf16[2,2,512,1280]{3,2,1,0:T(8,128)(2,1)S(1)} fusion(s32[512]{0:T(512)S(1)} %shift_right_arithmetic.23, s32[2,2,32,1280]{3,2,1,0:T(8,128)S(1)} %copy-done.2), kind=kLoop, calls=%fused_computation.4 | loop fusion | flops 13107200 | bytes 5900288 | tf_op jit(solution)/shard_map/convert_element_type | solution.py:39
  17.2 0.0 copy-done.6
  17.3 0.0 copy-start
  17.3 0.5 fusion.4
  17.8 0.5 fusion.5
  18.4 1.2 copy-done
  19.6 0.0 copy-start.3
  19.6 0.0 copy-start.1
  19.6 0.0 copy-start.8
  19.6 0.5 fusion.7
  20.8 0.0 copy-done.3
  20.8 0.0 copy-done.1
  20.8 0.1 multiply_reduce_fusion
  21.0 0.0 copy-done.8
  21.0 0.6 dynamic-slice
  22.2 2.1 %fusion.6 = f32[512,256]{1,0:T(8,128)S(1)} fusion(bf16[2,2,512,1280]{3,2,1,0:T(8,128)(2,1)} %copy-done, bf16[1,2,256,1280]{3,2,1,0:T(8,128)(2,1)} %param.8), kind=kOutput, calls=%fused_computation.10 | convolution fusion | flops 335544320 | bytes 2490368 | tf_op jit(solution)/shard_map/esd,kd->esk/dot_general | solution.py:82
  24.3 27.0 %all-reduce.5.cloned.1.call-done = (f32[256,128]{1,0:T(8,128)}, f32[256,128]{1,0:T(8,128)}, f32[256,128]{1,0:T(8,128)}, f32[256,128]{1,0:T(8,128)}) async-done(((f32[256,128]{1,0:T(8,128)}, f32[256,128]{1,0:T(8,128)}, f32[256,128]{1,0:T(8,128)}, f32[256,128]{1,0:T(8,128)}), (f32[256,128]{1,0:T(8,128)}, f32[256,128]{1,0:T(8,128)}, f32[256,128]{1,0:T(8,128)}, ...) | async-done | bytes 524304 | tf_op jit(solution)/shard_map/psum | solution.py:57
  51.2 1.1 convolution_multiply_fusion
  52.3 1.1 convolution_multiply_fusion.1
  53.5 1.1 convolution_multiply_fusion.3
  54.6 1.1 convolution_multiply_fusion.2
  55.7 0.6 convolution_bitcast_fusion
  56.3 0.5 convolution_bitcast_fusion.1
  56.8 0.5 convolution_bitcast_fusion.3
  57.3 0.5 convolution_bitcast_fusion.2
  57.9 10.3 %all-reduce = f32[1,16,512]{2,1,0:T(8,128)S(1)} all-reduce(f32[1,16,512]{2,1,0:T(8,128)S(1)} %reshape.128), channel_id=2, replica_groups=mesh['grp'=2,'ex'=4,'col'=4] {'col'}, use_global_device_ids=true, to_apply=%region_4.5.clone | all-reduce | flops 8192 | bytes 65536
  68.2 0.6 multiply_reduce_fusion.1
  68.8 6.4 %all-reduce.1 = (f32[1]{0:T(128)}, f32[64]{0:T(128)S(1)}) all-reduce(f32[1]{0:T(128)} %bitcast.25, f32[64]{0:T(128)S(1)} %multiply_reduce_fusion), channel_id=1, replica_groups=mesh['grp'=2,'ex'=4,'col'=4] {'col'}, use_global_device_ids=true, to_apply=%region_6.7 | all-reduce | flops 65 | bytes 520 | tf_op jit(solution)/shard_map/psum | solution.py:93
  75.9 13.3 %all-gather = f32[4,1,2048]{2,1,0:T(1,128)S(1)} all-gather(f32[1,1,2048]{2,1,0:T(1,128)S(1)} %reshape.134), channel_id=1, replica_groups=mesh['grp'=2,'ex'=4,'col'=4] {'ex'}, dimensions={0}, use_global_device_ids=true | all-gather | bytes 40960 | tf_op jit(solution)/shard_map/all_gather | solution.py:100
  89.2 0.6 fusion.28
  89.8 9.9 %all_to_all.17 = f32[4,1,64]{2,1,0:T(1,128)S(1)} all-to-all(f32[4,1,64]{2,1,0:T(1,128)S(1)} %bitcast.111), channel_id=1, replica_groups=mesh['grp'=2,'ex'=4,'col'=4] {'ex'}, dimensions={0} | all-to-all | bytes 2048 | tf_op jit(solution)/shard_map/all_to_all | solution.py:104
  99.7 0.5 broadcast.60
  100.2 0.7 reduce.4
  100.9 0.8 all_to_all.15
  101.7 0.0 reduce-scatter.5.cloned.1.call-update
  101.7 0.6 copy.16
  102.3 17.0 %reduce-scatter.5.cloned.1.call-done = f32[64,1]{1,0:T(8,128)} async-done(((f32[256,1]{1,0:T(8,128)}), f32[64,1]{1,0:T(8,128)}) %reduce-scatter.5.cloned.1.call-update) | async-done | bytes 272
  119.4 0.8 copy.14
  120.2 0.5 broadcast_multiply_fusion
  (10 shorter events, 0.1 us)
Async XLA Ops:
  7.2 2.4 %copy-start.5 = (bf16[1,2,256,1280]{3,2,1,0:T(8,128)(2,1)S(1)}, bf16[1,2,256,1280]{3,2,1,0:T(8,128)(2,1)}, u32[]{:S(2)}) copy-start(bf16[1,2,256,1280]{3,2,1,0:T(8,128)(2,1)} %param.8) | copy-start | bytes 3932164
  7.2 4.4 %copy-start.4 = (bf16[1,2,256,1280]{3,2,1,0:T(8,128)(2,1)S(1)}, bf16[1,2,256,1280]{3,2,1,0:T(8,128)(2,1)}, u32[]{:S(2)}) copy-start(bf16[1,2,256,1280]{3,2,1,0:T(8,128)(2,1)} %param.9) | copy-start | bytes 3932164
  7.2 44.1 %all-reduce.5.cloned.1.call-start = ((), (), s32[]{:S(2)}) async-start(), calls=%async_computation.3 | async-start | bytes 1048576 | tf_op jit(solution)/shard_map/psum | solution.py:57
  9.5 4.0 %copy-start.7 = (bf16[2,1280,128]{2,1,0:T(8,128)(2,1)S(1)}, bf16[2,1280,128]{2,1,0:T(8,128)(2,1)}, u32[]{:S(2)}) copy-start(bf16[2,1280,128]{2,1,0:T(8,128)(2,1)} %param.12) | copy-start | bytes 1966084
  11.6 3.2 %copy-start.2 = (s32[2,2,32,1280]{3,2,1,0:T(8,128)S(1)}, s32[2,2,32,1280]{3,2,1,0:T(8,128)}, u32[]{:S(2)}) copy-start(s32[2,2,32,1280]{3,2,1,0:T(8,128)} %param.13) | copy-start | bytes 1966084
  14.6 104.8 %reduce-scatter.5.cloned.1.call-start = ((), (), s32[]{:S(2)}) async-start(), calls=%async_computation.2 | async-start | bytes 163840
  14.7 2.5 %copy-start.6 = (bf16[1,2,256,1280]{3,2,1,0:T(8,128)(2,1)S(1)}, bf16[1,2,256,1280]{3,2,1,0:T(8,128)(2,1)}, u32[]{:S(2)}) copy-start(bf16[1,2,256,1280]{3,2,1,0:T(8,128)(2,1)} %param.8) | copy-start | bytes 3932164
  17.3 2.3 %copy-start = (bf16[2,2,512,1280]{3,2,1,0:T(8,128)(2,1)}, bf16[2,2,512,1280]{3,2,1,0:T(8,128)(2,1)S(1)}, u32[]{:S(2)}) copy-start(bf16[2,2,512,1280]{3,2,1,0:T(8,128)(2,1)S(1)} %fusion.3) | copy-start | bytes 15728644
  19.6 1.2 copy-start.3
  19.6 1.2 copy-start.1
  19.6 1.4 %copy-start.8 = (u32[32]{0:T(128)S(1)}, u32[32]{0:T(128)}, u32[]{:S(2)}) copy-start(u32[32]{0:T(128)} %constant.31) | copy-start | bytes 388
Sparse Core Ops, SparseCore 0:
  14.7 36.4 all-reduce.4
  101.8 17.4 reduce-scatter.4
where the time goes:
time: 128 us
  waiting for transfers between devices  44 us (34%)
  blocking collectives  39.8 us (31%)
  matrix products  18.2 us (14%)
  between operations  16.2 us (13%)
  local copies, waits for them, and re-layouts  4.68 us (4%)
  other arithmetic  4.52 us (4%)
    psum x1, waiting for transfers between devices, on_device(): lax.psum((shrunk_input, shrunk_gradient), 'col')  27 us
    unnamed x3, waiting for transfers between devices  17.1 us
    all_gather x1, blocking collectives, on_device(): lax.all_gather(gradient_features, 'ex', axis=0, tiled=True)  13.3 us
    unnamed x1, blocking collectives  10.3 us
    all_to_all x1, blocking collectives, on_device(): lax.all_to_all(by_target, 'ex', split_axis=0, concat_axis=1, tiled=True)  9.93 us
    psum x1, blocking collectives, on_device(): lax.psum(jnp.sum(own_columns * own_columns, axis=(1, 2)), 'col')  6.36 us
    dot_general x2, matrix products, on_device(): jnp.einsum('aom,cm->aoc', input_rows, adapter_down[index_of_layer], prefe...  4.33 us
    unnamed x22, local copies, waits for them, and re-layouts  3.29 us
  transfers between devices with their start and end apart: 2, of which 2 were waited for; matrix products, arithmetic and copies ran while one was open for 6% of the time, Pallas kernels for 0%

commit v1 on v0

v1 whole, which is shorter than its diff:
```python
import functools
import math

import jax
import jax.numpy as jnp
from jax import lax
from jax.experimental import pallas as pl
from jax.experimental.pallas import tpu as pltpu
from jax.sharding import PartitionSpec as P

epsilon = 1e-06
WORD = 16
f32, bf16 = jnp.float32, jnp.bfloat16
MIB = 1 << 20


def contract_last(a, b):
    return lax.dot_general(a, b, (((1,), (1,)), ((), ())), preferred_element_type=f32)


def halves(x):
    high = x.astype(bf16)
    return high, (x - high.astype(f32)).astype(bf16)


def partner(i, step, count):
    return i ^ step if count & (count - 1) == 0 else (i + step) % count


def shift(x, axis, count, step):
    return lax.ppermute(x, axis, [(i, partner(i, step, count)) for i in range(count)])


VMEM = pl.BlockSpec(memory_space=pltpu.VMEM)
SMEM = pl.BlockSpec(memory_space=pltpu.SMEM)
ANY = pl.BlockSpec(memory_space=pl.ANY)


def mix_kernel(right, hidden, grad, down, up, out, hid_buf, grad_buf, down_buf, up_buf, sems):
    layers = hidden.shape[1]
    copies = []
    for l in range(layers):
        group = []
        for k, (src, buf) in enumerate(
            (
                (down.at[l], down_buf.at[l]),
                (hidden.at[0, l], hid_buf.at[l]),
                (up.at[l], up_buf.at[l]),
                (grad.at[0, l], grad_buf.at[l]),
            )
        ):
            copy = pltpu.make_async_copy(src, buf, sems.at[l, k])
            copy.start()
            group.append(copy)
        copies.append(group)
    for l in range(layers):
        signs = (2 * right[l] - 1).astype(f32).astype(bf16)
        for j, (adapter, rows) in enumerate(((down_buf, hid_buf), (up_buf, grad_buf))):
            copies[l][2 * j].wait()
            if j == 0:
                mixed = jnp.dot(signs[j], adapter[l], preferred_element_type=f32)
            else:
                mixed = contract_last(signs[j], adapter[l])
            copies[l][2 * j + 1].wait()
            m = mixed.shape[0]
            both = contract_last(jnp.concatenate(halves(mixed), axis=0), rows[l])
            base = (2 * l + j) * m
            out[base : base + m, :] = both[:m] + both[m:]


def sign_kernel(words, hidden, grad, targets, high, low, target_high, target_low, squares,
                hid_buf, grad_buf, signs, sems):
    layers = hidden.shape[1]
    copies = []
    for l in range(layers):
        group = []
        for k, (src, buf) in enumerate(
            ((grad.at[0, l], grad_buf.at[l]), (hidden.at[0, l], hid_buf.at[l]))
        ):
            copy = pltpu.make_async_copy(src, buf, sems.at[l, k])
            copy.start()
            group.append(copy)
        copies.append(group)
    t = targets[...]
    target_high[...], target_low[...] = halves(t)
    squares[...] = jnp.sum(t * t, axis=1, keepdims=True)
    for l in range(layers):
        for j, rows in enumerate((grad_buf, hid_buf)):
            packed = words[l, j]
            w, d = packed.shape
            planes = [
                jnp.where((packed & (1 << b)) != 0, 1.0, -1.0).astype(f32)[:, None, :]
                for b in range(WORD)
            ]
            signs[...] = jnp.concatenate(planes, axis=1).reshape(w * WORD, d).astype(bf16)
            copies[l][j].wait()
            signed = contract_last(signs[...], rows[l])
            high[l, j], low[l, j] = halves(signed)


def sketch_kernel(cols, length, own, *refs):
    others, (high, low), outs, table = refs[: cols - 1], refs[cols - 1 : cols + 1], refs[cols + 1 : -1], refs[-1]
    me = lax.axis_index("col")
    mixed = own[...]
    for other in others:
        mixed = mixed + other[...]
    positions = lax.broadcasted_iota(jnp.int32, (1, mixed.shape[1]), 1)
    n = length[0]
    weights = jnp.where(positions < n, 1.0 / n.astype(f32), 0.0)
    mixed = mixed * weights
    layers, sides, k = high.shape[:3]
    m = mixed.shape[0] // (layers * sides)
    for l in range(layers):
        for j in range(sides):
            base = (2 * l + j) * m
            pair = jnp.concatenate(halves(mixed[base : base + m]), axis=0)
            both = contract_last(pair, high[l, j]) + contract_last(pair, low[l, j])
            rows = both[:m] + both[m:]
            for i in range(m):
                at = (base + i) * k
                block, within = divmod(at, table.shape[1])
                table[block : block + 1, within : within + k] = rows[i : i + 1]
    for step, out in enumerate(outs):
        to = partner(me, step, cols)
        out[...] = table[pl.ds(to, 1), :]


def sum_kernel(*refs):
    total = refs[0][...]
    for ref in refs[1:-1]:
        total = total + ref[...]
    refs[-1][...] = total


def score_kernel(exs, *refs):
    rows = jnp.concatenate([r[...] for r in refs[:exs]], axis=0)
    target_high, target_low, squares, out = refs[exs:]
    pair = jnp.concatenate(halves(rows), axis=0)
    both = contract_last(pair, target_high[...]) + contract_last(pair, target_low[...])
    count = target_high.shape[0]
    out[...] = jnp.zeros_like(out)
    out[0:exs, 0:count] = both[:exs] + both[exs:]
    out[0:exs, count : 2 * count] = jnp.broadcast_to(
        jnp.transpose(squares[...]), (exs, count)
    )
    out[exs : 2 * exs, :] = jnp.broadcast_to(
        jnp.sum(rows * rows, axis=1, keepdims=True), (exs, out.shape[1])
    )


def on_device(
    hidden_input,
    output_gradient,
    lengths,
    adapter_down,
    adapter_up,
    left_sign_words,
    right_sign_words,
    targets,
    *,
    exs,
    cols,
):
    _, layers, seq, width = hidden_input.shape
    m = right_sign_words.shape[3]
    rank = adapter_down.shape[1]
    k_left = left_sign_words.shape[2] * WORD
    count, own_cols = targets.shape
    all_cols = own_cols * cols
    params = functools.partial(pltpu.CompilerParams)
    right = jnp.swapaxes(right_sign_words, 2, 3)
    mixed = pl.pallas_call(
        mix_kernel,
        out_shape=jax.ShapeDtypeStruct((layers * 2 * m, seq), f32),
        in_specs=[VMEM, ANY, ANY, ANY, ANY],
        out_specs=VMEM,
        scratch_shapes=[
            pltpu.VMEM((layers, seq, width), bf16),
            pltpu.VMEM((layers, seq, width), bf16),
            pltpu.VMEM((layers, rank, width), bf16),
            pltpu.VMEM((layers, width, rank), bf16),
            pltpu.SemaphoreType.DMA((layers, 4)),
        ],
        compiler_params=params(vmem_limit_bytes=16 * MIB),
        name="mix",
    )(right, hidden_input, output_gradient, adapter_down, adapter_up)
    others = [shift(mixed, "col", cols, s) for s in range(1, cols)]
    signed = jax.ShapeDtypeStruct((layers, 2, k_left, seq), bf16)
    high, low, target_high, target_low, squares = pl.pallas_call(
        sign_kernel,
        out_shape=[
            signed,
            signed,
            jax.ShapeDtypeStruct(targets.shape, bf16),
            jax.ShapeDtypeStruct(targets.shape, bf16),
            jax.ShapeDtypeStruct((count, 1), f32),
        ],
        in_specs=[VMEM, ANY, ANY, VMEM],
        out_specs=[VMEM] * 5,
        scratch_shapes=[
            pltpu.VMEM((layers, seq, width), bf16),
            pltpu.VMEM((layers, seq, width), bf16),
            pltpu.VMEM((k_left, width), bf16),
            pltpu.SemaphoreType.DMA((layers, 2)),
        ],
        compiler_params=params(vmem_limit_bytes=24 * MIB),
        cost_estimate=pl.CostEstimate(
            flops=4 * layers * k_left * seq * width, bytes_accessed=4 * MIB, transcendentals=0
        ),
        name="sign",
    )(left_sign_words, hidden_input, output_gradient, targets)
    block = jax.ShapeDtypeStruct((1, own_cols), f32)
    blocks = pl.pallas_call(
        functools.partial(sketch_kernel, cols),
        out_shape=[block] * cols,
        in_specs=[SMEM] + [VMEM] * (cols + 2),
        out_specs=[VMEM] * cols,
        scratch_shapes=[pltpu.VMEM((cols, own_cols), f32)],
        compiler_params=params(vmem_limit_bytes=8 * MIB),
        name="sketch",
    )(lengths, mixed, *others, high, low)
    received = [shift(b, "col", cols, s) for s, b in enumerate(blocks) if s]
    own = pl.pallas_call(
        sum_kernel,
        out_shape=block,
        in_specs=[VMEM] * cols,
        out_specs=VMEM,
        compiler_params=params(vmem_limit_bytes=2 * MIB),
        name="own",
    )(blocks[0], *received)
    candidates = [own] + [shift(own, "ex", exs, s) for s in range(1, exs)]
    lanes = -(-2 * count // 128) * 128
    packed = pl.pallas_call(
        functools.partial(score_kernel, exs),
        out_shape=jax.ShapeDtypeStruct((2 * exs, lanes), f32),
        in_specs=[VMEM] * (exs + 3),
        out_specs=VMEM,
        compiler_params=params(vmem_limit_bytes=8 * MIB),
        name="score",
    )(*candidates, target_high, target_low, squares)
    me_ex = lax.axis_index("ex")
    order = jnp.stack([partner(me_ex, s, exs) if exs & (exs - 1) == 0 else (me_ex - s) % exs for s in range(exs)])
    per = exs // cols
    rows = jnp.stack([packed[:exs], packed[exs:]], axis=1)
    rows = jnp.zeros_like(rows).at[order].set(rows)
    grid = jnp.zeros((exs, cols) + rows.shape[1:], f32)
    grid = grid.at[:, me_ex // per].set(rows)
    back = lax.all_to_all(
        grid.reshape((exs * cols,) + rows.shape[1:]), ("ex", "col"), 0, 0, tiled=True
    ).reshape((exs, cols) + rows.shape[1:])
    me_col = lax.axis_index("col")
    mine = lax.dynamic_slice_in_dim(back, me_col * per, per, axis=0).sum(axis=1)
    raw = mine[:, 0, :count].reshape(1, -1)
    target_squares = mine[:, 0, count : 2 * count].reshape(1, -1)
    square = mine[0, 1, 0]
    scale = lax.rsqrt(square / all_cols + epsilon)
    features = own * scale
    scores = raw * scale * lax.rsqrt(target_squares / all_cols + epsilon) / math.sqrt(all_cols)
    return features, scores


def solution(mesh):
    body = functools.partial(on_device, exs=mesh.shape["ex"], cols=mesh.shape["col"])
    return jax.shard_map(
        body,
        mesh=mesh,
        in_specs=(
            P(("grp", "ex"), None, None, "col"),
            P(("grp", "ex"), None, None, "col"),
            P(("grp", "ex")),
            P(None, None, "col"),
            P(None, "col", None),
            P(None, None, None, "col"),
            P(),
            P(("grp", "ex"), "col"),
        ),
        out_specs=(P(("grp", "ex"), "col"), P(("grp", "ex"), "col")),
        check_vma=False,
    )
```

time: 128 us -> 61.4 us (0.48)
  blocking collectives: 39.8 us -> 0 us
  waiting for transfers between devices: 44 us -> 14 us
  Pallas kernels: 0 us -> 21.8 us
  matrix products: 18.2 us -> 0 us
  between operations: 16.2 us -> 2.14 us
  starting transfers between devices: 0.08 us -> 13.2 us
  local copies, waits for them, and re-layouts: 4.68 us -> 7.34 us
  other arithmetic: 4.52 us -> 2.54 us
    psum x1 -> x0, waiting for transfers between devices: 27 us -> none  [on_device(): lax.psum((shrunk_input, shrunk_gradient), 'col')]
    pallas_call x0 -> x5, Pallas kernels: none -> 21.8 us  [the longest x1 17 us: on_device(): pl.pallas_call(sign_kernel, out_shape=[signed, signed, jax.ShapeDtypeStru...]
    dot_general x17 -> x0, matrix products: 18.2 us -> none  [the longest x2 4.33 us: on_device(): jnp.einsum('aom,cm->aoc', input_rows, adapter_down[index_of_layer], prefe...]
    unnamed x3 -> x0, waiting for transfers between devices: 17.1 us -> none
    all_gather x1 -> x0, blocking collectives: 13.3 us -> none  [on_device(): lax.all_gather(gradient_features, 'ex', axis=0, tiled=True)]
    unnamed x1 -> x0, blocking collectives: 10.3 us -> none
    all_to_all x1 -> x0, blocking collectives: 9.93 us -> none  [on_device(): lax.all_to_all(by_target, 'ex', split_axis=0, concat_axis=1, tiled=True)]
    ppermute x0 -> x9, starting transfers between devices: none -> 9.71 us  [shift(): lax.ppermute(x, axis, [(i, partner(i, step, count)) for i in range(count)])]
  transfers between devices with their start and end apart: 2 -> 10, of which waited for: 2 -> 5; matrix products, arithmetic and copies ran while one was open for 6% -> 1% of each run, Pallas kernels for 0% -> 28%
where the time goes in v1:
time: 61.4 us; the launch traced here: 61 us
  Pallas kernels  21.8 us (36%)
  waiting for transfers between devices  14 us (23%)
  starting transfers between devices  13.2 us (21%)
  local copies, waits for them, and re-layouts  7.34 us (12%)
  other arithmetic  2.54 us (4%)
  between operations  2.14 us (3%)
    pallas_call x1, Pallas kernels, on_device(): pl.pallas_call(sign_kernel, out_shape=[signed, signed, jax.ShapeDtypeStru...  17 us
    ppermute x9, starting transfers between devices, shift(): lax.ppermute(x, axis, [(i, partner(i, step, count)) for i in range(count)])  9.71 us
    ppermute x9, waiting for transfers between devices, shift(): lax.ppermute(x, axis, [(i, partner(i, step, count)) for i in range(count)])  7.58 us
    all_to_all x1, waiting for transfers between devices, on_device(): lax.all_to_all(grid.reshape((exs * cols,) + rows.shape[1:]), ('ex', 'col'...  6.46 us
    unnamed x20, local copies, waits for them, and re-layouts  5.52 us
    pallas_call x1, Pallas kernels, on_device(): pl.pallas_call(mix_kernel, out_shape=jax.ShapeDtypeStruct((layers * 2 * m...  3.93 us
    all_to_all x1, starting transfers between devices, on_device(): lax.all_to_all(grid.reshape((exs * cols,) + rows.shape[1:]), ('ex', 'col'...  3.48 us
    another operation x2, other arithmetic  1.23 us
  transfers between devices with their start and end apart: 10, of which 5 were waited for; matrix products, arithmetic and copies ran while one was open for 1% of the time, Pallas kernels for 28%

profile of v1, /device:TPU:0, one launch (start us, length us, event | category | flops | bytes accessed | tf_op | source)
XLA Modules:
  0.0 61.0 jit_solution(6878721094199943252)
XLA Ops:
  0.6 0.0 copy-start
  0.6 1.3 %copy-done = bf16[1,2,256,1280]{3,2,1,0:T(8,128)(2,1)S(1)} copy-done((bf16[1,2,256,1280]{3,2,1,0:T(8,128)(2,1)S(1)}, bf16[1,2,256,1280]{3,2,1,0:T(8,128)(2,1)}, u32[]{:S(2)}) %copy-start) | copy-done | bytes 1310744
  1.9 0.0 copy-start.2
  2.0 1.3 %copy-done.2 = bf16[1,2,256,1280]{3,2,1,0:T(8,128)(2,1)S(1)} copy-done((bf16[1,2,256,1280]{3,2,1,0:T(8,128)(2,1)S(1)}, bf16[1,2,256,1280]{3,2,1,0:T(8,128)(2,1)}, u32[]{:S(2)}) %copy-start.2) | copy-done | bytes 1310744
  3.3 0.0 copy-start.4
  3.3 1.1 %copy-done.4 = bf16[2,128,1280]{2,1,0:T(8,128)(2,1)S(1)} copy-done((bf16[2,128,1280]{2,1,0:T(8,128)(2,1)S(1)}, bf16[2,128,1280]{2,1,0:T(8,128)(2,1)}, u32[]{:S(2)}) %copy-start.4) | copy-done | bytes 655384
  4.4 0.0 copy-start.5
  4.4 1.1 %copy-done.5 = bf16[2,1280,128]{2,1,0:T(8,128)(2,1)S(1)} copy-done((bf16[2,1280,128]{2,1,0:T(8,128)(2,1)S(1)}, bf16[2,1280,128]{2,1,0:T(8,128)(2,1)}, u32[]{:S(2)}) %copy-start.5) | copy-done | bytes 655384
  5.4 0.0 copy-start.6
  5.4 0.7 %copy-done.6 = s32[2,2,128,4]{2,3,1,0:T(4,128)S(1)} copy-done((s32[2,2,128,4]{2,3,1,0:T(4,128)S(1)}, s32[2,2,128,4]{2,3,1,0:T(4,128)}, u32[]{:S(2)}) %copy-start.6) | copy-done | bytes 8216
  6.1 0.0 copy-start.1
  6.1 0.0 copy-start.3
  6.1 0.0 copy-start.7
  6.1 0.0 copy-start.8
  6.2 3.9 %mix.1.own = f32[16,256]{1,0:T(8,128)S(1)} custom-call(s32[2,2,4,128]{3,2,1,0:T(4,128)S(1)} %bitcast.20, bf16[1,2,256,1280]{3,2,1,0:T(8,128)(2,1)S(1)} %copy-done, bf16[1,2,256,1280]{3,2,1,0:T(8,128)(2,1)S(1)} %copy-done.2, bf16[2,128,1280]{2,1,0:T(8,128)(2,1)S(1)} %copy-done.4, bf16[2,1280,128]{2,1,0:T(8,128)(2,1)S(1)} %copy-done.5), custom_call_target="tpu_custom_call" | custom-call | tf_op jit(solution)/shard_map/mix/pallas_call | solution.py:172
  10.1 0.6 collective-permute-start
  10.6 2.6 %collective-permute-start.1 = (f32[16,256]{1,0:T(8,128)S(1)}, f32[16,256]{1,0:T(8,128)S(1)}, u32[]{:S(2)}, u32[]{:S(2)}) collective-permute-start(f32[16,256]{1,0:T(8,128)S(1)} %mix.1.own), channel_id=1, source_target_pairs={{0,2},{1,3},{2,0},{3,1},{4,6},{5,7},{6,4},{7,5},{8,10},{9,11},{10,... | collective-permute-start | bytes 49160 | tf_op jit(solution)/shard_map/ppermute | solution.py:31
  13.2 0.0 collective-permute-start.2
  13.2 0.0 copy-done.1
  13.2 0.0 copy-done.3
  13.2 0.0 copy-done.7
  13.2 0.0 copy-done.8
  13.3 17.0 %sign.5 = (bf16[2,2,512,256]{3,2,1,0:T(8,128)(2,1)S(1)}, bf16[2,2,512,256]{3,2,1,0:T(8,128)(2,1)S(1)}, bf16[64,2048]{1,0:T(8,128)(2,1)S(1)}, bf16[64,2048]{1,0:T(8,128)(2,1)S(1)}, f32[64,1]{1,0:T(8,128)S(1)}) custom-call(s32[2,2,32,1280]{3,2,1,0:T(8,128)S(1)} %copy-done.7, bf16[1,2,256,1280]{3,2,1,0:T(8,128)(2,1)S(1)} %copy-done.1, ...), custom_call_target="tpu_custom_call" | custom-call | flops 1342177280 | bytes 4194304 | tf_op jit(solution)/shard_map/sign/pallas_call | solution.py:189
  30.2 0.0 copy-start.9
  30.9 0.0 collective-permute-done.refs_0_
  30.9 0.0 collective-permute-done.1.refs_1_
  30.9 0.0 collective-permute-done.2.refs_2_
  30.9 0.7 %sketch.1 = (f32[1,2048]{1,0:T(1,128)S(1)}, f32[1,2048]{1,0:T(1,128)S(1)}, f32[1,2048]{1,0:T(1,128)S(1)}, f32[1,2048]{1,0:T(1,128)S(1)}) custom-call(s32[1]{0:T(128)S(6)} %copy.18.length, f32[16,256]{1,0:T(8,128)S(1)} %mix.1.own, f32[16,256]{1,0:T(8,128)S(1)} %collective-permute-done.refs_0_, f32[16,256]{1,0:T(8,128)S(1)} %collective-permute-done.1.refs_1_, ...), custom_call_target="tpu_custom_call" | custom-call | tf_op jit(solution)/shard_map/sketch/pallas_call | solution.py:213
  31.6 0.2 collective-permute-start.3
  31.8 1.9 %collective-permute-start.4 = (f32[1,2048]{1,0:T(1,128)S(1)}, f32[1,2048]{1,0:T(1,128)S(1)}, u32[]{:S(2)}, u32[]{:S(2)}) collective-permute-start(f32[1,2048]{1,0:T(1,128)S(1)} %get-tuple-element.27), channel_id=1, source_target_pairs={{0,2},{1,3},{2,0},{3,1},{4,6},{5,7},{6,4},{7,5},{8,10},{9,11},{10,... | collective-permute-start | bytes 24584 | tf_op jit(solution)/shard_map/ppermute | solution.py:31
  33.8 0.0 collective-permute-start.5
  33.8 0.0 copy-done.9
  33.8 0.7 %and_reduce_fusion = pred[]{:T(512)} fusion(s32[4]{0:T(128)S(1)} %copy-done.9, s32[1]{0:T(128)} %constant.56.clone.1, s32[1]{0:T(128)} %bitcast.1), kind=kLoop, calls=%fused_computation.8 | loop fusion | flops 27 | bytes 25 | tf_op jit(solution)/shard_map/reduce.1
  34.5 0.0 collective-permute-done.3.refs_1_
  34.5 1.0 %collective-permute-done.4.refs_2_ = f32[1,2048]{1,0:T(1,128)S(1)} collective-permute-done((f32[1,2048]{1,0:T(1,128)S(1)}, f32[1,2048]{1,0:T(1,128)S(1)}, u32[]{:S(2)}, u32[]{:S(2)}) %collective-permute-start.4) | collective-permute-done | bytes 8224 | tf_op jit(solution)/shard_map/ppermute | solution.py:31
  35.5 1.4 %collective-permute-done.5.refs_3_ = f32[1,2048]{1,0:T(1,128)S(1)} collective-permute-done((f32[1,2048]{1,0:T(1,128)S(1)}, f32[1,2048]{1,0:T(1,128)S(1)}, u32[]{:S(2)}, u32[]{:S(2)}) %collective-permute-start.5) | collective-permute-done | bytes 8224 | tf_op jit(solution)/shard_map/ppermute | solution.py:31
  36.9 1.6 %collective-permute-start.6 = (f32[1,2048]{1,0:T(1,128)S(1)}, f32[1,2048]{1,0:T(1,128)S(1)}, u32[]{:S(2)}, u32[]{:S(2)}) collective-permute-start(f32[1,2048]{1,0:T(1,128)S(1)} %own.1.refs_0_), channel_id=1, source_target_pairs={{0,4},{4,0},{8,12},{12,8},{1,5},{5,1},{9,13},{13,9},{2,6},{6,2},{1... | collective-permute-start | bytes 24584 | tf_op jit(solution)/shard_map/ppermute | solution.py:31
  38.5 2.6 %collective-permute-start.7 = (f32[1,2048]{1,0:T(1,128)S(1)}, f32[1,2048]{1,0:T(1,128)S(1)}, u32[]{:S(2)}, u32[]{:S(2)}) collective-permute-start(f32[1,2048]{1,0:T(1,128)S(1)} %own.1.refs_0_), channel_id=1, source_target_pairs={{0,8},{4,12},{8,0},{12,4},{1,9},{5,13},{9,1},{13,5},{2,10},{6,14},... | collective-permute-start | bytes 24584 | tf_op jit(solution)/shard_map/ppermute | solution.py:31
  41.0 0.2 collective-permute-start.8
  41.3 0.1 fusion
  41.4 0.0 collective-permute-done.6.refs_1_
  41.4 1.7 %collective-permute-done.7.refs_2_ = f32[1,2048]{1,0:T(1,128)S(1)} collective-permute-done((f32[1,2048]{1,0:T(1,128)S(1)}, f32[1,2048]{1,0:T(1,128)S(1)}, u32[]{:S(2)}, u32[]{:S(2)}) %collective-permute-start.7) | collective-permute-done | bytes 8224 | tf_op jit(solution)/shard_map/ppermute | solution.py:31
  43.0 3.5 %collective-permute-done.8.refs_3_ = f32[1,2048]{1,0:T(1,128)S(1)} collective-permute-done((f32[1,2048]{1,0:T(1,128)S(1)}, f32[1,2048]{1,0:T(1,128)S(1)}, u32[]{:S(2)}, u32[]{:S(2)}) %collective-permute-start.8) | collective-permute-done | bytes 8224 | tf_op jit(solution)/shard_map/ppermute | solution.py:31
  46.5 0.2 score.1
  46.8 0.6 %scatter_fusion = f32[4,2,128]{2,1,0:T(2,128)S(1)} fusion(f32[4,2,128]{2,1,0:T(2,128)S(1)} %broadcast_in_dim.9, s32[4]{0:T(128)S(1)} %fusion, f32[4,2,128]{2,1,0:T(2,128)S(1)} %copy.13), kind=kCustom, calls=%fused_computation | custom fusion | bytes 12304 | tf_op jit(solution)/shard_map/scatter | solution.py:245
  47.4 0.5 select_bitcast_fusion
  48.1 0.6 copy.15
  48.7 3.5 %all-to-all-start = ((f32[16,2,128]{2,1,0:T(2,128)}), f32[16,2,128]{2,1,0:T(2,128)S(1)}, u32[]{:S(2)}, u32[]{:S(2)}) async-start(f32[16,2,128]{2,1,0:T(2,128)} %copy.15), calls=%async_computation | async-start | bytes 32768 | tf_op jit(solution)/shard_map/all_to_all | solution.py:248
  52.2 6.5 %all-to-all-done = f32[16,2,128]{2,1,0:T(2,128)S(1)} async-done(((f32[16,2,128]{2,1,0:T(2,128)}), f32[16,2,128]{2,1,0:T(2,128)S(1)}, u32[]{:S(2)}, u32[]{:S(2)}) %all-to-all-start) | async-done | bytes 16416 | tf_op jit(solution)/shard_map/all_to_all | solution.py:248
  58.6 0.5 slice.41
  59.8 0.6 multiply_bitcast_fusion
  60.4 0.6 broadcast_multiply_fusion
  (9 shorter events, 0.1 us)
Async XLA Ops:
  0.6 1.3 %copy-start = (bf16[1,2,256,1280]{3,2,1,0:T(8,128)(2,1)S(1)}, bf16[1,2,256,1280]{3,2,1,0:T(8,128)(2,1)}, u32[]{:S(2)}) copy-start(bf16[1,2,256,1280]{3,2,1,0:T(8,128)(2,1)} %hidden.3) | copy-start | bytes 3932164
  1.9 1.3 %copy-start.2 = (bf16[1,2,256,1280]{3,2,1,0:T(8,128)(2,1)S(1)}, bf16[1,2,256,1280]{3,2,1,0:T(8,128)(2,1)}, u32[]{:S(2)}) copy-start(bf16[1,2,256,1280]{3,2,1,0:T(8,128)(2,1)} %grad.3) | copy-start | bytes 3932164
  3.3 1.1 %copy-start.4 = (bf16[2,128,1280]{2,1,0:T(8,128)(2,1)S(1)}, bf16[2,128,1280]{2,1,0:T(8,128)(2,1)}, u32[]{:S(2)}) copy-start(bf16[2,128,1280]{2,1,0:T(8,128)(2,1)} %down.1) | copy-start | bytes 1966084
  4.4 1.1 %copy-start.5 = (bf16[2,1280,128]{2,1,0:T(8,128)(2,1)S(1)}, bf16[2,1280,128]{2,1,0:T(8,128)(2,1)}, u32[]{:S(2)}) copy-start(bf16[2,1280,128]{2,1,0:T(8,128)(2,1)} %up.1) | copy-start | bytes 1966084
  5.4 0.7 %copy-start.6 = (s32[2,2,128,4]{2,3,1,0:T(4,128)S(1)}, s32[2,2,128,4]{2,3,1,0:T(4,128)}, u32[]{:S(2)}) copy-start(s32[2,2,128,4]{2,3,1,0:T(4,128)} %param.16) | copy-start | bytes 24580
  6.1 7.1 %copy-start.1 = (bf16[1,2,256,1280]{3,2,1,0:T(8,128)(2,1)S(1)}, bf16[1,2,256,1280]{3,2,1,0:T(8,128)(2,1)}, u32[]{:S(2)}) copy-start(bf16[1,2,256,1280]{3,2,1,0:T(8,128)(2,1)} %hidden.3) | copy-start | bytes 3932164
  6.1 7.1 %copy-start.3 = (bf16[1,2,256,1280]{3,2,1,0:T(8,128)(2,1)S(1)}, bf16[1,2,256,1280]{3,2,1,0:T(8,128)(2,1)}, u32[]{:S(2)}) copy-start(bf16[1,2,256,1280]{3,2,1,0:T(8,128)(2,1)} %grad.3) | copy-start | bytes 3932164
  6.1 7.1 %copy-start.7 = (s32[2,2,32,1280]{3,2,1,0:T(8,128)S(1)}, s32[2,2,32,1280]{3,2,1,0:T(8,128)}, u32[]{:S(2)}) copy-start(s32[2,2,32,1280]{3,2,1,0:T(8,128)} %words.1) | copy-start | bytes 1966084
  6.1 7.1 %copy-start.8 = (f32[64,2048]{1,0:T(8,128)S(1)}, f32[64,2048]{1,0:T(8,128)}, u32[]{:S(2)}) copy-start(f32[64,2048]{1,0:T(8,128)} %targets.1) | copy-start | bytes 1572868
  10.1 20.8 %collective-permute-start = (f32[16,256]{1,0:T(8,128)S(1)}, f32[16,256]{1,0:T(8,128)S(1)}, u32[]{:S(2)}, u32[]{:S(2)}) collective-permute-start(f32[16,256]{1,0:T(8,128)S(1)} %mix.1.own), channel_id=1, source_target_pairs={{0,1},{1,0},{2,3},{3,2},{4,5},{5,4},{6,7},{7,6},{8,9},{9,8},{10,11... | collective-permute-start | bytes 49160 | tf_op jit(solution)/shard_map/ppermute | solution.py:31
  10.6 20.3 %collective-permute-start.1 = (f32[16,256]{1,0:T(8,128)S(1)}, f32[16,256]{1,0:T(8,128)S(1)}, u32[]{:S(2)}, u32[]{:S(2)}) collective-permute-start(f32[16,256]{1,0:T(8,128)S(1)} %mix.1.own), channel_id=1, source_target_pairs={{0,2},{1,3},{2,0},{3,1},{4,6},{5,7},{6,4},{7,5},{8,10},{9,11},{10,... | collective-permute-start | bytes 49160 | tf_op jit(solution)/shard_map/ppermute | solution.py:31
  13.2 17.7 %collective-permute-start.2 = (f32[16,256]{1,0:T(8,128)S(1)}, f32[16,256]{1,0:T(8,128)S(1)}, u32[]{:S(2)}, u32[]{:S(2)}) collective-permute-start(f32[16,256]{1,0:T(8,128)S(1)} %mix.1.own), channel_id=1, source_target_pairs={{0,3},{1,2},{2,1},{3,0},{4,7},{5,6},{6,5},{7,4},{8,11},{9,10},{10,... | collective-permute-start | bytes 49160 | tf_op jit(solution)/shard_map/ppermute | solution.py:31
  30.2 3.6 %copy-start.9 = (s32[4]{0:T(128)S(1)}, s32[4]{0:T(128)}, u32[]{:S(2)}) copy-start(s32[4]{0:T(128)} %constant.60.clone.1) | copy-start | bytes 52
  31.6 2.9 %collective-permute-start.3 = (f32[1,2048]{1,0:T(1,128)S(1)}, f32[1,2048]{1,0:T(1,128)S(1)}, u32[]{:S(2)}, u32[]{:S(2)}) collective-permute-start(f32[1,2048]{1,0:T(1,128)S(1)} %get-tuple-element.26), channel_id=1, source_target_pairs={{0,1},{1,0},{2,3},{3,2},{4,5},{5,4},{6,7},{7,6},{8,9},{9,8},{10,11... | collective-permute-start | bytes 24584 | tf_op jit(solution)/shard_map/ppermute | solution.py:31
  31.8 3.7 %collective-permute-start.4 = (f32[1,2048]{1,0:T(1,128)S(1)}, f32[1,2048]{1,0:T(1,128)S(1)}, u32[]{:S(2)}, u32[]{:S(2)}) collective-permute-start(f32[1,2048]{1,0:T(1,128)S(1)} %get-tuple-element.27), channel_id=1, source_target_pairs={{0,2},{1,3},{2,0},{3,1},{4,6},{5,7},{6,4},{7,5},{8,10},{9,11},{10,... | collective-permute-start | bytes 24584 | tf_op jit(solution)/shard_map/ppermute | solution.py:31
  33.8 3.1 %collective-permute-start.5 = (f32[1,2048]{1,0:T(1,128)S(1)}, f32[1,2048]{1,0:T(1,128)S(1)}, u32[]{:S(2)}, u32[]{:S(2)}) collective-permute-start(f32[1,2048]{1,0:T(1,128)S(1)} %get-tuple-element.28), channel_id=1, source_target_pairs={{0,3},{1,2},{2,1},{3,0},{4,7},{5,6},{6,5},{7,4},{8,11},{9,10},{10,... | collective-permute-start | bytes 24584 | tf_op jit(solution)/shard_map/ppermute | solution.py:31
  36.9 4.5 %collective-permute-start.6 = (f32[1,2048]{1,0:T(1,128)S(1)}, f32[1,2048]{1,0:T(1,128)S(1)}, u32[]{:S(2)}, u32[]{:S(2)}) collective-permute-start(f32[1,2048]{1,0:T(1,128)S(1)} %own.1.refs_0_), channel_id=1, source_target_pairs={{0,4},{4,0},{8,12},{12,8},{1,5},{5,1},{9,13},{13,9},{2,6},{6,2},{1... | collective-permute-start | bytes 24584 | tf_op jit(solution)/shard_map/ppermute | solution.py:31
  38.5 4.5 %collective-permute-start.7 = (f32[1,2048]{1,0:T(1,128)S(1)}, f32[1,2048]{1,0:T(1,128)S(1)}, u32[]{:S(2)}, u32[]{:S(2)}) collective-permute-start(f32[1,2048]{1,0:T(1,128)S(1)} %own.1.refs_0_), channel_id=1, source_target_pairs={{0,8},{4,12},{8,0},{12,4},{1,9},{5,13},{9,1},{13,5},{2,10},{6,14},... | collective-permute-start | bytes 24584 | tf_op jit(solution)/shard_map/ppermute | solution.py:31
  41.0 5.4 %collective-permute-start.8 = (f32[1,2048]{1,0:T(1,128)S(1)}, f32[1,2048]{1,0:T(1,128)S(1)}, u32[]{:S(2)}, u32[]{:S(2)}) collective-permute-start(f32[1,2048]{1,0:T(1,128)S(1)} %own.1.refs_0_), channel_id=1, source_target_pairs={{0,12},{4,8},{8,4},{12,0},{1,13},{5,9},{9,5},{13,1},{2,14},{6,10},... | collective-permute-start | bytes 24584 | tf_op jit(solution)/shard_map/ppermute | solution.py:31
  48.7 10.0 %all-to-all-start = ((f32[16,2,128]{2,1,0:T(2,128)}), f32[16,2,128]{2,1,0:T(2,128)S(1)}, u32[]{:S(2)}, u32[]{:S(2)}) async-start(f32[16,2,128]{2,1,0:T(2,128)} %copy.15), calls=%async_computation | async-start | bytes 32768 | tf_op jit(solution)/shard_map/all_to_all | solution.py:248

commit v2 on v0

v2 whole, which is shorter than its diff:
```python
import functools
import math

import jax
import jax.numpy as jnp
from jax import lax
from jax.experimental import pallas as pl
from jax.experimental.pallas import tpu as pltpu
from jax.sharding import PartitionSpec as P

epsilon = 1e-06
WORD = 16
LANES = 128
IN_FLIGHT = 2
f32, bf16 = jnp.float32, jnp.bfloat16
MIB = 1 << 20

VMEM = pl.BlockSpec(memory_space=pltpu.VMEM)
SMEM = pl.BlockSpec(memory_space=pltpu.SMEM)
HBM = pl.BlockSpec(memory_space=pltpu.HBM)


def contract_last(a, b):
    return lax.dot_general(a, b, (((1,), (1,)), ((), ())), preferred_element_type=f32)


def halves(x):
    high = x.astype(bf16)
    return high, (x - high.astype(f32)).astype(bf16)


def partner(i, step, count):
    return i ^ step if count & (count - 1) == 0 else (i + step) % count


def shift(x, axis, count, step):
    return lax.ppermute(x, axis, [(i, partner(i, step, count)) for i in range(count)])


def in_hbm(*arrays):
    return [pltpu.with_memory_space_constraint(x, pltpu.HBM) for x in arrays]


def mix_kernel(right, hidden, grad, down, up, out, hid_out, grad_out, right_buf, down_buf, up_buf, sems):
    layers = hidden.shape[1]
    groups = []
    for l in range(layers):
        for j, (adapter, adapter_to, rows, rows_to) in enumerate(
            ((down, down_buf, hidden, hid_out), (up, up_buf, grad, grad_out))
        ):
            at = 2 * l + j
            groups.append(
                (
                    pltpu.make_async_copy(adapter.at[l], adapter_to.at[l], sems.at[at, 0]),
                    pltpu.make_async_copy(rows.at[0, l], rows_to.at[0, l], sems.at[at, 1]),
                )
            )
    signs_copy = pltpu.make_async_copy(right, right_buf, sems.at[2 * layers, 0])
    signs_copy.start()
    for group in groups[:IN_FLIGHT]:
        for copy in group:
            copy.start()
    signs_copy.wait()
    for at, group in enumerate(groups):
        l, j = divmod(at, 2)
        signs = (2 * right_buf[l, j] - 1).astype(f32).astype(bf16)
        group[0].wait()
        if j == 0:
            mixed = jnp.dot(signs, down_buf[l], preferred_element_type=f32)
        else:
            mixed = contract_last(signs, up_buf[l])
        pair = jnp.concatenate(halves(mixed), axis=0)
        group[1].wait()
        for copy in groups[at + IN_FLIGHT] if at + IN_FLIGHT < len(groups) else ():
            copy.start()
        m = mixed.shape[0]
        both = contract_last(pair, (hid_out if j == 0 else grad_out)[0, l])
        out[at * m : (at + 1) * m, :] = both[:m] + both[m:]


def unpack(words, l, j, out):
    bits = 1 << lax.broadcasted_iota(jnp.int32, (WORD, 1), 0)
    width = words.shape[3]
    for w in range(words.shape[2]):
        word = jnp.broadcast_to(words[l, j, w : w + 1, :], (WORD, width))
        signs = jnp.where((word & bits) != 0, 1.0, -1.0)
        out[w * WORD : (w + 1) * WORD, :] = signs.astype(f32).astype(bf16)


def sign_kernel(words, hidden, grad, targets, high, low, target_high, target_low, squares, signs):
    t = targets[...]
    target_high[...], target_low[...] = halves(t)
    squares[...] = jnp.transpose(jnp.sum(t * t, axis=1, keepdims=True))
    items = [(l, j) for l in range(hidden.shape[1]) for j in range(2)]
    unpack(words, *items[0], signs.at[0])
    for i, (l, j) in enumerate(items):
        if i + 1 < len(items):
            unpack(words, *items[i + 1], signs.at[(i + 1) % 2])
        signed = contract_last(signs[i % 2], (grad if j == 0 else hidden)[0, l])
        high[l, j], low[l, j] = halves(signed)


def sketch_kernel(exs, cols, length, own, *refs):
    others, (high, low, out) = refs[: cols - 1], refs[cols - 1 :]
    mixed = own[...]
    for other in others:
        mixed = mixed + other[...]
    positions = lax.broadcasted_iota(jnp.int32, (1, mixed.shape[1]), 1)
    n = length[0]
    mixed = mixed * jnp.where(positions < n, 1.0 / n.astype(f32), 0.0)
    layers, sides, k = high.shape[:3]
    m = mixed.shape[0] // (layers * sides)
    pieces = []
    for l in range(layers):
        for j in range(sides):
            base = (2 * l + j) * m
            pair = jnp.concatenate(halves(mixed[base : base + m]), axis=0)
            both = contract_last(pair, high[l, j]) + contract_last(pair, low[l, j])
            both = both[:m] + both[m:]
            pieces += [both[:, q : q + LANES] for q in range(0, k, LANES)]
    per = len(pieces) // cols
    for i in range(cols):
        block = jnp.concatenate(pieces[i * per : (i + 1) * per], axis=0)
        for e in range(exs):
            out[e * cols + i] = block


def column_starts(m, k, count):
    per = k // LANES
    return [
        (r // (m * per)) * m * k + (r % m) * k + (r // m % per) * LANES for r in range(count)
    ]


def score_kernel(exs, cols, m, k, received, target_high, target_low, squares, own, out):
    x = received[...]
    x = x.reshape((exs, cols) + x.shape[1:])
    total = x[:, 0]
    for i in range(1, cols):
        total = total + x[:, i]
    starts = column_starts(m, k, total.shape[1])
    order = sorted(range(len(starts)), key=lambda r: starts[r])
    rows = jnp.concatenate([total[:, r, :] for r in order], axis=1)
    pair = jnp.concatenate(halves(rows), axis=0)
    both = contract_last(pair, target_high[...]) + contract_last(pair, target_low[...])
    count = target_high.shape[0]
    out[...] = jnp.zeros_like(out)
    out[0:exs, 0:count] = both[:exs] + both[exs:]
    out[0:exs, count : 2 * count] = jnp.broadcast_to(squares[...], (exs, count))
    out[exs : 2 * exs, :] = jnp.broadcast_to(
        jnp.sum(rows * rows, axis=1, keepdims=True), (exs, out.shape[1])
    )
    me = lax.axis_index("ex")
    mine = received[pl.ds(me * cols, cols)]
    total = mine[0]
    for i in range(1, cols):
        total = total + mine[i]
    own[...] = total


def send_kernel(exs, cols, a, b, *outs):
    me = lax.axis_index("col")
    for step, out in zip(range(0, exs, 2), outs):
        e = me ^ step
        out[...] = jnp.zeros_like(out)
        out[0:1] = a[pl.ds(e, 1), :] + b[pl.ds(e, 1), :]
        out[1:2] = a[pl.ds(exs + e, 1), :] + b[pl.ds(exs + e, 1), :]


def last_kernel(all_cols, m, k, own, *refs):
    parts, (features, scores) = refs[:-2], refs[-2:]
    total = parts[0][...]
    for part in parts[1:]:
        total = total + part[...]
    count = scores.shape[1]
    scale = lax.rsqrt(total[1:2, 0:1] / all_cols + epsilon)
    target_scale = lax.rsqrt(total[0:1, count : 2 * count] / all_cols + epsilon)
    scores[...] = total[0:1, 0:count] * scale * target_scale / math.sqrt(all_cols)
    block = own[...] * scale
    for r, at in enumerate(column_starts(m, k, block.shape[0])):
        features[:, at : at + LANES] = block[r : r + 1]


def call(kernel, out_shape, in_specs, name, limit, scratch=(), flops=0, moved=0):
    single = not isinstance(out_shape, list)
    return pl.pallas_call(
        kernel,
        out_shape=out_shape,
        in_specs=in_specs,
        out_specs=VMEM if single else [VMEM] * len(out_shape),
        scratch_shapes=scratch,
        compiler_params=pltpu.CompilerParams(vmem_limit_bytes=limit * MIB),
        cost_estimate=pl.CostEstimate(flops=flops, bytes_accessed=moved, transcendentals=0),
        name=name,
    )


def on_device(
    hidden_input,
    output_gradient,
    lengths,
    adapter_down,
    adapter_up,
    left_sign_words,
    right_sign_words,
    targets,
    *,
    exs,
    cols,
):
    _, layers, seq, width = hidden_input.shape
    m = right_sign_words.shape[3]
    rank = adapter_down.shape[1]
    k = left_sign_words.shape[2] * WORD
    count, own_cols = targets.shape
    all_cols = own_cols * cols
    right = jnp.swapaxes(right_sign_words, 2, 3)
    rows = jax.ShapeDtypeStruct(hidden_input.shape, bf16)
    mixed, hidden, grad = call(
        mix_kernel,
        [jax.ShapeDtypeStruct((layers * 2 * m, seq), f32), rows, rows],
        [HBM] * 5,
        "mix",
        8,
        [
            pltpu.VMEM(right.shape, jnp.int32),
            pltpu.VMEM((layers, rank, width), bf16),
            pltpu.VMEM((layers, width, rank), bf16),
            pltpu.SemaphoreType.DMA((2 * layers + 1, 2)),
        ],
        4 * layers * seq * width * rank,
        4 * MIB,
    )(*in_hbm(right, hidden_input, output_gradient, adapter_down, adapter_up))
    others = [shift(mixed, "col", cols, s) for s in range(1, cols)]
    signed = jax.ShapeDtypeStruct((layers, 2, k, seq), bf16)
    target_half = jax.ShapeDtypeStruct(targets.shape, bf16)
    high, low, target_high, target_low, squares = call(
        sign_kernel,
        [signed, signed, target_half, target_half, jax.ShapeDtypeStruct((1, count), f32)],
        [VMEM] * 4,
        "sign",
        8,
        [pltpu.VMEM((2, k, width), bf16)],
        4 * layers * k * seq * width,
        6 * MIB,
    )(left_sign_words, hidden, grad, targets)
    block = (own_cols // LANES, LANES)
    blocks = call(
        functools.partial(sketch_kernel, exs, cols),
        jax.ShapeDtypeStruct((exs * cols,) + block, f32),
        [SMEM] + [VMEM] * (cols + 2),
        "sketch",
        8,
    )(lengths, mixed, *others, high, low)
    received = lax.all_to_all(blocks, ("ex", "col"), 0, 0, tiled=True)
    lanes = -(-2 * count // LANES) * LANES
    own, packed = call(
        functools.partial(score_kernel, exs, cols, m, k),
        [jax.ShapeDtypeStruct(block, f32), jax.ShapeDtypeStruct((2 * exs, lanes), f32)],
        [VMEM] * 4,
        "score",
        16,
    )(received, target_high, target_low, squares)
    results = [
        jax.ShapeDtypeStruct((1, own_cols), f32),
        jax.ShapeDtypeStruct((1, count * exs // cols), f32),
    ]
    if exs == cols and exs % 2 == 0 and exs & (exs - 1) == 0:
        neighbour = shift(packed, "col", cols, 1)
        sent = call(
            functools.partial(send_kernel, exs, cols),
            [jax.ShapeDtypeStruct((8, lanes), f32)] * (exs // 2),
            [VMEM] * 2,
            "send",
            2,
        )(packed, neighbour)
        parts = [
            lax.ppermute(
                x,
                ("ex", "col"),
                [(a * cols + i, (i ^ step) * cols + a) for a in range(exs) for i in range(cols)],
            )
            for step, x in zip(range(0, exs, 2), sent)
        ]
        return tuple(
            call(
                functools.partial(last_kernel, all_cols, m, k),
                results,
                [VMEM] * (1 + len(parts)),
                "last",
                2,
            )(own, *parts)
        )
    per = exs // cols
    rows = jnp.stack([packed[:exs], packed[exs:]], axis=1)
    grid = jnp.zeros((exs, cols) + rows.shape[1:], f32)
    grid = grid.at[:, lax.axis_index("ex") // per].set(rows)
    back = lax.all_to_all(
        grid.reshape((exs * cols,) + rows.shape[1:]), ("ex", "col"), 0, 0, tiled=True
    ).reshape((exs, cols) + rows.shape[1:])
    mine = lax.dynamic_slice_in_dim(back, lax.axis_index("col") * per, per, axis=0).sum(axis=1)
    total = jnp.concatenate(
        [
            jnp.concatenate([mine[:, 0, :count].reshape(1, -1), mine[:, 0, count : 2 * count].reshape(1, -1)], axis=1),
            jnp.broadcast_to(mine[:1, 1, :1], (1, 2 * count * per)),
        ],
        axis=0,
    )
    return tuple(
        call(functools.partial(last_kernel, all_cols, m, k), results, [VMEM] * 2, "last", 2)(own, total)
    )


def solution(mesh):
    body = functools.partial(on_device, exs=mesh.shape["ex"], cols=mesh.shape["col"])
    return jax.shard_map(
        body,
        mesh=mesh,
        in_specs=(
            P(("grp", "ex"), None, None, "col"),
            P(("grp", "ex"), None, None, "col"),
            P(("grp", "ex")),
            P(None, None, "col"),
            P(None, "col", None),
            P(None, None, None, "col"),
            P(),
            P(("grp", "ex"), "col"),
        ),
        out_specs=(P(("grp", "ex"), "col"), P(("grp", "ex"), "col")),
        check_vma=False,
    )
```

time: 128 us -> 33.3 us (0.26)
  the two profiles are of different devices: /device:TPU:0 before, /device:TPU:3 now
where the time goes in v2:
time: 33.3 us; the launch traced here: 33.1 us
  blocking collectives  11.8 us (35%)
  starting transfers between devices  7.74 us (23%)
  Pallas kernels  7.28 us (22%)
  waiting for transfers between devices  4.91 us (15%)
  between operations  1.35 us (4%)
    all_to_all x1, blocking collectives, on_device(): received = lax.all_to_all(blocks, ('ex', 'col'), 0, 0, tiled=True)  11.8 us
    ppermute x2, starting transfers between devices, on_device(): lax.ppermute(x, ('ex', 'col'), [(a * cols + i, (i ^ step) * cols + a) for...  5.29 us
    pallas_call x1, Pallas kernels, on_device(): call(mix_kernel, [jax.ShapeDtypeStruct((layers * 2 * m, seq), f32), rows,...  3.92 us
    ppermute x2, waiting for transfers between devices, on_device(): lax.ppermute(x, ('ex', 'col'), [(a * cols + i, (i ^ step) * cols + a) for...  3.72 us
    ppermute x4, starting transfers between devices, shift(): lax.ppermute(x, axis, [(i, partner(i, step, count)) for i in range(count)])  2.45 us
    pallas_call x1, Pallas kernels, on_device(): call(sign_kernel, [signed, signed, target_half, target_half, jax.ShapeDty...  1.8 us
    ppermute x4, waiting for transfers between devices, shift(): lax.ppermute(x, axis, [(i, partner(i, step, count)) for i in range(count)])  1.2 us
  transfers between devices with their start and end apart: 6, of which 3 were waited for; matrix products, arithmetic and copies ran while one was open for 0% of the time, Pallas kernels for 5%

profile of v2, /device:TPU:3, one launch (start us, length us, event | category | flops | bytes accessed | tf_op | source)
XLA Modules:
  0.0 33.1 jit_solution(5058353770467228576)
XLA Ops:
  0.6 0.0 copy-start
  0.6 0.0 copy-start.1
  0.7 3.9 %mix.1 = (f32[16,256]{1,0:T(8,128)S(1)}, bf16[1,2,256,1280]{3,2,1,0:T(8,128)(2,1)S(1)}, bf16[1,2,256,1280]{3,2,1,0:T(8,128)(2,1)S(1)}) custom-call(s32[2,2,4,128]{3,2,1,0:T(4,128)} %bitcast.1, bf16[1,2,256,1280]{3,2,1,0:T(8,128)(2,1)} %hidden.1, bf16[1,2,256,1280]{3,2,1,0:T(8,128)(2,1)} %grad.1, bf16[2,128,1280]{2,1,0:T(8,128)(2,1)} %down.1, ...), custom_call_target="tpu_custom_call" | custom-call | flops 335544320 | bytes 4194304 | tf_op jit(solution)/shard_map/mix/pallas_call | solution.py:219
  4.6 0.7 %collective-permute-start = (f32[16,256]{1,0:T(8,128)S(1)}, f32[16,256]{1,0:T(8,128)S(1)}, u32[]{:S(2)}, u32[]{:S(2)}) collective-permute-start(f32[16,256]{1,0:T(8,128)S(1)} %get-tuple-element.14.own), channel_id=1, source_target_pairs={{0,1},{1,0},{2,3},{3,2},{4,5},{5,4},{6,7},{7,6},{8,9},{9,8},{10,11... | collective-permute-start | bytes 49160 | tf_op jit(solution)/shard_map/ppermute | solution.py:37
  5.3 0.0 collective-permute-start.1
  5.3 1.7 %collective-permute-start.2 = (f32[16,256]{1,0:T(8,128)S(1)}, f32[16,256]{1,0:T(8,128)S(1)}, u32[]{:S(2)}, u32[]{:S(2)}) collective-permute-start(f32[16,256]{1,0:T(8,128)S(1)} %get-tuple-element.14.own), channel_id=1, source_target_pairs={{0,3},{1,2},{2,1},{3,0},{4,7},{5,6},{6,5},{7,4},{8,11},{9,10},{10,... | collective-permute-start | bytes 49160 | tf_op jit(solution)/shard_map/ppermute | solution.py:37
  7.0 0.0 copy-done
  7.0 0.0 copy-done.1
  7.0 1.8 %sign.1 = (bf16[2,2,512,256]{3,2,1,0:T(8,128)(2,1)S(1)}, bf16[2,2,512,256]{3,2,1,0:T(8,128)(2,1)S(1)}, bf16[64,2048]{1,0:T(8,128)(2,1)S(1)}, bf16[64,2048]{1,0:T(8,128)(2,1)S(1)}, f32[1,64]{1,0:T(1,128)S(1)}) custom-call(s32[2,2,32,1280]{3,2,1,0:T(8,128)S(1)} %copy-done, bf16[1,2,256,1280]{3,2,1,0:T(8,128)(2,1)S(1)} %get-tuple-element.15.hidden, ...), custom_call_target="tpu_custom_call" | custom-call | flops 1342177280 | bytes 6291456 | tf_op jit(solution)/shard_map/sign/pallas_call | solution.py:237
  9.5 0.0 collective-permute-done.refs_0_
  9.5 0.0 collective-permute-done.1.refs_1_
  9.5 0.0 collective-permute-done.2.refs_2_
  9.5 0.7 %sketch.1 = f32[16,16,128]{2,1,0:T(8,128)S(1)} custom-call(s32[1]{0:T(128)S(6)} %copy.10.length, f32[16,256]{1,0:T(8,128)S(1)} %get-tuple-element.14.own, f32[16,256]{1,0:T(8,128)S(1)} %collective-permute-done.refs_0_, f32[16,256]{1,0:T(8,128)S(1)} %collective-permute-done.1.refs_1_, f32[16,256]{1,0:T(8,128)S(1)} %collective-permute-done.2.refs_2_, ...), custom_call_target="tpu_custom_call" | custom-call | tf_op jit(solution)/shard_map/sketch/pallas_call | solution.py:248
  10.2 11.8 %all_to_all.5.received = f32[16,16,128]{2,1,0:T(8,128)S(1)} all-to-all(f32[16,16,128]{2,1,0:T(8,128)S(1)} %sketch.1), channel_id=1, replica_groups=mesh['grp'=2,'ex'=4,'col'=4] {'ex','col'}, dimensions={0} | all-to-all | bytes 262144 | tf_op jit(solution)/shard_map/all_to_all | solution.py:255
  22.0 0.2 score.1
  22.2 0.0 collective-permute-start.3
  22.2 1.2 %collective-permute-done.3.b = f32[8,128]{1,0:T(8,128)S(1)} collective-permute-done((f32[8,128]{1,0:T(8,128)S(1)}, f32[8,128]{1,0:T(8,128)S(1)}, u32[]{:S(2)}, u32[]{:S(2)}) %collective-permute-start.3) | collective-permute-done | bytes 4128 | tf_op jit(solution)/shard_map/ppermute | solution.py:37
  23.4 4.1 %collective-permute-start.4 = (f32[8,128]{1,0:T(8,128)S(1)}, f32[8,128]{1,0:T(8,128)S(1)}, u32[]{:S(2)}, u32[]{:S(2)}) collective-permute-start(f32[8,128]{1,0:T(8,128)S(1)} %get-tuple-element.24), channel_id=1, source_target_pairs={{0,0},{1,4},{2,8},{3,12},{4,1},{5,5},{6,9},{7,13},{8,2},{9,6},{10,... | collective-permute-start | bytes 12296 | tf_op jit(solution)/shard_map/ppermute | solution.py:278
  27.6 1.2 %collective-permute-start.5 = (f32[8,128]{1,0:T(8,128)S(1)}, f32[8,128]{1,0:T(8,128)S(1)}, u32[]{:S(2)}, u32[]{:S(2)}) collective-permute-start(f32[8,128]{1,0:T(8,128)S(1)} %get-tuple-element.25), channel_id=1, source_target_pairs={{0,8},{1,12},{2,0},{3,4},{4,9},{5,13},{6,1},{7,5},{8,10},{9,14},{1... | collective-permute-start | bytes 12296 | tf_op jit(solution)/shard_map/ppermute | solution.py:278
  28.7 2.3 %collective-permute-done.4.refs_0_ = f32[8,128]{1,0:T(8,128)S(1)} collective-permute-done((f32[8,128]{1,0:T(8,128)S(1)}, f32[8,128]{1,0:T(8,128)S(1)}, u32[]{:S(2)}, u32[]{:S(2)}) %collective-permute-start.4) | collective-permute-done | bytes 4128 | tf_op jit(solution)/shard_map/ppermute | solution.py:278
  31.0 1.4 %collective-permute-done.5.refs_1_ = f32[8,128]{1,0:T(8,128)S(1)} collective-permute-done((f32[8,128]{1,0:T(8,128)S(1)}, f32[8,128]{1,0:T(8,128)S(1)}, u32[]{:S(2)}, u32[]{:S(2)}) %collective-permute-start.5) | collective-permute-done | bytes 4128 | tf_op jit(solution)/shard_map/ppermute | solution.py:278
  32.4 0.7 %last.1 = (f32[1,2048]{1,0:T(1,128)}, f32[1,64]{1,0:T(1,128)}) custom-call(f32[16,128]{1,0:T(8,128)S(1)} %get-tuple-element.22.own, f32[8,128]{1,0:T(8,128)S(1)} %collective-permute-done.4.refs_0_, f32[8,128]{1,0:T(8,128)S(1)} %collective-permute-done.5.refs_1_), custom_call_target="tpu_custom_call" | custom-call | tf_op jit(solution)/shard_map/last/pallas_call | solution.py:286
  (1 shorter events, 0.0 us)
Async XLA Ops:
  0.6 6.4 %copy-start = (s32[2,2,32,1280]{3,2,1,0:T(8,128)S(1)}, s32[2,2,32,1280]{3,2,1,0:T(8,128)}, u32[]{:S(2)}) copy-start(s32[2,2,32,1280]{3,2,1,0:T(8,128)} %words.1) | copy-start | bytes 1966084
  0.6 6.4 %copy-start.1 = (f32[64,2048]{1,0:T(8,128)S(1)}, f32[64,2048]{1,0:T(8,128)}, u32[]{:S(2)}) copy-start(f32[64,2048]{1,0:T(8,128)} %targets.1) | copy-start | bytes 1572868
  4.6 4.9 %collective-permute-start = (f32[16,256]{1,0:T(8,128)S(1)}, f32[16,256]{1,0:T(8,128)S(1)}, u32[]{:S(2)}, u32[]{:S(2)}) collective-permute-start(f32[16,256]{1,0:T(8,128)S(1)} %get-tuple-element.14.own), channel_id=1, source_target_pairs={{0,1},{1,0},{2,3},{3,2},{4,5},{5,4},{6,7},{7,6},{8,9},{9,8},{10,11... | collective-permute-start | bytes 49160 | tf_op jit(solution)/shard_map/ppermute | solution.py:37
  5.3 4.2 %collective-permute-start.1 = (f32[16,256]{1,0:T(8,128)S(1)}, f32[16,256]{1,0:T(8,128)S(1)}, u32[]{:S(2)}, u32[]{:S(2)}) collective-permute-start(f32[16,256]{1,0:T(8,128)S(1)} %get-tuple-element.14.own), channel_id=1, source_target_pairs={{0,2},{1,3},{2,0},{3,1},{4,6},{5,7},{6,4},{7,5},{8,10},{9,11},{10,... | collective-permute-start | bytes 49160 | tf_op jit(solution)/shard_map/ppermute | solution.py:37
  5.3 4.2 %collective-permute-start.2 = (f32[16,256]{1,0:T(8,128)S(1)}, f32[16,256]{1,0:T(8,128)S(1)}, u32[]{:S(2)}, u32[]{:S(2)}) collective-permute-start(f32[16,256]{1,0:T(8,128)S(1)} %get-tuple-element.14.own), channel_id=1, source_target_pairs={{0,3},{1,2},{2,1},{3,0},{4,7},{5,6},{6,5},{7,4},{8,11},{9,10},{10,... | collective-permute-start | bytes 49160 | tf_op jit(solution)/shard_map/ppermute | solution.py:37
  22.2 1.2 %collective-permute-start.3 = (f32[8,128]{1,0:T(8,128)S(1)}, f32[8,128]{1,0:T(8,128)S(1)}, u32[]{:S(2)}, u32[]{:S(2)}) collective-permute-start(f32[8,128]{1,0:T(8,128)S(1)} %get-tuple-element.23.a), channel_id=1, source_target_pairs={{0,1},{1,0},{2,3},{3,2},{4,5},{5,4},{6,7},{7,6},{8,9},{9,8},{10,11... | collective-permute-start | bytes 12296 | tf_op jit(solution)/shard_map/ppermute | solution.py:37
  23.4 7.6 %collective-permute-start.4 = (f32[8,128]{1,0:T(8,128)S(1)}, f32[8,128]{1,0:T(8,128)S(1)}, u32[]{:S(2)}, u32[]{:S(2)}) collective-permute-start(f32[8,128]{1,0:T(8,128)S(1)} %get-tuple-element.24), channel_id=1, source_target_pairs={{0,0},{1,4},{2,8},{3,12},{4,1},{5,5},{6,9},{7,13},{8,2},{9,6},{10,... | collective-permute-start | bytes 12296 | tf_op jit(solution)/shard_map/ppermute | solution.py:278
  27.6 4.9 %collective-permute-start.5 = (f32[8,128]{1,0:T(8,128)S(1)}, f32[8,128]{1,0:T(8,128)S(1)}, u32[]{:S(2)}, u32[]{:S(2)}) collective-permute-start(f32[8,128]{1,0:T(8,128)S(1)} %get-tuple-element.25), channel_id=1, source_target_pairs={{0,8},{1,12},{2,0},{3,4},{4,9},{5,13},{6,1},{7,5},{8,10},{9,14},{1... | collective-permute-start | bytes 12296 | tf_op jit(solution)/shard_map/ppermute | solution.py:278

commit v3 on v2

--- a/solution.py
+++ b/solution.py
@@ -11,12 +11,10 @@
 epsilon = 1e-06
 WORD = 16
 LANES = 128
-IN_FLIGHT = 2
 f32, bf16 = jnp.float32, jnp.bfloat16
 MIB = 1 << 20
 
 VMEM = pl.BlockSpec(memory_space=pltpu.VMEM)
-SMEM = pl.BlockSpec(memory_space=pltpu.SMEM)
 HBM = pl.BlockSpec(memory_space=pltpu.HBM)
 
 
@@ -41,40 +39,34 @@
     return [pltpu.with_memory_space_constraint(x, pltpu.HBM) for x in arrays]
 
 
-def mix_kernel(right, hidden, grad, down, up, out, hid_out, grad_out, right_buf, down_buf, up_buf, sems):
+def mix_kernel(
+    right, hidden, grad, down, up, out, hid_out, grad_out, right_buf, down_buf, up_buf, sems
+):
     layers = hidden.shape[1]
-    groups = []
-    for l in range(layers):
-        for j, (adapter, adapter_to, rows, rows_to) in enumerate(
-            ((down, down_buf, hidden, hid_out), (up, up_buf, grad, grad_out))
-        ):
-            at = 2 * l + j
-            groups.append(
-                (
-                    pltpu.make_async_copy(adapter.at[l], adapter_to.at[l], sems.at[at, 0]),
-                    pltpu.make_async_copy(rows.at[0, l], rows_to.at[0, l], sems.at[at, 1]),
-                )
-            )
-    signs_copy = pltpu.make_async_copy(right, right_buf, sems.at[2 * layers, 0])
-    signs_copy.start()
-    for group in groups[:IN_FLIGHT]:
-        for copy in group:
-            copy.start()
-    signs_copy.wait()
-    for at, group in enumerate(groups):
-        l, j = divmod(at, 2)
+    sides = [(l, j) for l in range(layers) for j in range(2)]
+    first = [(right, right_buf)]
+    first += [((up if j else down).at[l], (up_buf if j else down_buf).at[l]) for l, j in sides]
+    rows = [
+        ((grad if j else hidden).at[0, l], (grad_out if j else hid_out).at[0, l]) for l, j in sides
+    ]
+    copies = [pltpu.make_async_copy(a, b, sems.at[i]) for i, (a, b) in enumerate(first + rows)]
+    for copy in copies:
+        copy.start()
+    for copy in copies[: len(first)]:
+        copy.wait()
+    pairs = []
+    for l, j in sides:
         signs = (2 * right_buf[l, j] - 1).astype(f32).astype(bf16)
-        group[0].wait()
         if j == 0:
-            mixed = jnp.dot(signs, down_buf[l], preferred_element_type=f32)
+            folded = jnp.dot(signs, down_buf[l], preferred_element_type=f32)
         else:
-            mixed = contract_last(signs, up_buf[l])
-        pair = jnp.concatenate(halves(mixed), axis=0)
-        group[1].wait()
-        for copy in groups[at + IN_FLIGHT] if at + IN_FLIGHT < len(groups) else ():
-            copy.start()
-        m = mixed.shape[0]
-        both = contract_last(pair, (hid_out if j == 0 else grad_out)[0, l])
+            folded = contract_last(signs, up_buf[l])
+        pairs.append(jnp.concatenate(halves(folded), axis=0))
+    for copy in copies[len(first) :]:
+        copy.wait()
+    for at, (l, j) in enumerate(sides):
+        both = contract_last(pairs[at], (grad_out if j else hid_out)[0, l])
+        m = both.shape[0] // 2
         out[at * m : (at + 1) * m, :] = both[:m] + both[m:]
 
 
@@ -105,8 +97,8 @@
     mixed = own[...]
     for other in others:
         mixed = mixed + other[...]
+    n = length[...]
     positions = lax.broadcasted_iota(jnp.int32, (1, mixed.shape[1]), 1)
-    n = length[0]
     mixed = mixed * jnp.where(positions < n, 1.0 / n.astype(f32), 0.0)
     layers, sides, k = high.shape[:3]
     m = mixed.shape[0] // (layers * sides)
@@ -226,7 +218,7 @@
             pltpu.VMEM(right.shape, jnp.int32),
             pltpu.VMEM((layers, rank, width), bf16),
             pltpu.VMEM((layers, width, rank), bf16),
-            pltpu.SemaphoreType.DMA((2 * layers + 1, 2)),
+            pltpu.SemaphoreType.DMA((4 * layers + 1,)),
         ],
         4 * layers * seq * width * rank,
         4 * MIB,
@@ -248,10 +240,10 @@
     blocks = call(
         functools.partial(sketch_kernel, exs, cols),
         jax.ShapeDtypeStruct((exs * cols,) + block, f32),
-        [SMEM] + [VMEM] * (cols + 2),
+        [VMEM] * (cols + 3),
         "sketch",
         8,
-    )(lengths, mixed, *others, high, low)
+    )(lengths.reshape(1, 1), mixed, *others, high, low)
     received = lax.all_to_all(blocks, ("ex", "col"), 0, 0, tiled=True)
     lanes = -(-2 * count // LANES) * LANES
     own, packed = call(

time: 33.3 us -> 32.4 us (0.973)
  Pallas kernels: 7.28 us -> 6.42 us
    pallas_call x1, Pallas kernels: 3.92 us -> 3.06 us  [on_device(): call(mix_kernel, [jax.ShapeDtypeStruct((layers * 2 * m, seq), f32), rows,...]
  transfers between devices with their start and end apart: 6 -> 6, of which waited for: 3 -> 3; matrix products, arithmetic and copies ran while one was open for 0% -> 0% of each run, Pallas kernels for 5% -> 6%
where the time goes in v3:
time: 32.4 us; the launch traced here: 32.2 us
  blocking collectives  11.8 us (36%)
  starting transfers between devices  7.74 us (24%)
  Pallas kernels  6.42 us (20%)
  waiting for transfers between devices  4.91 us (15%)
  between operations  1.35 us (4%)
    all_to_all x1, blocking collectives, on_device(): received = lax.all_to_all(blocks, ('ex', 'col'), 0, 0, tiled=True)  11.8 us
    ppermute x2, starting transfers between devices, on_device(): lax.ppermute(x, ('ex', 'col'), [(a * cols + i, (i ^ step) * cols + a) for...  5.29 us
    ppermute x2, waiting for transfers between devices, on_device(): lax.ppermute(x, ('ex', 'col'), [(a * cols + i, (i ^ step) * cols + a) for...  3.72 us
    pallas_call x1, Pallas kernels, on_device(): call(mix_kernel, [jax.ShapeDtypeStruct((layers * 2 * m, seq), f32), rows,...  3.06 us
    ppermute x4, starting transfers between devices, shift(): lax.ppermute(x, axis, [(i, partner(i, step, count)) for i in range(count)])  2.45 us
    pallas_call x1, Pallas kernels, on_device(): call(sign_kernel, [signed, signed, target_half, target_half, jax.ShapeDty...  1.8 us
    ppermute x4, waiting for transfers between devices, shift(): lax.ppermute(x, axis, [(i, partner(i, step, count)) for i in range(count)])  1.2 us
    pallas_call x1, Pallas kernels, on_device(): call(functools.partial(sketch_kernel, exs, cols), jax.ShapeDtypeStruct((e...  0.67 us
  transfers between devices with their start and end apart: 6, of which 3 were waited for; matrix products, arithmetic and copies ran while one was open for 0% of the time, Pallas kernels for 6%

profile of v3, /device:TPU:3, one launch (start us, length us, event | category | flops | bytes accessed | tf_op | source)
XLA Modules:
  0.0 32.2 jit_solution(785857153070495750)
XLA Ops:
  0.6 0.0 copy-start
  0.6 0.0 copy-start.1
  0.7 3.1 %mix.1 = (f32[16,256]{1,0:T(8,128)S(1)}, bf16[1,2,256,1280]{3,2,1,0:T(8,128)(2,1)S(1)}, bf16[1,2,256,1280]{3,2,1,0:T(8,128)(2,1)S(1)}) custom-call(s32[2,2,4,128]{3,2,1,0:T(4,128)} %bitcast.3, bf16[1,2,256,1280]{3,2,1,0:T(8,128)(2,1)} %hidden.1, bf16[1,2,256,1280]{3,2,1,0:T(8,128)(2,1)} %grad.1, bf16[2,128,1280]{2,1,0:T(8,128)(2,1)} %down.1, ...), custom_call_target="tpu_custom_call" | custom-call | flops 335544320 | bytes 4194304 | tf_op jit(solution)/shard_map/mix/pallas_call | solution.py:211
  3.7 0.7 %collective-permute-start = (f32[16,256]{1,0:T(8,128)S(1)}, f32[16,256]{1,0:T(8,128)S(1)}, u32[]{:S(2)}, u32[]{:S(2)}) collective-permute-start(f32[16,256]{1,0:T(8,128)S(1)} %get-tuple-element.14.own), channel_id=1, source_target_pairs={{0,1},{1,0},{2,3},{3,2},{4,5},{5,4},{6,7},{7,6},{8,9},{9,8},{10,11... | collective-permute-start | bytes 49160 | tf_op jit(solution)/shard_map/ppermute | solution.py:35
  4.5 0.0 collective-permute-start.1
  4.5 1.7 %collective-permute-start.2 = (f32[16,256]{1,0:T(8,128)S(1)}, f32[16,256]{1,0:T(8,128)S(1)}, u32[]{:S(2)}, u32[]{:S(2)}) collective-permute-start(f32[16,256]{1,0:T(8,128)S(1)} %get-tuple-element.14.own), channel_id=1, source_target_pairs={{0,3},{1,2},{2,1},{3,0},{4,7},{5,6},{6,5},{7,4},{8,11},{9,10},{10,... | collective-permute-start | bytes 49160 | tf_op jit(solution)/shard_map/ppermute | solution.py:35
  6.2 0.0 copy-done
  6.2 0.0 copy-done.1
  6.2 1.8 %sign.1 = (bf16[2,2,512,256]{3,2,1,0:T(8,128)(2,1)S(1)}, bf16[2,2,512,256]{3,2,1,0:T(8,128)(2,1)S(1)}, bf16[64,2048]{1,0:T(8,128)(2,1)S(1)}, bf16[64,2048]{1,0:T(8,128)(2,1)S(1)}, f32[1,64]{1,0:T(1,128)S(1)}) custom-call(s32[2,2,32,1280]{3,2,1,0:T(8,128)S(1)} %copy-done, bf16[1,2,256,1280]{3,2,1,0:T(8,128)(2,1)S(1)} %get-tuple-element.15.hidden, ...), custom_call_target="tpu_custom_call" | custom-call | flops 1342177280 | bytes 6291456 | tf_op jit(solution)/shard_map/sign/pallas_call | solution.py:229
  8.6 0.0 collective-permute-done.refs_0_
  8.6 0.0 collective-permute-done.1.refs_1_
  8.7 0.0 collective-permute-done.2.refs_2_
  8.7 0.7 %sketch.1 = f32[16,16,128]{2,1,0:T(8,128)S(1)} custom-call(s32[1,1]{1,0:T(1,128)} %bitcast.2.length, f32[16,256]{1,0:T(8,128)S(1)} %get-tuple-element.14.own, f32[16,256]{1,0:T(8,128)S(1)} %collective-permute-done.refs_0_, f32[16,256]{1,0:T(8,128)S(1)} %collective-permute-done.1.refs_1_, f32[16,256]{1,0:T(8,128)S(1)} %collective-permute-done.2.refs_2_, ...), custom_call_target="tpu_custom_call" | custom-call | tf_op jit(solution)/shard_map/sketch/pallas_call | solution.py:240
  9.3 11.8 %all_to_all.5.received = f32[16,16,128]{2,1,0:T(8,128)S(1)} all-to-all(f32[16,16,128]{2,1,0:T(8,128)S(1)} %sketch.1), channel_id=1, replica_groups=mesh['grp'=2,'ex'=4,'col'=4] {'ex','col'}, dimensions={0} | all-to-all | bytes 262144 | tf_op jit(solution)/shard_map/all_to_all | solution.py:247
  21.1 0.2 score.1
  21.4 0.0 collective-permute-start.3
  21.4 1.2 %collective-permute-done.3.b = f32[8,128]{1,0:T(8,128)S(1)} collective-permute-done((f32[8,128]{1,0:T(8,128)S(1)}, f32[8,128]{1,0:T(8,128)S(1)}, u32[]{:S(2)}, u32[]{:S(2)}) %collective-permute-start.3) | collective-permute-done | bytes 4128 | tf_op jit(solution)/shard_map/ppermute | solution.py:35
  22.6 4.1 %collective-permute-start.4 = (f32[8,128]{1,0:T(8,128)S(1)}, f32[8,128]{1,0:T(8,128)S(1)}, u32[]{:S(2)}, u32[]{:S(2)}) collective-permute-start(f32[8,128]{1,0:T(8,128)S(1)} %get-tuple-element.24), channel_id=1, source_target_pairs={{0,0},{1,4},{2,8},{3,12},{4,1},{5,5},{6,9},{7,13},{8,2},{9,6},{10,... | collective-permute-start | bytes 12296 | tf_op jit(solution)/shard_map/ppermute | solution.py:270
  26.7 1.2 %collective-permute-start.5 = (f32[8,128]{1,0:T(8,128)S(1)}, f32[8,128]{1,0:T(8,128)S(1)}, u32[]{:S(2)}, u32[]{:S(2)}) collective-permute-start(f32[8,128]{1,0:T(8,128)S(1)} %get-tuple-element.25), channel_id=1, source_target_pairs={{0,8},{1,12},{2,0},{3,4},{4,9},{5,13},{6,1},{7,5},{8,10},{9,14},{1... | collective-permute-start | bytes 12296 | tf_op jit(solution)/shard_map/ppermute | solution.py:270
  27.9 2.3 %collective-permute-done.4.refs_0_ = f32[8,128]{1,0:T(8,128)S(1)} collective-permute-done((f32[8,128]{1,0:T(8,128)S(1)}, f32[8,128]{1,0:T(8,128)S(1)}, u32[]{:S(2)}, u32[]{:S(2)}) %collective-permute-start.4) | collective-permute-done | bytes 4128 | tf_op jit(solution)/shard_map/ppermute | solution.py:270
  30.2 1.4 %collective-permute-done.5.refs_1_ = f32[8,128]{1,0:T(8,128)S(1)} collective-permute-done((f32[8,128]{1,0:T(8,128)S(1)}, f32[8,128]{1,0:T(8,128)S(1)}, u32[]{:S(2)}, u32[]{:S(2)}) %collective-permute-start.5) | collective-permute-done | bytes 4128 | tf_op jit(solution)/shard_map/ppermute | solution.py:270
  31.6 0.7 %last.1 = (f32[1,2048]{1,0:T(1,128)}, f32[1,64]{1,0:T(1,128)}) custom-call(f32[16,128]{1,0:T(8,128)S(1)} %get-tuple-element.22.own, f32[8,128]{1,0:T(8,128)S(1)} %collective-permute-done.4.refs_0_, f32[8,128]{1,0:T(8,128)S(1)} %collective-permute-done.5.refs_1_), custom_call_target="tpu_custom_call" | custom-call | tf_op jit(solution)/shard_map/last/pallas_call | solution.py:278
  (1 shorter events, 0.0 us)
Async XLA Ops:
  0.6 5.5 %copy-start = (s32[2,2,32,1280]{3,2,1,0:T(8,128)S(1)}, s32[2,2,32,1280]{3,2,1,0:T(8,128)}, u32[]{:S(2)}) copy-start(s32[2,2,32,1280]{3,2,1,0:T(8,128)} %words.1) | copy-start | bytes 1966084
  0.6 5.5 %copy-start.1 = (f32[64,2048]{1,0:T(8,128)S(1)}, f32[64,2048]{1,0:T(8,128)}, u32[]{:S(2)}) copy-start(f32[64,2048]{1,0:T(8,128)} %targets.1) | copy-start | bytes 1572868
  3.7 4.9 %collective-permute-start = (f32[16,256]{1,0:T(8,128)S(1)}, f32[16,256]{1,0:T(8,128)S(1)}, u32[]{:S(2)}, u32[]{:S(2)}) collective-permute-start(f32[16,256]{1,0:T(8,128)S(1)} %get-tuple-element.14.own), channel_id=1, source_target_pairs={{0,1},{1,0},{2,3},{3,2},{4,5},{5,4},{6,7},{7,6},{8,9},{9,8},{10,11... | collective-permute-start | bytes 49160 | tf_op jit(solution)/shard_map/ppermute | solution.py:35
  4.5 4.2 %collective-permute-start.1 = (f32[16,256]{1,0:T(8,128)S(1)}, f32[16,256]{1,0:T(8,128)S(1)}, u32[]{:S(2)}, u32[]{:S(2)}) collective-permute-start(f32[16,256]{1,0:T(8,128)S(1)} %get-tuple-element.14.own), channel_id=1, source_target_pairs={{0,2},{1,3},{2,0},{3,1},{4,6},{5,7},{6,4},{7,5},{8,10},{9,11},{10,... | collective-permute-start | bytes 49160 | tf_op jit(solution)/shard_map/ppermute | solution.py:35
  4.5 4.2 %collective-permute-start.2 = (f32[16,256]{1,0:T(8,128)S(1)}, f32[16,256]{1,0:T(8,128)S(1)}, u32[]{:S(2)}, u32[]{:S(2)}) collective-permute-start(f32[16,256]{1,0:T(8,128)S(1)} %get-tuple-element.14.own), channel_id=1, source_target_pairs={{0,3},{1,2},{2,1},{3,0},{4,7},{5,6},{6,5},{7,4},{8,11},{9,10},{10,... | collective-permute-start | bytes 49160 | tf_op jit(solution)/shard_map/ppermute | solution.py:35
  21.4 1.2 %collective-permute-start.3 = (f32[8,128]{1,0:T(8,128)S(1)}, f32[8,128]{1,0:T(8,128)S(1)}, u32[]{:S(2)}, u32[]{:S(2)}) collective-permute-start(f32[8,128]{1,0:T(8,128)S(1)} %get-tuple-element.23.a), channel_id=1, source_target_pairs={{0,1},{1,0},{2,3},{3,2},{4,5},{5,4},{6,7},{7,6},{8,9},{9,8},{10,11... | collective-permute-start | bytes 12296 | tf_op jit(solution)/shard_map/ppermute | solution.py:35
  22.6 7.6 %collective-permute-start.4 = (f32[8,128]{1,0:T(8,128)S(1)}, f32[8,128]{1,0:T(8,128)S(1)}, u32[]{:S(2)}, u32[]{:S(2)}) collective-permute-start(f32[8,128]{1,0:T(8,128)S(1)} %get-tuple-element.24), channel_id=1, source_target_pairs={{0,0},{1,4},{2,8},{3,12},{4,1},{5,5},{6,9},{7,13},{8,2},{9,6},{10,... | collective-permute-start | bytes 12296 | tf_op jit(solution)/shard_map/ppermute | solution.py:270
  26.7 4.9 %collective-permute-start.5 = (f32[8,128]{1,0:T(8,128)S(1)}, f32[8,128]{1,0:T(8,128)S(1)}, u32[]{:S(2)}, u32[]{:S(2)}) collective-permute-start(f32[8,128]{1,0:T(8,128)S(1)} %get-tuple-element.25), channel_id=1, source_target_pairs={{0,8},{1,12},{2,0},{3,4},{4,9},{5,13},{6,1},{7,5},{8,10},{9,14},{1... | collective-permute-start | bytes 12296 | tf_op jit(solution)/shard_map/ppermute | solution.py:270

commit v4 on v3

--- a/solution.py
+++ b/solution.py
@@ -10,6 +10,7 @@
 
 epsilon = 1e-06
 WORD = 16
+STEPS = (3, 2, 1)
 LANES = 128
 f32, bf16 = jnp.float32, jnp.bfloat16
 MIB = 1 << 20
@@ -79,10 +80,13 @@
         out[w * WORD : (w + 1) * WORD, :] = signs.astype(f32).astype(bf16)
 
 
-def sign_kernel(words, hidden, grad, targets, high, low, target_high, target_low, squares, signs):
+def split_kernel(targets, high, low, squares):
     t = targets[...]
-    target_high[...], target_low[...] = halves(t)
+    high[...], low[...] = halves(t)
     squares[...] = jnp.transpose(jnp.sum(t * t, axis=1, keepdims=True))
+
+
+def sign_kernel(words, hidden, grad, high, low, signs):
     items = [(l, j) for l in range(hidden.shape[1]) for j in range(2)]
     unpack(words, *items[0], signs.at[0])
     for i, (l, j) in enumerate(items):
@@ -92,8 +96,7 @@
         high[l, j], low[l, j] = halves(signed)
 
 
-def sketch_kernel(exs, cols, length, own, *refs):
-    others, (high, low, out) = refs[: cols - 1], refs[cols - 1 :]
+def sketch_blocks(cols, length, own, others, high, low):
     mixed = own[...]
     for other in others:
         mixed = mixed + other[...]
@@ -111,10 +114,30 @@
             both = both[:m] + both[m:]
             pieces += [both[:, q : q + LANES] for q in range(0, k, LANES)]
     per = len(pieces) // cols
-    for i in range(cols):
-        block = jnp.concatenate(pieces[i * per : (i + 1) * per], axis=0)
+    return [jnp.concatenate(pieces[i * per : (i + 1) * per], axis=0) for i in range(cols)]
+
+
+def spread_kernel(exs, cols, length, own, *refs):
+    others, (high, low, out) = refs[: cols - 1], refs[cols - 1 :]
+    for i, block in enumerate(sketch_blocks(cols, length, own, others, high, low)):
         for e in range(exs):
             out[e * cols + i] = block
+
+
+def pair_kernel(cols, length, own, *refs):
+    others, (high, low), outs, table = refs[: cols - 1], refs[cols - 1 : cols + 1], refs[cols + 1 : -1], refs[-1]
+    for i, block in enumerate(sketch_blocks(cols, length, own, others, high, low)):
+        table[i] = block
+    me = lax.axis_index("col")
+    for step, out in enumerate(outs):
+        out[...] = table[partner(me, step, cols)]
+
+
+def sum_kernel(*refs):
+    total = refs[0][...]
+    for ref in refs[1:-1]:
+        total = total + ref[...]
+    refs[-1][...] = total
 
 
 def column_starts(m, k, count):
@@ -124,12 +147,8 @@
     ]
 
 
-def score_kernel(exs, cols, m, k, received, target_high, target_low, squares, own, out):
-    x = received[...]
-    x = x.reshape((exs, cols) + x.shape[1:])
-    total = x[:, 0]
-    for i in range(1, cols):
-        total = total + x[:, i]
+def score(total, m, k, target_high, target_low, squares, out):
+    exs = total.shape[0]
     starts = column_starts(m, k, total.shape[1])
     order = sorted(range(len(starts)), key=lambda r: starts[r])
     rows = jnp.concatenate([total[:, r, :] for r in order], axis=1)
@@ -142,21 +161,53 @@
     out[exs : 2 * exs, :] = jnp.broadcast_to(
         jnp.sum(rows * rows, axis=1, keepdims=True), (exs, out.shape[1])
     )
-    me = lax.axis_index("ex")
-    mine = received[pl.ds(me * cols, cols)]
-    total = mine[0]
-    for i in range(1, cols):
-        total = total + mine[i]
-    own[...] = total
-
-
-def send_kernel(exs, cols, a, b, *outs):
-    me = lax.axis_index("col")
-    for step, out in zip(range(0, exs, 2), outs):
-        e = me ^ step
-        out[...] = jnp.zeros_like(out)
-        out[0:1] = a[pl.ds(e, 1), :] + b[pl.ds(e, 1), :]
-        out[1:2] = a[pl.ds(exs + e, 1), :] + b[pl.ds(exs + e, 1), :]
+
+
+def gathered_kernel(exs, cols, m, k, received, target_high, target_low, squares, own, out):
+    def collect(x):
+        total = x[:, 0]
+        for i in range(1, cols):
+            total = total + x[:, i]
+        return total
+
+    x = received[...]
+    score(
+        collect(x.reshape((exs, cols) + x.shape[1:])), m, k, target_high, target_low, squares, out
+    )
+    mine = received[pl.ds(lax.axis_index("ex") * cols, cols)]
+    own[...] = collect(mine[None])[0]
+
+
+def paired_kernel(m, k, own, other, *refs):
+    *tables, local, remote = refs
+    blocks = jnp.concatenate([own[...][None], other[...][None]], axis=0)
+    starts = column_starts(m, k, blocks.shape[1])
+    order = sorted(range(len(starts)), key=lambda r: starts[r])
+    rows = jnp.concatenate([blocks[:, r, :] for r in order], axis=1)
+    pair = jnp.concatenate(halves(rows), axis=0)
+    lines = []
+    for at in range(0, len(tables), 3):
+        high, low, squares = tables[at : at + 3]
+        both = contract_last(pair, high[...]) + contract_last(pair, low[...])
+        scores = both[:2] + both[2:]
+        lines.append(
+            jnp.concatenate([scores, jnp.broadcast_to(squares[...], scores.shape)], axis=1)
+        )
+    square = jnp.broadcast_to(jnp.sum(rows[:1] * rows[:1], axis=1, keepdims=True), lines[0][:1].shape)
+    pad = jnp.zeros((8 - len(lines), square.shape[1]), f32)
+    local[...] = jnp.concatenate([line[:1] for line in lines] + [square, pad[1:]], axis=0)
+    remote[...] = jnp.concatenate([line[1:] for line in lines] + [pad], axis=0)
+
+
+def send_kernel(local, remote, *refs):
+    *outs, table = refs
+    table[0:2] = local[0:2]
+    table[2:4] = remote[0:2]
+    mine = lax.axis_index("ex") ^ lax.axis_index("col")
+    for step, out in enumerate(outs):
+        out[...] = jnp.concatenate(
+            [table[pl.ds(mine ^ step, 1), :], local[2:8], local[7:8]], axis=0
+        )
 
 
 def last_kernel(all_cols, m, k, own, *refs):
@@ -207,6 +258,7 @@
     count, own_cols = targets.shape
     all_cols = own_cols * cols
     right = jnp.swapaxes(right_sign_words, 2, 3)
+    neighbours = shift(targets, "ex", exs, 1)
     rows = jax.ShapeDtypeStruct(hidden_input.shape, bf16)
     mixed, hidden, grad = call(
         mix_kernel,
@@ -223,66 +275,71 @@
         4 * layers * seq * width * rank,
         4 * MIB,
     )(*in_hbm(right, hidden_input, output_gradient, adapter_down, adapter_up))
-    others = [shift(mixed, "col", cols, s) for s in range(1, cols)]
+    others = [shift(mixed, "col", cols, s) for s in range(cols - 1, 0, -1)]
     signed = jax.ShapeDtypeStruct((layers, 2, k, seq), bf16)
-    target_half = jax.ShapeDtypeStruct(targets.shape, bf16)
-    high, low, target_high, target_low, squares = call(
+    high, low = call(
         sign_kernel,
-        [signed, signed, target_half, target_half, jax.ShapeDtypeStruct((1, count), f32)],
-        [VMEM] * 4,
+        [signed, signed],
+        [VMEM] * 3,
         "sign",
         8,
         [pltpu.VMEM((2, k, width), bf16)],
         4 * layers * k * seq * width,
         6 * MIB,
-    )(left_sign_words, hidden, grad, targets)
+    )(left_sign_words, hidden, grad)
+    target_half = jax.ShapeDtypeStruct(targets.shape, bf16)
+    split = call(
+        split_kernel,
+        [target_half, target_half, jax.ShapeDtypeStruct((1, count), f32)],
+        [VMEM],
+        "split",
+        4,
+        moved=MIB,
+    )
     block = (own_cols // LANES, LANES)
-    blocks = call(
-        functools.partial(sketch_kernel, exs, cols),
-        jax.ShapeDtypeStruct((exs * cols,) + block, f32),
-        [VMEM] * (cols + 3),
-        "sketch",
-        8,
-    )(lengths.reshape(1, 1), mixed, *others, high, low)
-    received = lax.all_to_all(blocks, ("ex", "col"), 0, 0, tiled=True)
     lanes = -(-2 * count // LANES) * LANES
-    own, packed = call(
-        functools.partial(score_kernel, exs, cols, m, k),
-        [jax.ShapeDtypeStruct(block, f32), jax.ShapeDtypeStruct((2 * exs, lanes), f32)],
-        [VMEM] * 4,
-        "score",
-        16,
-    )(received, target_high, target_low, squares)
+    shape = jax.ShapeDtypeStruct(block, f32)
+    packed = jax.ShapeDtypeStruct((2 * exs, lanes), f32)
     results = [
         jax.ShapeDtypeStruct((1, own_cols), f32),
         jax.ShapeDtypeStruct((1, count * exs // cols), f32),
     ]
-    if exs == cols and exs % 2 == 0 and exs & (exs - 1) == 0:
-        neighbour = shift(packed, "col", cols, 1)
-        sent = call(
-            functools.partial(send_kernel, exs, cols),
-            [jax.ShapeDtypeStruct((8, lanes), f32)] * (exs // 2),
-            [VMEM] * 2,
-            "send",
-            2,
-        )(packed, neighbour)
-        parts = [
-            lax.ppermute(
-                x,
-                ("ex", "col"),
-                [(a * cols + i, (i ^ step) * cols + a) for a in range(exs) for i in range(cols)],
-            )
-            for step, x in zip(range(0, exs, 2), sent)
-        ]
+    inputs = (lengths.reshape(1, 1), mixed, *others, high, low)
+    last = functools.partial(last_kernel, all_cols, m, k)
+    if exs == 4 and cols == 4:
+        blocks = call(
+            functools.partial(pair_kernel, cols),
+            [shape] * cols,
+            [VMEM] * len(inputs),
+            "sketch",
+            8,
+            [pltpu.VMEM((cols,) + block, f32)],
+        )(*inputs)
+        received = [shift(blocks[s], "col", cols, s) for s in STEPS]
+        own = call(sum_kernel, shape, [VMEM] * cols, "own", 2)(blocks[0], *received)
+        other = shift(own, "ex", exs, 2)
+        line = jax.ShapeDtypeStruct((8, lanes), f32)
+        local, remote = call(
+            functools.partial(paired_kernel, m, k), [line, line], [VMEM] * 8, "score", 8
+        )(own, other, *split(targets), *split(neighbours))
+        lines = call(
+            send_kernel, [line] * cols, [VMEM] * 2, "send", 2, [pltpu.VMEM((4, lanes), f32)]
+        )(local, shift(remote, "ex", exs, 2))
+        parts = [lines[0]] + [shift(lines[s], "col", cols, s) for s in STEPS]
         return tuple(
-            call(
-                functools.partial(last_kernel, all_cols, m, k),
-                results,
-                [VMEM] * (1 + len(parts)),
-                "last",
-                2,
-            )(own, *parts)
+            call(last, results, [VMEM] * (1 + len(parts)), "last", 2)(own, *parts)
         )
+    blocks = call(
+        functools.partial(spread_kernel, exs, cols),
+        jax.ShapeDtypeStruct((exs * cols,) + block, f32),
+        [VMEM] * len(inputs),
+        "sketch",
+        8,
+    )(*inputs)
+    received = lax.all_to_all(blocks, ("ex", "col"), 0, 0, tiled=True)
+    own, packed = call(
+        functools.partial(gathered_kernel, exs, cols, m, k), [shape, packed], [VMEM] * 4, "score", 16
+    )(received, *split(targets))
     per = exs // cols
     rows = jnp.stack([packed[:exs], packed[exs:]], axis=1)
     grid = jnp.zeros((exs, cols) + rows.shape[1:], f32)
@@ -299,7 +356,7 @@
         axis=0,
     )
     return tuple(
-        call(functools.partial(last_kernel, all_cols, m, k), results, [VMEM] * 2, "last", 2)(own, total)
+        call(last, results, [VMEM] * 2, "last", 2)(own, total)
     )
 
 

time: 32.4 us -> 30.9 us (0.954)
  the two profiles are of different devices: /device:TPU:3 before, /device:TPU:0 now
where the time goes in v4:
time: 30.9 us; the launch traced here: 30.7 us
  starting transfers between devices  14.3 us (46%)
  waiting for transfers between devices  8.07 us (26%)
  Pallas kernels  6.92 us (22%)
  between operations  1.39 us (4%)
    ppermute x12, starting transfers between devices, shift(): lax.ppermute(x, axis, [(i, partner(i, step, count)) for i in range(count)])  14.3 us
    ppermute x12, waiting for transfers between devices, shift(): lax.ppermute(x, axis, [(i, partner(i, step, count)) for i in range(count)])  8.07 us
    pallas_call x1, Pallas kernels, on_device(): call(mix_kernel, [jax.ShapeDtypeStruct((layers * 2 * m, seq), f32), rows,...  3.03 us
    pallas_call x1, Pallas kernels, on_device(): call(sign_kernel, [signed, signed], [VMEM] * 3, 'sign', 8, [pltpu.VMEM((2...  1.69 us
    pallas_call x1, Pallas kernels, on_device(): call(functools.partial(pair_kernel, cols), [shape] * cols, [VMEM] * len(i...  0.68 us
    pallas_call x1, Pallas kernels, on_device(): call(last, results, [VMEM] * (1 + len(parts)), 'last', 2)(own, *parts)  0.65 us
  transfers between devices with their start and end apart: 12, of which 7 were waited for; matrix products, arithmetic and copies ran while one was open for 0% of the time, Pallas kernels for 19%

profile of v4, /device:TPU:0, one launch (start us, length us, event | category | flops | bytes accessed | tf_op | source)
XLA Modules:
  0.0 30.7 jit_solution(7603942603983255505)
XLA Ops:
  0.6 3.1 %collective-permute-start.7 = (f32[64,2048]{1,0:T(8,128)}, f32[64,2048]{1,0:T(8,128)S(1)}, u32[]{:S(2)}, u32[]{:S(2)}) collective-permute-start(f32[64,2048]{1,0:T(8,128)} %targets.1), channel_id=1, source_target_pairs={{0,4},{4,0},{8,12},{12,8},{1,5},{5,1},{9,13},{13,9},{2,6},{6,2},{1... | collective-permute-start | bytes 1572872 | tf_op jit(solution)/shard_map/ppermute | solution.py:36
  3.7 0.0 copy-start.1
  3.8 3.0 %mix.1 = (f32[16,256]{1,0:T(8,128)S(1)}, bf16[1,2,256,1280]{3,2,1,0:T(8,128)(2,1)S(1)}, bf16[1,2,256,1280]{3,2,1,0:T(8,128)(2,1)S(1)}) custom-call(s32[2,2,4,128]{3,2,1,0:T(4,128)} %bitcast.3, bf16[1,2,256,1280]{3,2,1,0:T(8,128)(2,1)} %hidden.1, bf16[1,2,256,1280]{3,2,1,0:T(8,128)(2,1)} %grad.1, bf16[2,128,1280]{2,1,0:T(8,128)(2,1)} %down.1, ...), custom_call_target="tpu_custom_call" | custom-call | flops 335544320 | bytes 4194304 | tf_op jit(solution)/shard_map/mix/pallas_call | solution.py:263
  6.8 0.7 %collective-permute-start = (f32[16,256]{1,0:T(8,128)S(1)}, f32[16,256]{1,0:T(8,128)S(1)}, u32[]{:S(2)}, u32[]{:S(2)}) collective-permute-start(f32[16,256]{1,0:T(8,128)S(1)} %get-tuple-element.23.own), channel_id=1, source_target_pairs={{0,3},{1,2},{2,1},{3,0},{4,7},{5,6},{6,5},{7,4},{8,11},{9,10},{10,... | collective-permute-start | bytes 49160 | tf_op jit(solution)/shard_map/ppermute | solution.py:36
  7.5 0.9 %collective-permute-start.1 = (f32[16,256]{1,0:T(8,128)S(1)}, f32[16,256]{1,0:T(8,128)S(1)}, u32[]{:S(2)}, u32[]{:S(2)}) collective-permute-start(f32[16,256]{1,0:T(8,128)S(1)} %get-tuple-element.23.own), channel_id=1, source_target_pairs={{0,2},{1,3},{2,0},{3,1},{4,6},{5,7},{6,4},{7,5},{8,10},{9,11},{10,... | collective-permute-start | bytes 49160 | tf_op jit(solution)/shard_map/ppermute | solution.py:36
  8.4 0.3 collective-permute-start.2
  8.7 0.0 copy-done.1
  8.7 1.7 %sign.1 = (bf16[2,2,512,256]{3,2,1,0:T(8,128)(2,1)S(1)}, bf16[2,2,512,256]{3,2,1,0:T(8,128)(2,1)S(1)}) custom-call(s32[2,2,32,1280]{3,2,1,0:T(8,128)S(1)} %copy-done.1, bf16[1,2,256,1280]{3,2,1,0:T(8,128)(2,1)S(1)} %get-tuple-element.24.hidden, bf16[1,2,256,1280]{3,2,1,0:T(8,128)(2,1)S(1)} %get-tuple-element.25.grad), custom_call_target="tpu_custom_call" | custom-call | flops 1342177280 | bytes 6291456 | tf_op jit(solution)/shard_map/sign/pallas_call | solution.py:280
  10.4 0.0 copy-start
  11.1 0.0 collective-permute-done.refs_0_
  11.1 0.3 collective-permute-done.1.refs_1_
  11.4 0.0 collective-permute-done.2.refs_2_
  11.4 0.7 %sketch.1 = (f32[16,128]{1,0:T(8,128)S(1)}, f32[16,128]{1,0:T(8,128)S(1)}, f32[16,128]{1,0:T(8,128)S(1)}, f32[16,128]{1,0:T(8,128)S(1)}) custom-call(s32[1,1]{1,0:T(1,128)} %bitcast.2.length, f32[16,256]{1,0:T(8,128)S(1)} %get-tuple-element.23.own, f32[16,256]{1,0:T(8,128)S(1)} %collective-permute-done.refs_0_, ...), custom_call_target="tpu_custom_call" | custom-call | tf_op jit(solution)/shard_map/sketch/pallas_call | solution.py:310
  12.1 0.9 %collective-permute-start.3 = (f32[16,128]{1,0:T(8,128)S(1)}, f32[16,128]{1,0:T(8,128)S(1)}, u32[]{:S(2)}, u32[]{:S(2)}) collective-permute-start(f32[16,128]{1,0:T(8,128)S(1)} %get-tuple-element.29), channel_id=1, source_target_pairs={{0,3},{1,2},{2,1},{3,0},{4,7},{5,6},{6,5},{7,4},{8,11},{9,10},{10,... | collective-permute-start | bytes 24584 | tf_op jit(solution)/shard_map/ppermute | solution.py:36
  13.0 0.9 %collective-permute-start.4 = (f32[16,128]{1,0:T(8,128)S(1)}, f32[16,128]{1,0:T(8,128)S(1)}, u32[]{:S(2)}, u32[]{:S(2)}) collective-permute-start(f32[16,128]{1,0:T(8,128)S(1)} %get-tuple-element.30), channel_id=1, source_target_pairs={{0,2},{1,3},{2,0},{3,1},{4,6},{5,7},{6,4},{7,5},{8,10},{9,11},{10,... | collective-permute-start | bytes 24584 | tf_op jit(solution)/shard_map/ppermute | solution.py:36
  13.8 0.1 collective-permute-start.5
  14.0 1.2 %collective-permute-done.3.refs_1_ = f32[16,128]{1,0:T(8,128)S(1)} collective-permute-done((f32[16,128]{1,0:T(8,128)S(1)}, f32[16,128]{1,0:T(8,128)S(1)}, u32[]{:S(2)}, u32[]{:S(2)}) %collective-permute-start.3) | collective-permute-done | bytes 8224 | tf_op jit(solution)/shard_map/ppermute | solution.py:36
  15.2 1.4 %collective-permute-done.4.refs_2_ = f32[16,128]{1,0:T(8,128)S(1)} collective-permute-done((f32[16,128]{1,0:T(8,128)S(1)}, f32[16,128]{1,0:T(8,128)S(1)}, u32[]{:S(2)}, u32[]{:S(2)}) %collective-permute-start.4) | collective-permute-done | bytes 8224 | tf_op jit(solution)/shard_map/ppermute | solution.py:36
  16.6 0.0 collective-permute-done.5.refs_3_
  16.6 2.7 %collective-permute-start.6 = (f32[16,128]{1,0:T(8,128)S(1)}, f32[16,128]{1,0:T(8,128)S(1)}, u32[]{:S(2)}, u32[]{:S(2)}) collective-permute-start(f32[16,128]{1,0:T(8,128)S(1)} %own.1), channel_id=1, source_target_pairs={{0,8},{4,12},{8,0},{12,4},{1,9},{5,13},{9,1},{13,5},{2,10},{6,14},... | collective-permute-start | bytes 24584 | tf_op jit(solution)/shard_map/ppermute | solution.py:36
  19.3 0.0 copy-done
  19.3 0.2 split.2
  19.5 0.0 collective-permute-done.7.targets
  19.5 0.2 split.3
  19.8 1.5 %collective-permute-done.6.other = f32[16,128]{1,0:T(8,128)S(1)} collective-permute-done((f32[16,128]{1,0:T(8,128)S(1)}, f32[16,128]{1,0:T(8,128)S(1)}, u32[]{:S(2)}, u32[]{:S(2)}) %collective-permute-start.6) | collective-permute-done | bytes 8224 | tf_op jit(solution)/shard_map/ppermute | solution.py:36
  21.2 0.4 %score.1 = (f32[8,128]{1,0:T(8,128)S(1)}, f32[8,128]{1,0:T(8,128)S(1)}) custom-call(f32[16,128]{1,0:T(8,128)S(1)} %own.1, f32[16,128]{1,0:T(8,128)S(1)} %collective-permute-done.6.other, bf16[64,2048]{1,0:T(8,128)(2,1)S(1)} %get-tuple-element.32.refs_0_, bf16[64,2048]{1,0:T(8,128)(2,1)S(1)} %get-tuple-element.33.refs_1_, ...), custom_call_target="tpu_custom_call" | custom-call | tf_op jit(solution)/shard_map/score/pallas_call | solution.py:322
  21.6 2.6 %collective-permute-start.8 = (f32[8,128]{1,0:T(8,128)S(1)}, f32[8,128]{1,0:T(8,128)S(1)}, u32[]{:S(2)}, u32[]{:S(2)}) collective-permute-start(f32[8,128]{1,0:T(8,128)S(1)} %get-tuple-element.39), channel_id=1, source_target_pairs={{0,8},{4,12},{8,0},{12,4},{1,9},{5,13},{9,1},{13,5},{2,10},{6,14},... | collective-permute-start | bytes 12296 | tf_op jit(solution)/shard_map/ppermute | solution.py:36
  24.2 1.9 %collective-permute-done.8.remote = f32[8,128]{1,0:T(8,128)S(1)} collective-permute-done((f32[8,128]{1,0:T(8,128)S(1)}, f32[8,128]{1,0:T(8,128)S(1)}, u32[]{:S(2)}, u32[]{:S(2)}) %collective-permute-start.8) | collective-permute-done | bytes 4128 | tf_op jit(solution)/shard_map/ppermute | solution.py:36
  26.1 0.9 %collective-permute-start.10 = (f32[8,128]{1,0:T(8,128)S(1)}, f32[8,128]{1,0:T(8,128)S(1)}, u32[]{:S(2)}, u32[]{:S(2)}) collective-permute-start(f32[8,128]{1,0:T(8,128)S(1)} %get-tuple-element.42), channel_id=1, source_target_pairs={{0,2},{1,3},{2,0},{3,1},{4,6},{5,7},{6,4},{7,5},{8,10},{9,11},{10,... | collective-permute-start | bytes 12296 | tf_op jit(solution)/shard_map/ppermute | solution.py:36
  27.0 0.0 collective-permute-start.11
  27.0 1.3 %collective-permute-start.9 = (f32[8,128]{1,0:T(8,128)S(1)}, f32[8,128]{1,0:T(8,128)S(1)}, u32[]{:S(2)}, u32[]{:S(2)}) collective-permute-start(f32[8,128]{1,0:T(8,128)S(1)} %get-tuple-element.41), channel_id=1, source_target_pairs={{0,3},{1,2},{2,1},{3,0},{4,7},{5,6},{6,5},{7,4},{8,11},{9,10},{10,... | collective-permute-start | bytes 12296 | tf_op jit(solution)/shard_map/ppermute | solution.py:36
  28.3 1.5 %collective-permute-done.10.refs_2_ = f32[8,128]{1,0:T(8,128)S(1)} collective-permute-done((f32[8,128]{1,0:T(8,128)S(1)}, f32[8,128]{1,0:T(8,128)S(1)}, u32[]{:S(2)}, u32[]{:S(2)}) %collective-permute-start.10) | collective-permute-done | bytes 4128 | tf_op jit(solution)/shard_map/ppermute | solution.py:36
  29.8 0.0 collective-permute-done.11.refs_3_
  29.8 0.3 collective-permute-done.9.refs_1_
  30.1 0.7 %last.1 = (f32[1,2048]{1,0:T(1,128)}, f32[1,64]{1,0:T(1,128)}) custom-call(f32[16,128]{1,0:T(8,128)S(1)} %own.1, f32[8,128]{1,0:T(8,128)S(1)} %get-tuple-element.40.refs_0_, f32[8,128]{1,0:T(8,128)S(1)} %collective-permute-done.9.refs_1_, f32[8,128]{1,0:T(8,128)S(1)} %collective-permute-done.10.refs_2_, f32[8,128]{1,0:T(8,128)S(1)} %collective-permute-done.11.refs_3_), custom_call_target="tpu_custom_call" | custom-call | tf_op jit(solution)/shard_map/last/pallas_call | solution.py:330
  (2 shorter events, 0.0 us)
Async XLA Ops:
  0.6 18.9 %collective-permute-start.7 = (f32[64,2048]{1,0:T(8,128)}, f32[64,2048]{1,0:T(8,128)S(1)}, u32[]{:S(2)}, u32[]{:S(2)}) collective-permute-start(f32[64,2048]{1,0:T(8,128)} %targets.1), channel_id=1, source_target_pairs={{0,4},{4,0},{8,12},{12,8},{1,5},{5,1},{9,13},{13,9},{2,6},{6,2},{1... | collective-permute-start | bytes 1572872 | tf_op jit(solution)/shard_map/ppermute | solution.py:36
  3.7 5.0 %copy-start.1 = (s32[2,2,32,1280]{3,2,1,0:T(8,128)S(1)}, s32[2,2,32,1280]{3,2,1,0:T(8,128)}, u32[]{:S(2)}) copy-start(s32[2,2,32,1280]{3,2,1,0:T(8,128)} %words.1) | copy-start | bytes 1966084
  6.8 4.3 %collective-permute-start = (f32[16,256]{1,0:T(8,128)S(1)}, f32[16,256]{1,0:T(8,128)S(1)}, u32[]{:S(2)}, u32[]{:S(2)}) collective-permute-start(f32[16,256]{1,0:T(8,128)S(1)} %get-tuple-element.23.own), channel_id=1, source_target_pairs={{0,3},{1,2},{2,1},{3,0},{4,7},{5,6},{6,5},{7,4},{8,11},{9,10},{10,... | collective-permute-start | bytes 49160 | tf_op jit(solution)/shard_map/ppermute | solution.py:36
  7.5 3.9 %collective-permute-start.1 = (f32[16,256]{1,0:T(8,128)S(1)}, f32[16,256]{1,0:T(8,128)S(1)}, u32[]{:S(2)}, u32[]{:S(2)}) collective-permute-start(f32[16,256]{1,0:T(8,128)S(1)} %get-tuple-element.23.own), channel_id=1, source_target_pairs={{0,2},{1,3},{2,0},{3,1},{4,6},{5,7},{6,4},{7,5},{8,10},{9,11},{10,... | collective-permute-start | bytes 49160 | tf_op jit(solution)/shard_map/ppermute | solution.py:36
  8.4 3.0 %collective-permute-start.2 = (f32[16,256]{1,0:T(8,128)S(1)}, f32[16,256]{1,0:T(8,128)S(1)}, u32[]{:S(2)}, u32[]{:S(2)}) collective-permute-start(f32[16,256]{1,0:T(8,128)S(1)} %get-tuple-element.23.own), channel_id=1, source_target_pairs={{0,1},{1,0},{2,3},{3,2},{4,5},{5,4},{6,7},{7,6},{8,9},{9,8},{10,11... | collective-permute-start | bytes 49160 | tf_op jit(solution)/shard_map/ppermute | solution.py:36
  10.4 8.9 %copy-start = (f32[64,2048]{1,0:T(8,128)S(1)}, f32[64,2048]{1,0:T(8,128)}, u32[]{:S(2)}) copy-start(f32[64,2048]{1,0:T(8,128)} %targets.1) | copy-start | bytes 1572868
  12.1 3.1 %collective-permute-start.3 = (f32[16,128]{1,0:T(8,128)S(1)}, f32[16,128]{1,0:T(8,128)S(1)}, u32[]{:S(2)}, u32[]{:S(2)}) collective-permute-start(f32[16,128]{1,0:T(8,128)S(1)} %get-tuple-element.29), channel_id=1, source_target_pairs={{0,3},{1,2},{2,1},{3,0},{4,7},{5,6},{6,5},{7,4},{8,11},{9,10},{10,... | collective-permute-start | bytes 24584 | tf_op jit(solution)/shard_map/ppermute | solution.py:36
  13.0 3.7 %collective-permute-start.4 = (f32[16,128]{1,0:T(8,128)S(1)}, f32[16,128]{1,0:T(8,128)S(1)}, u32[]{:S(2)}, u32[]{:S(2)}) collective-permute-start(f32[16,128]{1,0:T(8,128)S(1)} %get-tuple-element.30), channel_id=1, source_target_pairs={{0,2},{1,3},{2,0},{3,1},{4,6},{5,7},{6,4},{7,5},{8,10},{9,11},{10,... | collective-permute-start | bytes 24584 | tf_op jit(solution)/shard_map/ppermute | solution.py:36
  13.8 2.8 %collective-permute-start.5 = (f32[16,128]{1,0:T(8,128)S(1)}, f32[16,128]{1,0:T(8,128)S(1)}, u32[]{:S(2)}, u32[]{:S(2)}) collective-permute-start(f32[16,128]{1,0:T(8,128)S(1)} %get-tuple-element.31), channel_id=1, source_target_pairs={{0,1},{1,0},{2,3},{3,2},{4,5},{5,4},{6,7},{7,6},{8,9},{9,8},{10,11... | collective-permute-start | bytes 24584 | tf_op jit(solution)/shard_map/ppermute | solution.py:36
  16.6 4.6 %collective-permute-start.6 = (f32[16,128]{1,0:T(8,128)S(1)}, f32[16,128]{1,0:T(8,128)S(1)}, u32[]{:S(2)}, u32[]{:S(2)}) collective-permute-start(f32[16,128]{1,0:T(8,128)S(1)} %own.1), channel_id=1, source_target_pairs={{0,8},{4,12},{8,0},{12,4},{1,9},{5,13},{9,1},{13,5},{2,10},{6,14},... | collective-permute-start | bytes 24584 | tf_op jit(solution)/shard_map/ppermute | solution.py:36
  21.6 4.5 %collective-permute-start.8 = (f32[8,128]{1,0:T(8,128)S(1)}, f32[8,128]{1,0:T(8,128)S(1)}, u32[]{:S(2)}, u32[]{:S(2)}) collective-permute-start(f32[8,128]{1,0:T(8,128)S(1)} %get-tuple-element.39), channel_id=1, source_target_pairs={{0,8},{4,12},{8,0},{12,4},{1,9},{5,13},{9,1},{13,5},{2,10},{6,14},... | collective-permute-start | bytes 12296 | tf_op jit(solution)/shard_map/ppermute | solution.py:36
  26.1 3.6 %collective-permute-start.10 = (f32[8,128]{1,0:T(8,128)S(1)}, f32[8,128]{1,0:T(8,128)S(1)}, u32[]{:S(2)}, u32[]{:S(2)}) collective-permute-start(f32[8,128]{1,0:T(8,128)S(1)} %get-tuple-element.42), channel_id=1, source_target_pairs={{0,2},{1,3},{2,0},{3,1},{4,6},{5,7},{6,4},{7,5},{8,10},{9,11},{10,... | collective-permute-start | bytes 12296 | tf_op jit(solution)/shard_map/ppermute | solution.py:36
  27.0 2.7 %collective-permute-start.11 = (f32[8,128]{1,0:T(8,128)S(1)}, f32[8,128]{1,0:T(8,128)S(1)}, u32[]{:S(2)}, u32[]{:S(2)}) collective-permute-start(f32[8,128]{1,0:T(8,128)S(1)} %get-tuple-element.43), channel_id=1, source_target_pairs={{0,1},{1,0},{2,3},{3,2},{4,5},{5,4},{6,7},{7,6},{8,9},{9,8},{10,11... | collective-permute-start | bytes 12296 | tf_op jit(solution)/shard_map/ppermute | solution.py:36
  27.0 3.0 %collective-permute-start.9 = (f32[8,128]{1,0:T(8,128)S(1)}, f32[8,128]{1,0:T(8,128)S(1)}, u32[]{:S(2)}, u32[]{:S(2)}) collective-permute-start(f32[8,128]{1,0:T(8,128)S(1)} %get-tuple-element.41), channel_id=1, source_target_pairs={{0,3},{1,2},{2,1},{3,0},{4,7},{5,6},{6,5},{7,4},{8,11},{9,10},{10,... | collective-permute-start | bytes 12296 | tf_op jit(solution)/shard_map/ppermute | solution.py:36

commit v5 on v4

--- a/solution.py
+++ b/solution.py
@@ -10,7 +10,7 @@
 
 epsilon = 1e-06
 WORD = 16
-STEPS = (3, 2, 1)
+STEPS = (1, 2, 3)
 LANES = 128
 f32, bf16 = jnp.float32, jnp.bfloat16
 MIB = 1 << 20
@@ -21,6 +21,10 @@
 
 def contract_last(a, b):
     return lax.dot_general(a, b, (((1,), (1,)), ((), ())), preferred_element_type=f32)
+
+
+def product(a, b):
+    return jnp.dot(a, b, preferred_element_type=f32)
 
 
 def halves(x):
@@ -59,7 +63,7 @@
     for l, j in sides:
         signs = (2 * right_buf[l, j] - 1).astype(f32).astype(bf16)
         if j == 0:
-            folded = jnp.dot(signs, down_buf[l], preferred_element_type=f32)
+            folded = product(signs, down_buf[l])
         else:
             folded = contract_last(signs, up_buf[l])
         pairs.append(jnp.concatenate(halves(folded), axis=0))
@@ -92,7 +96,7 @@
     for i, (l, j) in enumerate(items):
         if i + 1 < len(items):
             unpack(words, *items[i + 1], signs.at[(i + 1) % 2])
-        signed = contract_last(signs[i % 2], (grad if j == 0 else hidden)[0, l])
+        signed = contract_last((grad if j == 0 else hidden)[0, l], signs[i % 2])
         high[l, j], low[l, j] = halves(signed)
 
 
@@ -103,14 +107,14 @@
     n = length[...]
     positions = lax.broadcasted_iota(jnp.int32, (1, mixed.shape[1]), 1)
     mixed = mixed * jnp.where(positions < n, 1.0 / n.astype(f32), 0.0)
-    layers, sides, k = high.shape[:3]
+    layers, sides, _, k = high.shape
     m = mixed.shape[0] // (layers * sides)
     pieces = []
     for l in range(layers):
         for j in range(sides):
             base = (2 * l + j) * m
             pair = jnp.concatenate(halves(mixed[base : base + m]), axis=0)
-            both = contract_last(pair, high[l, j]) + contract_last(pair, low[l, j])
+            both = product(pair, high[l, j]) + product(pair, low[l, j])
             both = both[:m] + both[m:]
             pieces += [both[:, q : q + LANES] for q in range(0, k, LANES)]
     per = len(pieces) // cols
@@ -276,7 +280,7 @@
         4 * MIB,
     )(*in_hbm(right, hidden_input, output_gradient, adapter_down, adapter_up))
     others = [shift(mixed, "col", cols, s) for s in range(cols - 1, 0, -1)]
-    signed = jax.ShapeDtypeStruct((layers, 2, k, seq), bf16)
+    signed = jax.ShapeDtypeStruct((layers, 2, seq, k), bf16)
     high, low = call(
         sign_kernel,
         [signed, signed],

time: 30.9 us -> 30.5 us (0.987)
  no operation moved by 1% of the time
where the time goes in v5:
time: 30.5 us; the launch traced here: 30.3 us
  starting transfers between devices  14.3 us (47%)
  waiting for transfers between devices  7.77 us (25%)
  Pallas kernels  6.89 us (23%)
  between operations  1.38 us (5%)
    ppermute x12, starting transfers between devices, shift(): lax.ppermute(x, axis, [(i, partner(i, step, count)) for i in range(count)])  14.3 us
    ppermute x12, waiting for transfers between devices, shift(): lax.ppermute(x, axis, [(i, partner(i, step, count)) for i in range(count)])  7.77 us
    pallas_call x1, Pallas kernels, on_device(): call(mix_kernel, [jax.ShapeDtypeStruct((layers * 2 * m, seq), f32), rows,...  3.03 us
    pallas_call x1, Pallas kernels, on_device(): call(sign_kernel, [signed, signed], [VMEM] * 3, 'sign', 8, [pltpu.VMEM((2...  1.88 us
    pallas_call x1, Pallas kernels, on_device(): call(last, results, [VMEM] * (1 + len(parts)), 'last', 2)(own, *parts)  0.66 us
  transfers between devices with their start and end apart: 12, of which 7 were waited for; matrix products, arithmetic and copies ran while one was open for 0% of the time, Pallas kernels for 19%

profile of v5, /device:TPU:0, one launch (start us, length us, event | category | flops | bytes accessed | tf_op | source)
XLA Modules:
  0.0 30.3 jit_solution(8292315690788479144)
XLA Ops:
  0.6 3.1 %collective-permute-start.7 = (f32[64,2048]{1,0:T(8,128)}, f32[64,2048]{1,0:T(8,128)S(1)}, u32[]{:S(2)}, u32[]{:S(2)}) collective-permute-start(f32[64,2048]{1,0:T(8,128)} %targets.1), channel_id=1, source_target_pairs={{0,4},{4,0},{8,12},{12,8},{1,5},{5,1},{9,13},{13,9},{2,6},{6,2},{1... | collective-permute-start | bytes 1572872 | tf_op jit(solution)/shard_map/ppermute | solution.py:40
  3.7 0.0 copy-start.1
  3.8 3.0 %mix.1 = (f32[16,256]{1,0:T(8,128)S(1)}, bf16[1,2,256,1280]{3,2,1,0:T(8,128)(2,1)S(1)}, bf16[1,2,256,1280]{3,2,1,0:T(8,128)(2,1)S(1)}) custom-call(s32[2,2,4,128]{3,2,1,0:T(4,128)} %bitcast.3, bf16[1,2,256,1280]{3,2,1,0:T(8,128)(2,1)} %hidden.1, bf16[1,2,256,1280]{3,2,1,0:T(8,128)(2,1)} %grad.1, bf16[2,128,1280]{2,1,0:T(8,128)(2,1)} %down.1, ...), custom_call_target="tpu_custom_call" | custom-call | flops 335544320 | bytes 4194304 | tf_op jit(solution)/shard_map/mix/pallas_call | solution.py:267
  6.8 0.7 %collective-permute-start = (f32[16,256]{1,0:T(8,128)S(1)}, f32[16,256]{1,0:T(8,128)S(1)}, u32[]{:S(2)}, u32[]{:S(2)}) collective-permute-start(f32[16,256]{1,0:T(8,128)S(1)} %get-tuple-element.23.own), channel_id=1, source_target_pairs={{0,3},{1,2},{2,1},{3,0},{4,7},{5,6},{6,5},{7,4},{8,11},{9,10},{10,... | collective-permute-start | bytes 49160 | tf_op jit(solution)/shard_map/ppermute | solution.py:40
  7.5 0.9 %collective-permute-start.1 = (f32[16,256]{1,0:T(8,128)S(1)}, f32[16,256]{1,0:T(8,128)S(1)}, u32[]{:S(2)}, u32[]{:S(2)}) collective-permute-start(f32[16,256]{1,0:T(8,128)S(1)} %get-tuple-element.23.own), channel_id=1, source_target_pairs={{0,2},{1,3},{2,0},{3,1},{4,6},{5,7},{6,4},{7,5},{8,10},{9,11},{10,... | collective-permute-start | bytes 49160 | tf_op jit(solution)/shard_map/ppermute | solution.py:40
  8.4 0.3 collective-permute-start.2
  8.7 0.0 copy-done.1
  8.7 1.9 %sign.1 = (bf16[2,2,256,512]{3,2,1,0:T(8,128)(2,1)S(1)}, bf16[2,2,256,512]{3,2,1,0:T(8,128)(2,1)S(1)}) custom-call(s32[2,2,32,1280]{3,2,1,0:T(8,128)S(1)} %copy-done.1, bf16[1,2,256,1280]{3,2,1,0:T(8,128)(2,1)S(1)} %get-tuple-element.24.hidden, bf16[1,2,256,1280]{3,2,1,0:T(8,128)(2,1)S(1)} %get-tuple-element.25.grad), custom_call_target="tpu_custom_call" | custom-call | flops 1342177280 | bytes 6291456 | tf_op jit(solution)/shard_map/sign/pallas_call | solution.py:284
  10.6 0.0 copy-start
  11.3 0.0 collective-permute-done.refs_0_
  11.3 0.1 collective-permute-done.1.refs_1_
  11.4 0.0 collective-permute-done.2.refs_2_
  11.4 0.4 %sketch.1 = (f32[16,128]{1,0:T(8,128)S(1)}, f32[16,128]{1,0:T(8,128)S(1)}, f32[16,128]{1,0:T(8,128)S(1)}, f32[16,128]{1,0:T(8,128)S(1)}) custom-call(s32[1,1]{1,0:T(1,128)} %bitcast.2.length, f32[16,256]{1,0:T(8,128)S(1)} %get-tuple-element.23.own, f32[16,256]{1,0:T(8,128)S(1)} %collective-permute-done.refs_0_, ...), custom_call_target="tpu_custom_call" | custom-call | tf_op jit(solution)/shard_map/sketch/pallas_call | solution.py:314
  11.9 0.2 collective-permute-start.3
  12.1 1.4 %collective-permute-start.4 = (f32[16,128]{1,0:T(8,128)S(1)}, f32[16,128]{1,0:T(8,128)S(1)}, u32[]{:S(2)}, u32[]{:S(2)}) collective-permute-start(f32[16,128]{1,0:T(8,128)S(1)} %get-tuple-element.30), channel_id=1, source_target_pairs={{0,2},{1,3},{2,0},{3,1},{4,6},{5,7},{6,4},{7,5},{8,10},{9,11},{10,... | collective-permute-start | bytes 24584 | tf_op jit(solution)/shard_map/ppermute | solution.py:40
  13.4 0.3 %collective-permute-start.5 = (f32[16,128]{1,0:T(8,128)S(1)}, f32[16,128]{1,0:T(8,128)S(1)}, u32[]{:S(2)}, u32[]{:S(2)}) collective-permute-start(f32[16,128]{1,0:T(8,128)S(1)} %get-tuple-element.31), channel_id=1, source_target_pairs={{0,3},{1,2},{2,1},{3,0},{4,7},{5,6},{6,5},{7,4},{8,11},{9,10},{10,... | collective-permute-start | bytes 24584 | tf_op jit(solution)/shard_map/ppermute | solution.py:40
  13.8 0.0 collective-permute-done.3.refs_1_
  13.8 2.0 %collective-permute-done.4.refs_2_ = f32[16,128]{1,0:T(8,128)S(1)} collective-permute-done((f32[16,128]{1,0:T(8,128)S(1)}, f32[16,128]{1,0:T(8,128)S(1)}, u32[]{:S(2)}, u32[]{:S(2)}) %collective-permute-start.4) | collective-permute-done | bytes 8224 | tf_op jit(solution)/shard_map/ppermute | solution.py:40
  15.7 0.8 %collective-permute-done.5.refs_3_ = f32[16,128]{1,0:T(8,128)S(1)} collective-permute-done((f32[16,128]{1,0:T(8,128)S(1)}, f32[16,128]{1,0:T(8,128)S(1)}, u32[]{:S(2)}, u32[]{:S(2)}) %collective-permute-start.5) | collective-permute-done | bytes 8224 | tf_op jit(solution)/shard_map/ppermute | solution.py:40
  16.5 2.6 %collective-permute-start.6 = (f32[16,128]{1,0:T(8,128)S(1)}, f32[16,128]{1,0:T(8,128)S(1)}, u32[]{:S(2)}, u32[]{:S(2)}) collective-permute-start(f32[16,128]{1,0:T(8,128)S(1)} %own.1), channel_id=1, source_target_pairs={{0,8},{4,12},{8,0},{12,4},{1,9},{5,13},{9,1},{13,5},{2,10},{6,14},... | collective-permute-start | bytes 24584 | tf_op jit(solution)/shard_map/ppermute | solution.py:40
  19.1 0.0 copy-done
  19.1 0.2 split.2
  19.3 0.0 collective-permute-done.7.targets
  19.3 0.2 split.3
  19.6 1.5 %collective-permute-done.6.other = f32[16,128]{1,0:T(8,128)S(1)} collective-permute-done((f32[16,128]{1,0:T(8,128)S(1)}, f32[16,128]{1,0:T(8,128)S(1)}, u32[]{:S(2)}, u32[]{:S(2)}) %collective-permute-start.6) | collective-permute-done | bytes 8224 | tf_op jit(solution)/shard_map/ppermute | solution.py:40
  21.0 0.4 %score.1 = (f32[8,128]{1,0:T(8,128)S(1)}, f32[8,128]{1,0:T(8,128)S(1)}) custom-call(f32[16,128]{1,0:T(8,128)S(1)} %own.1, f32[16,128]{1,0:T(8,128)S(1)} %collective-permute-done.6.other, bf16[64,2048]{1,0:T(8,128)(2,1)S(1)} %get-tuple-element.32.refs_0_, bf16[64,2048]{1,0:T(8,128)(2,1)S(1)} %get-tuple-element.33.refs_1_, ...), custom_call_target="tpu_custom_call" | custom-call | tf_op jit(solution)/shard_map/score/pallas_call | solution.py:326
  21.4 2.6 %collective-permute-start.8 = (f32[8,128]{1,0:T(8,128)S(1)}, f32[8,128]{1,0:T(8,128)S(1)}, u32[]{:S(2)}, u32[]{:S(2)}) collective-permute-start(f32[8,128]{1,0:T(8,128)S(1)} %get-tuple-element.39), channel_id=1, source_target_pairs={{0,8},{4,12},{8,0},{12,4},{1,9},{5,13},{9,1},{13,5},{2,10},{6,14},... | collective-permute-start | bytes 12296 | tf_op jit(solution)/shard_map/ppermute | solution.py:40
  24.0 1.9 %collective-permute-done.8.remote = f32[8,128]{1,0:T(8,128)S(1)} collective-permute-done((f32[8,128]{1,0:T(8,128)S(1)}, f32[8,128]{1,0:T(8,128)S(1)}, u32[]{:S(2)}, u32[]{:S(2)}) %collective-permute-start.8) | collective-permute-done | bytes 4128 | tf_op jit(solution)/shard_map/ppermute | solution.py:40
  26.0 0.7 %collective-permute-start.10 = (f32[8,128]{1,0:T(8,128)S(1)}, f32[8,128]{1,0:T(8,128)S(1)}, u32[]{:S(2)}, u32[]{:S(2)}) collective-permute-start(f32[8,128]{1,0:T(8,128)S(1)} %get-tuple-element.42), channel_id=1, source_target_pairs={{0,2},{1,3},{2,0},{3,1},{4,6},{5,7},{6,4},{7,5},{8,10},{9,11},{10,... | collective-permute-start | bytes 12296 | tf_op jit(solution)/shard_map/ppermute | solution.py:40
  26.6 0.0 collective-permute-start.11
  26.6 1.5 %collective-permute-start.9 = (f32[8,128]{1,0:T(8,128)S(1)}, f32[8,128]{1,0:T(8,128)S(1)}, u32[]{:S(2)}, u32[]{:S(2)}) collective-permute-start(f32[8,128]{1,0:T(8,128)S(1)} %get-tuple-element.41), channel_id=1, source_target_pairs={{0,1},{1,0},{2,3},{3,2},{4,5},{5,4},{6,7},{7,6},{8,9},{9,8},{10,11... | collective-permute-start | bytes 12296 | tf_op jit(solution)/shard_map/ppermute | solution.py:40
  28.1 1.5 %collective-permute-done.10.refs_2_ = f32[8,128]{1,0:T(8,128)S(1)} collective-permute-done((f32[8,128]{1,0:T(8,128)S(1)}, f32[8,128]{1,0:T(8,128)S(1)}, u32[]{:S(2)}, u32[]{:S(2)}) %collective-permute-start.10) | collective-permute-done | bytes 4128 | tf_op jit(solution)/shard_map/ppermute | solution.py:40
  29.6 0.1 collective-permute-done.11.refs_3_
  29.7 0.0 collective-permute-done.9.refs_1_
  29.7 0.7 %last.1 = (f32[1,2048]{1,0:T(1,128)}, f32[1,64]{1,0:T(1,128)}) custom-call(f32[16,128]{1,0:T(8,128)S(1)} %own.1, f32[8,128]{1,0:T(8,128)S(1)} %get-tuple-element.40.refs_0_, f32[8,128]{1,0:T(8,128)S(1)} %collective-permute-done.9.refs_1_, f32[8,128]{1,0:T(8,128)S(1)} %collective-permute-done.10.refs_2_, f32[8,128]{1,0:T(8,128)S(1)} %collective-permute-done.11.refs_3_), custom_call_target="tpu_custom_call" | custom-call | tf_op jit(solution)/shard_map/last/pallas_call | solution.py:334
  (2 shorter events, 0.0 us)
Async XLA Ops:
  0.6 18.7 %collective-permute-start.7 = (f32[64,2048]{1,0:T(8,128)}, f32[64,2048]{1,0:T(8,128)S(1)}, u32[]{:S(2)}, u32[]{:S(2)}) collective-permute-start(f32[64,2048]{1,0:T(8,128)} %targets.1), channel_id=1, source_target_pairs={{0,4},{4,0},{8,12},{12,8},{1,5},{5,1},{9,13},{13,9},{2,6},{6,2},{1... | collective-permute-start | bytes 1572872 | tf_op jit(solution)/shard_map/ppermute | solution.py:40
  3.7 5.0 %copy-start.1 = (s32[2,2,32,1280]{3,2,1,0:T(8,128)S(1)}, s32[2,2,32,1280]{3,2,1,0:T(8,128)}, u32[]{:S(2)}) copy-start(s32[2,2,32,1280]{3,2,1,0:T(8,128)} %words.1) | copy-start | bytes 1966084
  6.8 4.5 %collective-permute-start = (f32[16,256]{1,0:T(8,128)S(1)}, f32[16,256]{1,0:T(8,128)S(1)}, u32[]{:S(2)}, u32[]{:S(2)}) collective-permute-start(f32[16,256]{1,0:T(8,128)S(1)} %get-tuple-element.23.own), channel_id=1, source_target_pairs={{0,3},{1,2},{2,1},{3,0},{4,7},{5,6},{6,5},{7,4},{8,11},{9,10},{10,... | collective-permute-start | bytes 49160 | tf_op jit(solution)/shard_map/ppermute | solution.py:40
  7.5 3.9 %collective-permute-start.1 = (f32[16,256]{1,0:T(8,128)S(1)}, f32[16,256]{1,0:T(8,128)S(1)}, u32[]{:S(2)}, u32[]{:S(2)}) collective-permute-start(f32[16,256]{1,0:T(8,128)S(1)} %get-tuple-element.23.own), channel_id=1, source_target_pairs={{0,2},{1,3},{2,0},{3,1},{4,6},{5,7},{6,4},{7,5},{8,10},{9,11},{10,... | collective-permute-start | bytes 49160 | tf_op jit(solution)/shard_map/ppermute | solution.py:40
  8.4 3.0 %collective-permute-start.2 = (f32[16,256]{1,0:T(8,128)S(1)}, f32[16,256]{1,0:T(8,128)S(1)}, u32[]{:S(2)}, u32[]{:S(2)}) collective-permute-start(f32[16,256]{1,0:T(8,128)S(1)} %get-tuple-element.23.own), channel_id=1, source_target_pairs={{0,1},{1,0},{2,3},{3,2},{4,5},{5,4},{6,7},{7,6},{8,9},{9,8},{10,11... | collective-permute-start | bytes 49160 | tf_op jit(solution)/shard_map/ppermute | solution.py:40
  10.6 8.5 %copy-start = (f32[64,2048]{1,0:T(8,128)S(1)}, f32[64,2048]{1,0:T(8,128)}, u32[]{:S(2)}) copy-start(f32[64,2048]{1,0:T(8,128)} %targets.1) | copy-start | bytes 1572868
  11.9 1.9 %collective-permute-start.3 = (f32[16,128]{1,0:T(8,128)S(1)}, f32[16,128]{1,0:T(8,128)S(1)}, u32[]{:S(2)}, u32[]{:S(2)}) collective-permute-start(f32[16,128]{1,0:T(8,128)S(1)} %get-tuple-element.29), channel_id=1, source_target_pairs={{0,1},{1,0},{2,3},{3,2},{4,5},{5,4},{6,7},{7,6},{8,9},{9,8},{10,11... | collective-permute-start | bytes 24584 | tf_op jit(solution)/shard_map/ppermute | solution.py:40
  12.1 3.7 %collective-permute-start.4 = (f32[16,128]{1,0:T(8,128)S(1)}, f32[16,128]{1,0:T(8,128)S(1)}, u32[]{:S(2)}, u32[]{:S(2)}) collective-permute-start(f32[16,128]{1,0:T(8,128)S(1)} %get-tuple-element.30), channel_id=1, source_target_pairs={{0,2},{1,3},{2,0},{3,1},{4,6},{5,7},{6,4},{7,5},{8,10},{9,11},{10,... | collective-permute-start | bytes 24584 | tf_op jit(solution)/shard_map/ppermute | solution.py:40
  13.4 3.1 %collective-permute-start.5 = (f32[16,128]{1,0:T(8,128)S(1)}, f32[16,128]{1,0:T(8,128)S(1)}, u32[]{:S(2)}, u32[]{:S(2)}) collective-permute-start(f32[16,128]{1,0:T(8,128)S(1)} %get-tuple-element.31), channel_id=1, source_target_pairs={{0,3},{1,2},{2,1},{3,0},{4,7},{5,6},{6,5},{7,4},{8,11},{9,10},{10,... | collective-permute-start | bytes 24584 | tf_op jit(solution)/shard_map/ppermute | solution.py:40
  16.5 4.5 %collective-permute-start.6 = (f32[16,128]{1,0:T(8,128)S(1)}, f32[16,128]{1,0:T(8,128)S(1)}, u32[]{:S(2)}, u32[]{:S(2)}) collective-permute-start(f32[16,128]{1,0:T(8,128)S(1)} %own.1), channel_id=1, source_target_pairs={{0,8},{4,12},{8,0},{12,4},{1,9},{5,13},{9,1},{13,5},{2,10},{6,14},... | collective-permute-start | bytes 24584 | tf_op jit(solution)/shard_map/ppermute | solution.py:40
  21.4 4.5 %collective-permute-start.8 = (f32[8,128]{1,0:T(8,128)S(1)}, f32[8,128]{1,0:T(8,128)S(1)}, u32[]{:S(2)}, u32[]{:S(2)}) collective-permute-start(f32[8,128]{1,0:T(8,128)S(1)} %get-tuple-element.39), channel_id=1, source_target_pairs={{0,8},{4,12},{8,0},{12,4},{1,9},{5,13},{9,1},{13,5},{2,10},{6,14},... | collective-permute-start | bytes 12296 | tf_op jit(solution)/shard_map/ppermute | solution.py:40
  26.0 3.6 %collective-permute-start.10 = (f32[8,128]{1,0:T(8,128)S(1)}, f32[8,128]{1,0:T(8,128)S(1)}, u32[]{:S(2)}, u32[]{:S(2)}) collective-permute-start(f32[8,128]{1,0:T(8,128)S(1)} %get-tuple-element.42), channel_id=1, source_target_pairs={{0,2},{1,3},{2,0},{3,1},{4,6},{5,7},{6,4},{7,5},{8,10},{9,11},{10,... | collective-permute-start | bytes 12296 | tf_op jit(solution)/shard_map/ppermute | solution.py:40
  26.6 3.0 %collective-permute-start.11 = (f32[8,128]{1,0:T(8,128)S(1)}, f32[8,128]{1,0:T(8,128)S(1)}, u32[]{:S(2)}, u32[]{:S(2)}) collective-permute-start(f32[8,128]{1,0:T(8,128)S(1)} %get-tuple-element.43), channel_id=1, source_target_pairs={{0,3},{1,2},{2,1},{3,0},{4,7},{5,6},{6,5},{7,4},{8,11},{9,10},{10,... | collective-permute-start | bytes 12296 | tf_op jit(solution)/shard_map/ppermute | solution.py:40
  26.6 3.0 %collective-permute-start.9 = (f32[8,128]{1,0:T(8,128)S(1)}, f32[8,128]{1,0:T(8,128)S(1)}, u32[]{:S(2)}, u32[]{:S(2)}) collective-permute-start(f32[8,128]{1,0:T(8,128)S(1)} %get-tuple-element.41), channel_id=1, source_target_pairs={{0,1},{1,0},{2,3},{3,2},{4,5},{5,4},{6,7},{7,6},{8,9},{9,8},{10,11... | collective-permute-start | bytes 12296 | tf_op jit(solution)/shard_map/ppermute | solution.py:40

commit v6 on v5

--- a/solution.py
+++ b/solution.py
@@ -14,6 +14,11 @@
 LANES = 128
 f32, bf16 = jnp.float32, jnp.bfloat16
 MIB = 1 << 20
+
+def crossed(x, exs, cols):
+    pairs = [(e * cols + i, (e ^ 2) * cols + (i ^ 1)) for e in range(exs) for i in range(cols)]
+    return lax.ppermute(x, ("ex", "col"), pairs)
+
 
 VMEM = pl.BlockSpec(memory_space=pltpu.VMEM)
 HBM = pl.BlockSpec(memory_space=pltpu.HBM)
@@ -134,14 +139,16 @@
         table[i] = block
     me = lax.axis_index("col")
     for step, out in enumerate(outs):
-        out[...] = table[partner(me, step, cols)]
+        to = partner(me, step, cols)
+        out[0] = table[to]
+        out[1] = table[to ^ 1]
 
 
 def sum_kernel(*refs):
-    total = refs[0][...]
-    for ref in refs[1:-1]:
-        total = total + ref[...]
-    refs[-1][...] = total
+    *parts, own, pair = refs
+    total = sum(part[...] for part in parts)
+    own[...] = total[0]
+    pair[...] = total[1]
 
 
 def column_starts(m, k, count):
@@ -313,22 +320,22 @@
     if exs == 4 and cols == 4:
         blocks = call(
             functools.partial(pair_kernel, cols),
-            [shape] * cols,
+            [jax.ShapeDtypeStruct((2,) + block, f32)] * cols,
             [VMEM] * len(inputs),
             "sketch",
             8,
             [pltpu.VMEM((cols,) + block, f32)],
         )(*inputs)
         received = [shift(blocks[s], "col", cols, s) for s in STEPS]
-        own = call(sum_kernel, shape, [VMEM] * cols, "own", 2)(blocks[0], *received)
-        other = shift(own, "ex", exs, 2)
+        own, pair = call(sum_kernel, [shape] * 2, [VMEM] * cols, "own", 2)(blocks[0], *received)
+        other = crossed(pair, exs, cols)
         line = jax.ShapeDtypeStruct((8, lanes), f32)
         local, remote = call(
             functools.partial(paired_kernel, m, k), [line, line], [VMEM] * 8, "score", 8
         )(own, other, *split(targets), *split(neighbours))
         lines = call(
             send_kernel, [line] * cols, [VMEM] * 2, "send", 2, [pltpu.VMEM((4, lanes), f32)]
-        )(local, shift(remote, "ex", exs, 2))
+        )(local, crossed(remote, exs, cols))
         parts = [lines[0]] + [shift(lines[s], "col", cols, s) for s in STEPS]
         return tuple(
             call(last, results, [VMEM] * (1 + len(parts)), "last", 2)(own, *parts)

time: 30.5 us -> 29.6 us (0.970)
  starting transfers between devices: 14.3 us -> 13.8 us
  waiting for transfers between devices: 7.77 us -> 7.32 us
    ppermute x12 -> x10, starting transfers between devices: 14.3 us -> 9.11 us  [shift(): lax.ppermute(x, axis, [(i, partner(i, step, count)) for i in range(count)])]
    ppermute x0 -> x2, starting transfers between devices: none -> 4.71 us  [crossed(): return lax.ppermute(x, ('ex', 'col'), pairs)]
    ppermute x12 -> x10, waiting for transfers between devices: 7.77 us -> 4.59 us  [shift(): lax.ppermute(x, axis, [(i, partner(i, step, count)) for i in range(count)])]
    ppermute x0 -> x2, waiting for transfers between devices: none -> 2.73 us  [crossed(): return lax.ppermute(x, ('ex', 'col'), pairs)]
  transfers between devices with their start and end apart: 12 -> 12, of which waited for: 7 -> 7; matrix products, arithmetic and copies ran while one was open for 0% -> 0% of each run, Pallas kernels for 19% -> 20%
where the time goes in v6:
time: 29.6 us; the launch traced here: 29.4 us
  starting transfers between devices  13.8 us (47%)
  waiting for transfers between devices  7.32 us (25%)
  Pallas kernels  6.89 us (23%)
  between operations  1.39 us (5%)
    ppermute x10, starting transfers between devices, shift(): lax.ppermute(x, axis, [(i, partner(i, step, count)) for i in range(count)])  9.11 us
    ppermute x2, starting transfers between devices, crossed(): return lax.ppermute(x, ('ex', 'col'), pairs)  4.71 us
    ppermute x10, waiting for transfers between devices, shift(): lax.ppermute(x, axis, [(i, partner(i, step, count)) for i in range(count)])  4.59 us
    pallas_call x1, Pallas kernels, on_device(): call(mix_kernel, [jax.ShapeDtypeStruct((layers * 2 * m, seq), f32), rows,...  3.03 us
    ppermute x2, waiting for transfers between devices, crossed(): return lax.ppermute(x, ('ex', 'col'), pairs)  2.73 us
    pallas_call x1, Pallas kernels, on_device(): call(sign_kernel, [signed, signed], [VMEM] * 3, 'sign', 8, [pltpu.VMEM((2...  1.88 us
    pallas_call x1, Pallas kernels, on_device(): call(last, results, [VMEM] * (1 + len(parts)), 'last', 2)(own, *parts)  0.66 us
  transfers between devices with their start and end apart: 12, of which 7 were waited for; matrix products, arithmetic and copies ran while one was open for 0% of the time, Pallas kernels for 20%

profile of v6, /device:TPU:0, one launch (start us, length us, event | category | flops | bytes accessed | tf_op | source)
XLA Modules:
  0.0 29.4 jit_solution(6662801524879123824)
XLA Ops:
  0.6 3.1 %collective-permute-start.7 = (f32[64,2048]{1,0:T(8,128)}, f32[64,2048]{1,0:T(8,128)S(1)}, u32[]{:S(2)}, u32[]{:S(2)}) collective-permute-start(f32[64,2048]{1,0:T(8,128)} %targets.1), channel_id=1, source_target_pairs={{0,4},{4,0},{8,12},{12,8},{1,5},{5,1},{9,13},{13,9},{2,6},{6,2},{1... | collective-permute-start | bytes 1572872 | tf_op jit(solution)/shard_map/ppermute | solution.py:45
  3.7 0.0 copy-start.1
  3.8 3.0 %mix.1 = (f32[16,256]{1,0:T(8,128)S(1)}, bf16[1,2,256,1280]{3,2,1,0:T(8,128)(2,1)S(1)}, bf16[1,2,256,1280]{3,2,1,0:T(8,128)(2,1)S(1)}) custom-call(s32[2,2,4,128]{3,2,1,0:T(4,128)} %bitcast.3, bf16[1,2,256,1280]{3,2,1,0:T(8,128)(2,1)} %hidden.1, bf16[1,2,256,1280]{3,2,1,0:T(8,128)(2,1)} %grad.1, bf16[2,128,1280]{2,1,0:T(8,128)(2,1)} %down.1, ...), custom_call_target="tpu_custom_call" | custom-call | flops 335544320 | bytes 4194304 | tf_op jit(solution)/shard_map/mix/pallas_call | solution.py:274
  6.8 0.7 %collective-permute-start = (f32[16,256]{1,0:T(8,128)S(1)}, f32[16,256]{1,0:T(8,128)S(1)}, u32[]{:S(2)}, u32[]{:S(2)}) collective-permute-start(f32[16,256]{1,0:T(8,128)S(1)} %get-tuple-element.25.own), channel_id=1, source_target_pairs={{0,3},{1,2},{2,1},{3,0},{4,7},{5,6},{6,5},{7,4},{8,11},{9,10},{10,... | collective-permute-start | bytes 49160 | tf_op jit(solution)/shard_map/ppermute | solution.py:45
  7.5 0.9 %collective-permute-start.1 = (f32[16,256]{1,0:T(8,128)S(1)}, f32[16,256]{1,0:T(8,128)S(1)}, u32[]{:S(2)}, u32[]{:S(2)}) collective-permute-start(f32[16,256]{1,0:T(8,128)S(1)} %get-tuple-element.25.own), channel_id=1, source_target_pairs={{0,2},{1,3},{2,0},{3,1},{4,6},{5,7},{6,4},{7,5},{8,10},{9,11},{10,... | collective-permute-start | bytes 49160 | tf_op jit(solution)/shard_map/ppermute | solution.py:45
  8.4 0.3 collective-permute-start.2
  8.7 0.0 copy-done.1
  8.7 1.9 %sign.1 = (bf16[2,2,256,512]{3,2,1,0:T(8,128)(2,1)S(1)}, bf16[2,2,256,512]{3,2,1,0:T(8,128)(2,1)S(1)}) custom-call(s32[2,2,32,1280]{3,2,1,0:T(8,128)S(1)} %copy-done.1, bf16[1,2,256,1280]{3,2,1,0:T(8,128)(2,1)S(1)} %get-tuple-element.26.hidden, bf16[1,2,256,1280]{3,2,1,0:T(8,128)(2,1)S(1)} %get-tuple-element.27.grad), custom_call_target="tpu_custom_call" | custom-call | flops 1342177280 | bytes 6291456 | tf_op jit(solution)/shard_map/sign/pallas_call | solution.py:291
  10.6 0.0 copy-start
  11.3 0.0 collective-permute-done.refs_0_
  11.3 0.1 collective-permute-done.1.refs_1_
  11.4 0.0 collective-permute-done.2.refs_2_
  11.4 0.4 %sketch.1 = (f32[2,16,128]{2,1,0:T(8,128)S(1)}, f32[2,16,128]{2,1,0:T(8,128)S(1)}, f32[2,16,128]{2,1,0:T(8,128)S(1)}, f32[2,16,128]{2,1,0:T(8,128)S(1)}) custom-call(s32[1,1]{1,0:T(1,128)} %bitcast.2.length, f32[16,256]{1,0:T(8,128)S(1)} %get-tuple-element.25.own, f32[16,256]{1,0:T(8,128)S(1)} %collective-permute-done.refs_0_, ...), custom_call_target="tpu_custom_call" | custom-call | tf_op jit(solution)/shard_map/sketch/pallas_call | solution.py:321
  11.9 0.2 collective-permute-start.3
  12.1 1.4 %collective-permute-start.4 = (f32[2,16,128]{2,1,0:T(8,128)S(1)}, f32[2,16,128]{2,1,0:T(8,128)S(1)}, u32[]{:S(2)}, u32[]{:S(2)}) collective-permute-start(f32[2,16,128]{2,1,0:T(8,128)S(1)} %get-tuple-element.32), channel_id=1, source_target_pairs={{0,2},{1,3},{2,0},{3,1},{4,6},{5,7},{6,4},{7,5},{8,10},{9,11},{10,... | collective-permute-start | bytes 49160 | tf_op jit(solution)/shard_map/ppermute | solution.py:45
  13.4 0.3 %collective-permute-start.5 = (f32[2,16,128]{2,1,0:T(8,128)S(1)}, f32[2,16,128]{2,1,0:T(8,128)S(1)}, u32[]{:S(2)}, u32[]{:S(2)}) collective-permute-start(f32[2,16,128]{2,1,0:T(8,128)S(1)} %get-tuple-element.33), channel_id=1, source_target_pairs={{0,3},{1,2},{2,1},{3,0},{4,7},{5,6},{6,5},{7,4},{8,11},{9,10},{10,... | collective-permute-start | bytes 49160 | tf_op jit(solution)/shard_map/ppermute | solution.py:45
  13.8 0.0 collective-permute-done.3.refs_1_
  13.8 2.0 %collective-permute-done.4.refs_2_ = f32[2,16,128]{2,1,0:T(8,128)S(1)} collective-permute-done((f32[2,16,128]{2,1,0:T(8,128)S(1)}, f32[2,16,128]{2,1,0:T(8,128)S(1)}, u32[]{:S(2)}, u32[]{:S(2)}) %collective-permute-start.4) | collective-permute-done | bytes 16416 | tf_op jit(solution)/shard_map/ppermute | solution.py:45
  15.8 0.8 %collective-permute-done.5.refs_3_ = f32[2,16,128]{2,1,0:T(8,128)S(1)} collective-permute-done((f32[2,16,128]{2,1,0:T(8,128)S(1)}, f32[2,16,128]{2,1,0:T(8,128)S(1)}, u32[]{:S(2)}, u32[]{:S(2)}) %collective-permute-start.5) | collective-permute-done | bytes 16416 | tf_op jit(solution)/shard_map/ppermute | solution.py:45
  16.6 2.3 %collective-permute-start.6 = (f32[16,128]{1,0:T(8,128)S(1)}, f32[16,128]{1,0:T(8,128)S(1)}, u32[]{:S(2)}, u32[]{:S(2)}) collective-permute-start(f32[16,128]{1,0:T(8,128)S(1)} %get-tuple-element.35), channel_id=1, source_target_pairs={{0,9},{1,8},{2,11},{3,10},{4,13},{5,12},{6,15},{7,14},{8,1},{9,0},... | collective-permute-start | bytes 24584 | tf_op jit(solution)/shard_map/ppermute | solution.py:20
  19.0 0.0 copy-done
  19.0 0.2 split.2
  19.2 0.0 collective-permute-done.7.targets
  19.2 0.2 split.3
  19.5 1.1 %collective-permute-done.6.other = f32[16,128]{1,0:T(8,128)S(1)} collective-permute-done((f32[16,128]{1,0:T(8,128)S(1)}, f32[16,128]{1,0:T(8,128)S(1)}, u32[]{:S(2)}, u32[]{:S(2)}) %collective-permute-start.6) | collective-permute-done | bytes 8224 | tf_op jit(solution)/shard_map/ppermute | solution.py:20
  20.6 0.4 %score.1 = (f32[8,128]{1,0:T(8,128)S(1)}, f32[8,128]{1,0:T(8,128)S(1)}) custom-call(f32[16,128]{1,0:T(8,128)S(1)} %get-tuple-element.34.own, f32[16,128]{1,0:T(8,128)S(1)} %collective-permute-done.6.other, bf16[64,2048]{1,0:T(8,128)(2,1)S(1)} %get-tuple-element.36.refs_0_, bf16[64,2048]{1,0:T(8,128)(2,1)S(1)} %get-tuple-element.37.refs_1_, ...), custom_call_target="tpu_custom_call" | custom-call | tf_op jit(solution)/shard_map/score/pallas_call | solution.py:333
  21.0 2.4 %collective-permute-start.8 = (f32[8,128]{1,0:T(8,128)S(1)}, f32[8,128]{1,0:T(8,128)S(1)}, u32[]{:S(2)}, u32[]{:S(2)}) collective-permute-start(f32[8,128]{1,0:T(8,128)S(1)} %get-tuple-element.43), channel_id=1, source_target_pairs={{0,9},{1,8},{2,11},{3,10},{4,13},{5,12},{6,15},{7,14},{8,1},{9,0},... | collective-permute-start | bytes 12296 | tf_op jit(solution)/shard_map/ppermute | solution.py:20
  23.3 1.6 %collective-permute-done.8.remote = f32[8,128]{1,0:T(8,128)S(1)} collective-permute-done((f32[8,128]{1,0:T(8,128)S(1)}, f32[8,128]{1,0:T(8,128)S(1)}, u32[]{:S(2)}, u32[]{:S(2)}) %collective-permute-start.8) | collective-permute-done | bytes 4128 | tf_op jit(solution)/shard_map/ppermute | solution.py:20
  24.9 0.8 %collective-permute-start.10 = (f32[8,128]{1,0:T(8,128)S(1)}, f32[8,128]{1,0:T(8,128)S(1)}, u32[]{:S(2)}, u32[]{:S(2)}) collective-permute-start(f32[8,128]{1,0:T(8,128)S(1)} %get-tuple-element.46), channel_id=1, source_target_pairs={{0,2},{1,3},{2,0},{3,1},{4,6},{5,7},{6,4},{7,5},{8,10},{9,11},{10,... | collective-permute-start | bytes 12296 | tf_op jit(solution)/shard_map/ppermute | solution.py:45
  25.7 0.7 %collective-permute-start.11 = (f32[8,128]{1,0:T(8,128)S(1)}, f32[8,128]{1,0:T(8,128)S(1)}, u32[]{:S(2)}, u32[]{:S(2)}) collective-permute-start(f32[8,128]{1,0:T(8,128)S(1)} %get-tuple-element.47), channel_id=1, source_target_pairs={{0,3},{1,2},{2,1},{3,0},{4,7},{5,6},{6,5},{7,4},{8,11},{9,10},{10,... | collective-permute-start | bytes 12296 | tf_op jit(solution)/shard_map/ppermute | solution.py:45
  26.4 0.6 %collective-permute-start.9 = (f32[8,128]{1,0:T(8,128)S(1)}, f32[8,128]{1,0:T(8,128)S(1)}, u32[]{:S(2)}, u32[]{:S(2)}) collective-permute-start(f32[8,128]{1,0:T(8,128)S(1)} %get-tuple-element.45), channel_id=1, source_target_pairs={{0,1},{1,0},{2,3},{3,2},{4,5},{5,4},{6,7},{7,6},{8,9},{9,8},{10,11... | collective-permute-start | bytes 12296 | tf_op jit(solution)/shard_map/ppermute | solution.py:45
  27.1 1.5 %collective-permute-done.10.refs_2_ = f32[8,128]{1,0:T(8,128)S(1)} collective-permute-done((f32[8,128]{1,0:T(8,128)S(1)}, f32[8,128]{1,0:T(8,128)S(1)}, u32[]{:S(2)}, u32[]{:S(2)}) %collective-permute-start.10) | collective-permute-done | bytes 4128 | tf_op jit(solution)/shard_map/ppermute | solution.py:45
  28.5 0.2 collective-permute-done.11.refs_3_
  28.8 0.0 collective-permute-done.9.refs_1_
  28.8 0.7 %last.1 = (f32[1,2048]{1,0:T(1,128)}, f32[1,64]{1,0:T(1,128)}) custom-call(f32[16,128]{1,0:T(8,128)S(1)} %get-tuple-element.34.own, f32[8,128]{1,0:T(8,128)S(1)} %get-tuple-element.44.refs_0_, f32[8,128]{1,0:T(8,128)S(1)} %collective-permute-done.9.refs_1_, f32[8,128]{1,0:T(8,128)S(1)} %collective-permute-done.10.refs_2_, ...), custom_call_target="tpu_custom_call" | custom-call | tf_op jit(solution)/shard_map/last/pallas_call | solution.py:341
  (2 shorter events, 0.0 us)
Async XLA Ops:
  0.6 18.6 %collective-permute-start.7 = (f32[64,2048]{1,0:T(8,128)}, f32[64,2048]{1,0:T(8,128)S(1)}, u32[]{:S(2)}, u32[]{:S(2)}) collective-permute-start(f32[64,2048]{1,0:T(8,128)} %targets.1), channel_id=1, source_target_pairs={{0,4},{4,0},{8,12},{12,8},{1,5},{5,1},{9,13},{13,9},{2,6},{6,2},{1... | collective-permute-start | bytes 1572872 | tf_op jit(solution)/shard_map/ppermute | solution.py:45
  3.7 5.0 %copy-start.1 = (s32[2,2,32,1280]{3,2,1,0:T(8,128)S(1)}, s32[2,2,32,1280]{3,2,1,0:T(8,128)}, u32[]{:S(2)}) copy-start(s32[2,2,32,1280]{3,2,1,0:T(8,128)} %words.1) | copy-start | bytes 1966084
  6.8 4.5 %collective-permute-start = (f32[16,256]{1,0:T(8,128)S(1)}, f32[16,256]{1,0:T(8,128)S(1)}, u32[]{:S(2)}, u32[]{:S(2)}) collective-permute-start(f32[16,256]{1,0:T(8,128)S(1)} %get-tuple-element.25.own), channel_id=1, source_target_pairs={{0,3},{1,2},{2,1},{3,0},{4,7},{5,6},{6,5},{7,4},{8,11},{9,10},{10,... | collective-permute-start | bytes 49160 | tf_op jit(solution)/shard_map/ppermute | solution.py:45
  7.5 3.9 %collective-permute-start.1 = (f32[16,256]{1,0:T(8,128)S(1)}, f32[16,256]{1,0:T(8,128)S(1)}, u32[]{:S(2)}, u32[]{:S(2)}) collective-permute-start(f32[16,256]{1,0:T(8,128)S(1)} %get-tuple-element.25.own), channel_id=1, source_target_pairs={{0,2},{1,3},{2,0},{3,1},{4,6},{5,7},{6,4},{7,5},{8,10},{9,11},{10,... | collective-permute-start | bytes 49160 | tf_op jit(solution)/shard_map/ppermute | solution.py:45
  8.4 3.0 %collective-permute-start.2 = (f32[16,256]{1,0:T(8,128)S(1)}, f32[16,256]{1,0:T(8,128)S(1)}, u32[]{:S(2)}, u32[]{:S(2)}) collective-permute-start(f32[16,256]{1,0:T(8,128)S(1)} %get-tuple-element.25.own), channel_id=1, source_target_pairs={{0,1},{1,0},{2,3},{3,2},{4,5},{5,4},{6,7},{7,6},{8,9},{9,8},{10,11... | collective-permute-start | bytes 49160 | tf_op jit(solution)/shard_map/ppermute | solution.py:45
  10.6 8.4 %copy-start = (f32[64,2048]{1,0:T(8,128)S(1)}, f32[64,2048]{1,0:T(8,128)}, u32[]{:S(2)}) copy-start(f32[64,2048]{1,0:T(8,128)} %targets.1) | copy-start | bytes 1572868
  11.9 1.9 %collective-permute-start.3 = (f32[2,16,128]{2,1,0:T(8,128)S(1)}, f32[2,16,128]{2,1,0:T(8,128)S(1)}, u32[]{:S(2)}, u32[]{:S(2)}) collective-permute-start(f32[2,16,128]{2,1,0:T(8,128)S(1)} %get-tuple-element.31), channel_id=1, source_target_pairs={{0,1},{1,0},{2,3},{3,2},{4,5},{5,4},{6,7},{7,6},{8,9},{9,8},{10,11... | collective-permute-start | bytes 49160 | tf_op jit(solution)/shard_map/ppermute | solution.py:45
  12.1 3.7 %collective-permute-start.4 = (f32[2,16,128]{2,1,0:T(8,128)S(1)}, f32[2,16,128]{2,1,0:T(8,128)S(1)}, u32[]{:S(2)}, u32[]{:S(2)}) collective-permute-start(f32[2,16,128]{2,1,0:T(8,128)S(1)} %get-tuple-element.32), channel_id=1, source_target_pairs={{0,2},{1,3},{2,0},{3,1},{4,6},{5,7},{6,4},{7,5},{8,10},{9,11},{10,... | collective-permute-start | bytes 49160 | tf_op jit(solution)/shard_map/ppermute | solution.py:45
  13.4 3.2 %collective-permute-start.5 = (f32[2,16,128]{2,1,0:T(8,128)S(1)}, f32[2,16,128]{2,1,0:T(8,128)S(1)}, u32[]{:S(2)}, u32[]{:S(2)}) collective-permute-start(f32[2,16,128]{2,1,0:T(8,128)S(1)} %get-tuple-element.33), channel_id=1, source_target_pairs={{0,3},{1,2},{2,1},{3,0},{4,7},{5,6},{6,5},{7,4},{8,11},{9,10},{10,... | collective-permute-start | bytes 49160 | tf_op jit(solution)/shard_map/ppermute | solution.py:45
  16.6 4.0 %collective-permute-start.6 = (f32[16,128]{1,0:T(8,128)S(1)}, f32[16,128]{1,0:T(8,128)S(1)}, u32[]{:S(2)}, u32[]{:S(2)}) collective-permute-start(f32[16,128]{1,0:T(8,128)S(1)} %get-tuple-element.35), channel_id=1, source_target_pairs={{0,9},{1,8},{2,11},{3,10},{4,13},{5,12},{6,15},{7,14},{8,1},{9,0},... | collective-permute-start | bytes 24584 | tf_op jit(solution)/shard_map/ppermute | solution.py:20
  21.0 4.0 %collective-permute-start.8 = (f32[8,128]{1,0:T(8,128)S(1)}, f32[8,128]{1,0:T(8,128)S(1)}, u32[]{:S(2)}, u32[]{:S(2)}) collective-permute-start(f32[8,128]{1,0:T(8,128)S(1)} %get-tuple-element.43), channel_id=1, source_target_pairs={{0,9},{1,8},{2,11},{3,10},{4,13},{5,12},{6,15},{7,14},{8,1},{9,0},... | collective-permute-start | bytes 12296 | tf_op jit(solution)/shard_map/ppermute | solution.py:20
  24.9 3.6 %collective-permute-start.10 = (f32[8,128]{1,0:T(8,128)S(1)}, f32[8,128]{1,0:T(8,128)S(1)}, u32[]{:S(2)}, u32[]{:S(2)}) collective-permute-start(f32[8,128]{1,0:T(8,128)S(1)} %get-tuple-element.46), channel_id=1, source_target_pairs={{0,2},{1,3},{2,0},{3,1},{4,6},{5,7},{6,4},{7,5},{8,10},{9,11},{10,... | collective-permute-start | bytes 12296 | tf_op jit(solution)/shard_map/ppermute | solution.py:45
  25.7 3.0 %collective-permute-start.11 = (f32[8,128]{1,0:T(8,128)S(1)}, f32[8,128]{1,0:T(8,128)S(1)}, u32[]{:S(2)}, u32[]{:S(2)}) collective-permute-start(f32[8,128]{1,0:T(8,128)S(1)} %get-tuple-element.47), channel_id=1, source_target_pairs={{0,3},{1,2},{2,1},{3,0},{4,7},{5,6},{6,5},{7,4},{8,11},{9,10},{10,... | collective-permute-start | bytes 12296 | tf_op jit(solution)/shard_map/ppermute | solution.py:45
  26.4 2.3 %collective-permute-start.9 = (f32[8,128]{1,0:T(8,128)S(1)}, f32[8,128]{1,0:T(8,128)S(1)}, u32[]{:S(2)}, u32[]{:S(2)}) collective-permute-start(f32[8,128]{1,0:T(8,128)S(1)} %get-tuple-element.45), channel_id=1, source_target_pairs={{0,1},{1,0},{2,3},{3,2},{4,5},{5,4},{6,7},{7,6},{8,9},{9,8},{10,11... | collective-permute-start | bytes 12296 | tf_op jit(solution)/shard_map/ppermute | solution.py:45

commit v7 on v6

--- a/solution.py
+++ b/solution.py
@@ -89,10 +89,13 @@
         out[w * WORD : (w + 1) * WORD, :] = signs.astype(f32).astype(bf16)
 
 
-def split_kernel(targets, high, low, squares):
-    t = targets[...]
-    high[...], low[...] = halves(t)
-    squares[...] = jnp.transpose(jnp.sum(t * t, axis=1, keepdims=True))
+def split_kernel(*refs):
+    *targets, table, squares = refs
+    t = jnp.concatenate([ref[...] for ref in targets], axis=0)
+    turned = jnp.transpose(t)
+    count = turned.shape[1]
+    table[:, :count], table[:, count:] = halves(turned)
+    squares[...] = jnp.sum(turned * turned, axis=0, keepdims=True)
 
 
 def sign_kernel(words, hidden, grad, high, low, signs):
@@ -158,14 +161,15 @@
     ]
 
 
-def score(total, m, k, target_high, target_low, squares, out):
+def score(total, m, k, table, squares, out):
     exs = total.shape[0]
     starts = column_starts(m, k, total.shape[1])
     order = sorted(range(len(starts)), key=lambda r: starts[r])
     rows = jnp.concatenate([total[:, r, :] for r in order], axis=1)
     pair = jnp.concatenate(halves(rows), axis=0)
-    both = contract_last(pair, target_high[...]) + contract_last(pair, target_low[...])
-    count = target_high.shape[0]
+    both = product(pair, table[...])
+    count = squares.shape[1]
+    both = both[:, :count] + both[:, count:]
     out[...] = jnp.zeros_like(out)
     out[0:exs, 0:count] = both[:exs] + both[exs:]
     out[0:exs, count : 2 * count] = jnp.broadcast_to(squares[...], (exs, count))
@@ -174,7 +178,7 @@
     )
 
 
-def gathered_kernel(exs, cols, m, k, received, target_high, target_low, squares, own, out):
+def gathered_kernel(exs, cols, m, k, received, table, squares, own, out):
     def collect(x):
         total = x[:, 0]
         for i in range(1, cols):
@@ -183,31 +187,33 @@
 
     x = received[...]
     score(
-        collect(x.reshape((exs, cols) + x.shape[1:])), m, k, target_high, target_low, squares, out
+        collect(x.reshape((exs, cols) + x.shape[1:])), m, k, table, squares, out
     )
     mine = received[pl.ds(lax.axis_index("ex") * cols, cols)]
     own[...] = collect(mine[None])[0]
 
 
-def paired_kernel(m, k, own, other, *refs):
-    *tables, local, remote = refs
+def paired_kernel(m, k, own, other, table, squares, local, remote):
     blocks = jnp.concatenate([own[...][None], other[...][None]], axis=0)
     starts = column_starts(m, k, blocks.shape[1])
     order = sorted(range(len(starts)), key=lambda r: starts[r])
     rows = jnp.concatenate([blocks[:, r, :] for r in order], axis=1)
     pair = jnp.concatenate(halves(rows), axis=0)
-    lines = []
-    for at in range(0, len(tables), 3):
-        high, low, squares = tables[at : at + 3]
-        both = contract_last(pair, high[...]) + contract_last(pair, low[...])
-        scores = both[:2] + both[2:]
-        lines.append(
-            jnp.concatenate([scores, jnp.broadcast_to(squares[...], scores.shape)], axis=1)
-        )
-    square = jnp.broadcast_to(jnp.sum(rows[:1] * rows[:1], axis=1, keepdims=True), lines[0][:1].shape)
-    pad = jnp.zeros((8 - len(lines), square.shape[1]), f32)
-    local[...] = jnp.concatenate([line[:1] for line in lines] + [square, pad[1:]], axis=0)
-    remote[...] = jnp.concatenate([line[1:] for line in lines] + [pad], axis=0)
+    both = product(pair, table[...])
+    both = both[:2] + both[2:]
+    total = squares.shape[1]
+    both = both[:, :total] + both[:, total:]
+    count = total // 2
+    q = squares[...]
+    for out, row in ((local, 0), (remote, 1)):
+        out[...] = jnp.zeros_like(out)
+        for u in range(2):
+            at = slice(u * count, (u + 1) * count)
+            out[u : u + 1, 0:count] = both[row : row + 1, at]
+            out[u : u + 1, count : 2 * count] = q[:, at]
+    local[2:3] = jnp.broadcast_to(
+        jnp.sum(rows[:1] * rows[:1], axis=1, keepdims=True), (1, local.shape[1])
+    )
 
 
 def send_kernel(local, remote, *refs):
@@ -298,15 +304,21 @@
         4 * layers * k * seq * width,
         6 * MIB,
     )(left_sign_words, hidden, grad)
-    target_half = jax.ShapeDtypeStruct(targets.shape, bf16)
-    split = call(
-        split_kernel,
-        [target_half, target_half, jax.ShapeDtypeStruct((1, count), f32)],
-        [VMEM],
-        "split",
-        4,
-        moved=MIB,
-    )
+
+    def split(*tables):
+        size = count * len(tables)
+        return call(
+            split_kernel,
+            [
+                jax.ShapeDtypeStruct((own_cols, 2 * size), bf16),
+                jax.ShapeDtypeStruct((1, size), f32),
+            ],
+            [VMEM] * len(tables),
+            "split",
+            8,
+            moved=MIB,
+        )(*tables)
+
     block = (own_cols // LANES, LANES)
     lanes = -(-2 * count // LANES) * LANES
     shape = jax.ShapeDtypeStruct(block, f32)
@@ -331,8 +343,8 @@
         other = crossed(pair, exs, cols)
         line = jax.ShapeDtypeStruct((8, lanes), f32)
         local, remote = call(
-            functools.partial(paired_kernel, m, k), [line, line], [VMEM] * 8, "score", 8
-        )(own, other, *split(targets), *split(neighbours))
+            functools.partial(paired_kernel, m, k), [line, line], [VMEM] * 4, "score", 8
+        )(own, other, *split(targets, neighbours))
         lines = call(
             send_kernel, [line] * cols, [VMEM] * 2, "send", 2, [pltpu.VMEM((4, lanes), f32)]
         )(local, crossed(remote, exs, cols))
@@ -349,7 +361,7 @@
     )(*inputs)
     received = lax.all_to_all(blocks, ("ex", "col"), 0, 0, tiled=True)
     own, packed = call(
-        functools.partial(gathered_kernel, exs, cols, m, k), [shape, packed], [VMEM] * 4, "score", 16
+        functools.partial(gathered_kernel, exs, cols, m, k), [shape, packed], [VMEM] * 3, "score", 16
     )(received, *split(targets))
     per = exs // cols
     rows = jnp.stack([packed[:exs], packed[exs:]], axis=1)

time: 29.6 us -> 29.5 us (level)
    pallas_call x3 -> x2, Pallas kernels: 0.86 us -> 0.65 us  [the longest x1 0.36 us: split(): call(split_kernel, [jax.ShapeDtypeStruct((own_cols, 2 * size), bf16), jax...]
  transfers between devices with their start and end apart: 12 -> 12, of which waited for: 7 -> 7; matrix products, arithmetic and copies ran while one was open for 0% -> 0% of each run, Pallas kernels for 20% -> 19%
where the time goes in v7:
time: 29.5 us; the launch traced here: 29.4 us
  starting transfers between devices  13.8 us (47%)
  waiting for transfers between devices  7.44 us (25%)
  Pallas kernels  6.68 us (23%)
  between operations  1.39 us (5%)
    ppermute x10, starting transfers between devices, shift(): lax.ppermute(x, axis, [(i, partner(i, step, count)) for i in range(count)])  9.11 us
    ppermute x2, starting transfers between devices, crossed(): return lax.ppermute(x, ('ex', 'col'), pairs)  4.73 us
    ppermute x10, waiting for transfers between devices, shift(): lax.ppermute(x, axis, [(i, partner(i, step, count)) for i in range(count)])  4.59 us
    pallas_call x1, Pallas kernels, on_device(): call(mix_kernel, [jax.ShapeDtypeStruct((layers * 2 * m, seq), f32), rows,...  3.03 us
    ppermute x2, waiting for transfers between devices, crossed(): return lax.ppermute(x, ('ex', 'col'), pairs)  2.85 us
    pallas_call x1, Pallas kernels, on_device(): call(sign_kernel, [signed, signed], [VMEM] * 3, 'sign', 8, [pltpu.VMEM((2...  1.88 us
    pallas_call x1, Pallas kernels, on_device(): call(last, results, [VMEM] * (1 + len(parts)), 'last', 2)(own, *parts)  0.66 us
  transfers between devices with their start and end apart: 12, of which 7 were waited for; matrix products, arithmetic and copies ran while one was open for 0% of the time, Pallas kernels for 19%

profile of v7, /device:TPU:0, one launch (start us, length us, event | category | flops | bytes accessed | tf_op | source)
XLA Modules:
  0.0 29.4 jit_solution(5218704924561347119)
XLA Ops:
  0.6 3.1 %collective-permute-start.7 = (f32[64,2048]{1,0:T(8,128)}, f32[64,2048]{1,0:T(8,128)S(1)}, u32[]{:S(2)}, u32[]{:S(2)}) collective-permute-start(f32[64,2048]{1,0:T(8,128)} %refs_0_.1), channel_id=1, source_target_pairs={{0,4},{4,0},{8,12},{12,8},{1,5},{5,1},{9,13},{13,9},{2,6},{6,2},{1... | collective-permute-start | bytes 1572872 | tf_op jit(solution)/shard_map/ppermute | solution.py:45
  3.7 0.0 copy-start.1
  3.8 3.0 %mix.1 = (f32[16,256]{1,0:T(8,128)S(1)}, bf16[1,2,256,1280]{3,2,1,0:T(8,128)(2,1)S(1)}, bf16[1,2,256,1280]{3,2,1,0:T(8,128)(2,1)S(1)}) custom-call(s32[2,2,4,128]{3,2,1,0:T(4,128)} %bitcast.3, bf16[1,2,256,1280]{3,2,1,0:T(8,128)(2,1)} %hidden.1, bf16[1,2,256,1280]{3,2,1,0:T(8,128)(2,1)} %grad.1, bf16[2,128,1280]{2,1,0:T(8,128)(2,1)} %down.1, ...), custom_call_target="tpu_custom_call" | custom-call | flops 335544320 | bytes 4194304 | tf_op jit(solution)/shard_map/mix/pallas_call | solution.py:280
  6.8 0.7 %collective-permute-start = (f32[16,256]{1,0:T(8,128)S(1)}, f32[16,256]{1,0:T(8,128)S(1)}, u32[]{:S(2)}, u32[]{:S(2)}) collective-permute-start(f32[16,256]{1,0:T(8,128)S(1)} %get-tuple-element.21.own), channel_id=1, source_target_pairs={{0,3},{1,2},{2,1},{3,0},{4,7},{5,6},{6,5},{7,4},{8,11},{9,10},{10,... | collective-permute-start | bytes 49160 | tf_op jit(solution)/shard_map/ppermute | solution.py:45
  7.5 0.9 %collective-permute-start.1 = (f32[16,256]{1,0:T(8,128)S(1)}, f32[16,256]{1,0:T(8,128)S(1)}, u32[]{:S(2)}, u32[]{:S(2)}) collective-permute-start(f32[16,256]{1,0:T(8,128)S(1)} %get-tuple-element.21.own), channel_id=1, source_target_pairs={{0,2},{1,3},{2,0},{3,1},{4,6},{5,7},{6,4},{7,5},{8,10},{9,11},{10,... | collective-permute-start | bytes 49160 | tf_op jit(solution)/shard_map/ppermute | solution.py:45
  8.4 0.3 collective-permute-start.2
  8.7 0.0 copy-done.1
  8.7 1.9 %sign.1 = (bf16[2,2,256,512]{3,2,1,0:T(8,128)(2,1)S(1)}, bf16[2,2,256,512]{3,2,1,0:T(8,128)(2,1)S(1)}) custom-call(s32[2,2,32,1280]{3,2,1,0:T(8,128)S(1)} %copy-done.1, bf16[1,2,256,1280]{3,2,1,0:T(8,128)(2,1)S(1)} %get-tuple-element.22.hidden, bf16[1,2,256,1280]{3,2,1,0:T(8,128)(2,1)S(1)} %get-tuple-element.23.grad), custom_call_target="tpu_custom_call" | custom-call | flops 1342177280 | bytes 6291456 | tf_op jit(solution)/shard_map/sign/pallas_call | solution.py:297
  10.6 0.0 copy-start
  11.3 0.0 collective-permute-done.refs_0_
  11.3 0.1 collective-permute-done.1.refs_1_
  11.4 0.0 collective-permute-done.2.refs_2_
  11.4 0.4 %sketch.1 = (f32[2,16,128]{2,1,0:T(8,128)S(1)}, f32[2,16,128]{2,1,0:T(8,128)S(1)}, f32[2,16,128]{2,1,0:T(8,128)S(1)}, f32[2,16,128]{2,1,0:T(8,128)S(1)}) custom-call(s32[1,1]{1,0:T(1,128)} %bitcast.2.length, f32[16,256]{1,0:T(8,128)S(1)} %get-tuple-element.21.own, f32[16,256]{1,0:T(8,128)S(1)} %collective-permute-done.refs_0_, ...), custom_call_target="tpu_custom_call" | custom-call | tf_op jit(solution)/shard_map/sketch/pallas_call | solution.py:333
  11.9 0.2 collective-permute-start.3
  12.1 1.4 %collective-permute-start.4 = (f32[2,16,128]{2,1,0:T(8,128)S(1)}, f32[2,16,128]{2,1,0:T(8,128)S(1)}, u32[]{:S(2)}, u32[]{:S(2)}) collective-permute-start(f32[2,16,128]{2,1,0:T(8,128)S(1)} %get-tuple-element.28), channel_id=1, source_target_pairs={{0,2},{1,3},{2,0},{3,1},{4,6},{5,7},{6,4},{7,5},{8,10},{9,11},{10,... | collective-permute-start | bytes 49160 | tf_op jit(solution)/shard_map/ppermute | solution.py:45
  13.4 0.3 %collective-permute-start.5 = (f32[2,16,128]{2,1,0:T(8,128)S(1)}, f32[2,16,128]{2,1,0:T(8,128)S(1)}, u32[]{:S(2)}, u32[]{:S(2)}) collective-permute-start(f32[2,16,128]{2,1,0:T(8,128)S(1)} %get-tuple-element.29), channel_id=1, source_target_pairs={{0,3},{1,2},{2,1},{3,0},{4,7},{5,6},{6,5},{7,4},{8,11},{9,10},{10,... | collective-permute-start | bytes 49160 | tf_op jit(solution)/shard_map/ppermute | solution.py:45
  13.8 0.0 collective-permute-done.3.refs_1_
  13.8 2.0 %collective-permute-done.4.refs_2_ = f32[2,16,128]{2,1,0:T(8,128)S(1)} collective-permute-done((f32[2,16,128]{2,1,0:T(8,128)S(1)}, f32[2,16,128]{2,1,0:T(8,128)S(1)}, u32[]{:S(2)}, u32[]{:S(2)}) %collective-permute-start.4) | collective-permute-done | bytes 16416 | tf_op jit(solution)/shard_map/ppermute | solution.py:45
  15.8 0.8 %collective-permute-done.5.refs_3_ = f32[2,16,128]{2,1,0:T(8,128)S(1)} collective-permute-done((f32[2,16,128]{2,1,0:T(8,128)S(1)}, f32[2,16,128]{2,1,0:T(8,128)S(1)}, u32[]{:S(2)}, u32[]{:S(2)}) %collective-permute-start.5) | collective-permute-done | bytes 16416 | tf_op jit(solution)/shard_map/ppermute | solution.py:45
  16.6 2.3 %collective-permute-start.6 = (f32[16,128]{1,0:T(8,128)S(1)}, f32[16,128]{1,0:T(8,128)S(1)}, u32[]{:S(2)}, u32[]{:S(2)}) collective-permute-start(f32[16,128]{1,0:T(8,128)S(1)} %get-tuple-element.31), channel_id=1, source_target_pairs={{0,9},{1,8},{2,11},{3,10},{4,13},{5,12},{6,15},{7,14},{8,1},{9,0},... | collective-permute-start | bytes 24584 | tf_op jit(solution)/shard_map/ppermute | solution.py:20
  19.0 0.0 collective-permute-done.7.refs_1_
  19.0 0.0 copy-done
  19.0 0.4 %split.1 = (bf16[2048,256]{1,0:T(8,128)(2,1)S(1)}, f32[1,128]{1,0:T(1,128)S(1)}) custom-call(f32[64,2048]{1,0:T(8,128)S(1)} %copy-done, f32[64,2048]{1,0:T(8,128)S(1)} %collective-permute-done.7.refs_1_), custom_call_target="tpu_custom_call" | custom-call | bytes 1048576 | tf_op jit(solution)/shard_map/split/pallas_call | solution.py:310
  19.3 1.3 %collective-permute-done.6.other = f32[16,128]{1,0:T(8,128)S(1)} collective-permute-done((f32[16,128]{1,0:T(8,128)S(1)}, f32[16,128]{1,0:T(8,128)S(1)}, u32[]{:S(2)}, u32[]{:S(2)}) %collective-permute-start.6) | collective-permute-done | bytes 8224 | tf_op jit(solution)/shard_map/ppermute | solution.py:20
  20.6 0.3 score.1
  20.9 2.4 %collective-permute-start.8 = (f32[8,128]{1,0:T(8,128)S(1)}, f32[8,128]{1,0:T(8,128)S(1)}, u32[]{:S(2)}, u32[]{:S(2)}) collective-permute-start(f32[8,128]{1,0:T(8,128)S(1)} %get-tuple-element.35), channel_id=1, source_target_pairs={{0,9},{1,8},{2,11},{3,10},{4,13},{5,12},{6,15},{7,14},{8,1},{9,0},... | collective-permute-start | bytes 12296 | tf_op jit(solution)/shard_map/ppermute | solution.py:20
  23.3 1.6 %collective-permute-done.8.remote = f32[8,128]{1,0:T(8,128)S(1)} collective-permute-done((f32[8,128]{1,0:T(8,128)S(1)}, f32[8,128]{1,0:T(8,128)S(1)}, u32[]{:S(2)}, u32[]{:S(2)}) %collective-permute-start.8) | collective-permute-done | bytes 4128 | tf_op jit(solution)/shard_map/ppermute | solution.py:20
  24.9 0.8 %collective-permute-start.10 = (f32[8,128]{1,0:T(8,128)S(1)}, f32[8,128]{1,0:T(8,128)S(1)}, u32[]{:S(2)}, u32[]{:S(2)}) collective-permute-start(f32[8,128]{1,0:T(8,128)S(1)} %get-tuple-element.38), channel_id=1, source_target_pairs={{0,2},{1,3},{2,0},{3,1},{4,6},{5,7},{6,4},{7,5},{8,10},{9,11},{10,... | collective-permute-start | bytes 12296 | tf_op jit(solution)/shard_map/ppermute | solution.py:45
  25.7 0.7 %collective-permute-start.11 = (f32[8,128]{1,0:T(8,128)S(1)}, f32[8,128]{1,0:T(8,128)S(1)}, u32[]{:S(2)}, u32[]{:S(2)}) collective-permute-start(f32[8,128]{1,0:T(8,128)S(1)} %get-tuple-element.39), channel_id=1, source_target_pairs={{0,3},{1,2},{2,1},{3,0},{4,7},{5,6},{6,5},{7,4},{8,11},{9,10},{10,... | collective-permute-start | bytes 12296 | tf_op jit(solution)/shard_map/ppermute | solution.py:45
  26.4 0.6 %collective-permute-start.9 = (f32[8,128]{1,0:T(8,128)S(1)}, f32[8,128]{1,0:T(8,128)S(1)}, u32[]{:S(2)}, u32[]{:S(2)}) collective-permute-start(f32[8,128]{1,0:T(8,128)S(1)} %get-tuple-element.37), channel_id=1, source_target_pairs={{0,1},{1,0},{2,3},{3,2},{4,5},{5,4},{6,7},{7,6},{8,9},{9,8},{10,11... | collective-permute-start | bytes 12296 | tf_op jit(solution)/shard_map/ppermute | solution.py:45
  27.0 1.5 %collective-permute-done.10.refs_2_ = f32[8,128]{1,0:T(8,128)S(1)} collective-permute-done((f32[8,128]{1,0:T(8,128)S(1)}, f32[8,128]{1,0:T(8,128)S(1)}, u32[]{:S(2)}, u32[]{:S(2)}) %collective-permute-start.10) | collective-permute-done | bytes 4128 | tf_op jit(solution)/shard_map/ppermute | solution.py:45
  28.5 0.2 collective-permute-done.11.refs_3_
  28.7 0.0 collective-permute-done.9.refs_1_
  28.7 0.7 %last.1 = (f32[1,2048]{1,0:T(1,128)}, f32[1,64]{1,0:T(1,128)}) custom-call(f32[16,128]{1,0:T(8,128)S(1)} %get-tuple-element.30.own, f32[8,128]{1,0:T(8,128)S(1)} %get-tuple-element.36.refs_0_, f32[8,128]{1,0:T(8,128)S(1)} %collective-permute-done.9.refs_1_, f32[8,128]{1,0:T(8,128)S(1)} %collective-permute-done.10.refs_2_, ...), custom_call_target="tpu_custom_call" | custom-call | tf_op jit(solution)/shard_map/last/pallas_call | solution.py:353
  (2 shorter events, 0.0 us)
Async XLA Ops:
  0.6 18.3 %collective-permute-start.7 = (f32[64,2048]{1,0:T(8,128)}, f32[64,2048]{1,0:T(8,128)S(1)}, u32[]{:S(2)}, u32[]{:S(2)}) collective-permute-start(f32[64,2048]{1,0:T(8,128)} %refs_0_.1), channel_id=1, source_target_pairs={{0,4},{4,0},{8,12},{12,8},{1,5},{5,1},{9,13},{13,9},{2,6},{6,2},{1... | collective-permute-start | bytes 1572872 | tf_op jit(solution)/shard_map/ppermute | solution.py:45
  3.7 5.0 %copy-start.1 = (s32[2,2,32,1280]{3,2,1,0:T(8,128)S(1)}, s32[2,2,32,1280]{3,2,1,0:T(8,128)}, u32[]{:S(2)}) copy-start(s32[2,2,32,1280]{3,2,1,0:T(8,128)} %words.1) | copy-start | bytes 1966084
  6.8 4.5 %collective-permute-start = (f32[16,256]{1,0:T(8,128)S(1)}, f32[16,256]{1,0:T(8,128)S(1)}, u32[]{:S(2)}, u32[]{:S(2)}) collective-permute-start(f32[16,256]{1,0:T(8,128)S(1)} %get-tuple-element.21.own), channel_id=1, source_target_pairs={{0,3},{1,2},{2,1},{3,0},{4,7},{5,6},{6,5},{7,4},{8,11},{9,10},{10,... | collective-permute-start | bytes 49160 | tf_op jit(solution)/shard_map/ppermute | solution.py:45
  7.5 3.9 %collective-permute-start.1 = (f32[16,256]{1,0:T(8,128)S(1)}, f32[16,256]{1,0:T(8,128)S(1)}, u32[]{:S(2)}, u32[]{:S(2)}) collective-permute-start(f32[16,256]{1,0:T(8,128)S(1)} %get-tuple-element.21.own), channel_id=1, source_target_pairs={{0,2},{1,3},{2,0},{3,1},{4,6},{5,7},{6,4},{7,5},{8,10},{9,11},{10,... | collective-permute-start | bytes 49160 | tf_op jit(solution)/shard_map/ppermute | solution.py:45
  8.4 3.0 %collective-permute-start.2 = (f32[16,256]{1,0:T(8,128)S(1)}, f32[16,256]{1,0:T(8,128)S(1)}, u32[]{:S(2)}, u32[]{:S(2)}) collective-permute-start(f32[16,256]{1,0:T(8,128)S(1)} %get-tuple-element.21.own), channel_id=1, source_target_pairs={{0,1},{1,0},{2,3},{3,2},{4,5},{5,4},{6,7},{7,6},{8,9},{9,8},{10,11... | collective-permute-start | bytes 49160 | tf_op jit(solution)/shard_map/ppermute | solution.py:45
  10.6 8.4 %copy-start = (f32[64,2048]{1,0:T(8,128)S(1)}, f32[64,2048]{1,0:T(8,128)}, u32[]{:S(2)}) copy-start(f32[64,2048]{1,0:T(8,128)} %refs_0_.1) | copy-start | bytes 1572868
  11.9 1.9 %collective-permute-start.3 = (f32[2,16,128]{2,1,0:T(8,128)S(1)}, f32[2,16,128]{2,1,0:T(8,128)S(1)}, u32[]{:S(2)}, u32[]{:S(2)}) collective-permute-start(f32[2,16,128]{2,1,0:T(8,128)S(1)} %get-tuple-element.27), channel_id=1, source_target_pairs={{0,1},{1,0},{2,3},{3,2},{4,5},{5,4},{6,7},{7,6},{8,9},{9,8},{10,11... | collective-permute-start | bytes 49160 | tf_op jit(solution)/shard_map/ppermute | solution.py:45
  12.1 3.7 %collective-permute-start.4 = (f32[2,16,128]{2,1,0:T(8,128)S(1)}, f32[2,16,128]{2,1,0:T(8,128)S(1)}, u32[]{:S(2)}, u32[]{:S(2)}) collective-permute-start(f32[2,16,128]{2,1,0:T(8,128)S(1)} %get-tuple-element.28), channel_id=1, source_target_pairs={{0,2},{1,3},{2,0},{3,1},{4,6},{5,7},{6,4},{7,5},{8,10},{9,11},{10,... | collective-permute-start | bytes 49160 | tf_op jit(solution)/shard_map/ppermute | solution.py:45
  13.4 3.2 %collective-permute-start.5 = (f32[2,16,128]{2,1,0:T(8,128)S(1)}, f32[2,16,128]{2,1,0:T(8,128)S(1)}, u32[]{:S(2)}, u32[]{:S(2)}) collective-permute-start(f32[2,16,128]{2,1,0:T(8,128)S(1)} %get-tuple-element.29), channel_id=1, source_target_pairs={{0,3},{1,2},{2,1},{3,0},{4,7},{5,6},{6,5},{7,4},{8,11},{9,10},{10,... | collective-permute-start | bytes 49160 | tf_op jit(solution)/shard_map/ppermute | solution.py:45
  16.6 4.0 %collective-permute-start.6 = (f32[16,128]{1,0:T(8,128)S(1)}, f32[16,128]{1,0:T(8,128)S(1)}, u32[]{:S(2)}, u32[]{:S(2)}) collective-permute-start(f32[16,128]{1,0:T(8,128)S(1)} %get-tuple-element.31), channel_id=1, source_target_pairs={{0,9},{1,8},{2,11},{3,10},{4,13},{5,12},{6,15},{7,14},{8,1},{9,0},... | collective-permute-start | bytes 24584 | tf_op jit(solution)/shard_map/ppermute | solution.py:20
  20.9 4.0 %collective-permute-start.8 = (f32[8,128]{1,0:T(8,128)S(1)}, f32[8,128]{1,0:T(8,128)S(1)}, u32[]{:S(2)}, u32[]{:S(2)}) collective-permute-start(f32[8,128]{1,0:T(8,128)S(1)} %get-tuple-element.35), channel_id=1, source_target_pairs={{0,9},{1,8},{2,11},{3,10},{4,13},{5,12},{6,15},{7,14},{8,1},{9,0},... | collective-permute-start | bytes 12296 | tf_op jit(solution)/shard_map/ppermute | solution.py:20
  24.9 3.6 %collective-permute-start.10 = (f32[8,128]{1,0:T(8,128)S(1)}, f32[8,128]{1,0:T(8,128)S(1)}, u32[]{:S(2)}, u32[]{:S(2)}) collective-permute-start(f32[8,128]{1,0:T(8,128)S(1)} %get-tuple-element.38), channel_id=1, source_target_pairs={{0,2},{1,3},{2,0},{3,1},{4,6},{5,7},{6,4},{7,5},{8,10},{9,11},{10,... | collective-permute-start | bytes 12296 | tf_op jit(solution)/shard_map/ppermute | solution.py:45
  25.7 3.0 %collective-permute-start.11 = (f32[8,128]{1,0:T(8,128)S(1)}, f32[8,128]{1,0:T(8,128)S(1)}, u32[]{:S(2)}, u32[]{:S(2)}) collective-permute-start(f32[8,128]{1,0:T(8,128)S(1)} %get-tuple-element.39), channel_id=1, source_target_pairs={{0,3},{1,2},{2,1},{3,0},{4,7},{5,6},{6,5},{7,4},{8,11},{9,10},{10,... | collective-permute-start | bytes 12296 | tf_op jit(solution)/shard_map/ppermute | solution.py:45
  26.4 2.3 %collective-permute-start.9 = (f32[8,128]{1,0:T(8,128)S(1)}, f32[8,128]{1,0:T(8,128)S(1)}, u32[]{:S(2)}, u32[]{:S(2)}) collective-permute-start(f32[8,128]{1,0:T(8,128)S(1)} %get-tuple-element.37), channel_id=1, source_target_pairs={{0,1},{1,0},{2,3},{3,2},{4,5},{5,4},{6,7},{7,6},{8,9},{9,8},{10,11... | collective-permute-start | bytes 12296 | tf_op jit(solution)/shard_map/ppermute | solution.py:45

commit v8 on v7

--- a/solution.py
+++ b/solution.py
@@ -137,14 +137,18 @@
 
 
 def pair_kernel(cols, length, own, *refs):
-    others, (high, low), outs, table = refs[: cols - 1], refs[cols - 1 : cols + 1], refs[cols + 1 : -1], refs[-1]
-    for i, block in enumerate(sketch_blocks(cols, length, own, others, high, low)):
-        table[i] = block
+    others, (high, low), outs = refs[: cols - 1], refs[cols - 1 : cols + 1], refs[cols + 1 :]
+    blocks = sketch_blocks(cols, length, own, others, high, low)
     me = lax.axis_index("col")
+
+    def pick(at):
+        low_pair = [jnp.where(at & 1 == 0, blocks[i], blocks[i + 1]) for i in (0, 2)]
+        return jnp.where(at & 2 == 0, *low_pair)
+
     for step, out in enumerate(outs):
         to = partner(me, step, cols)
-        out[0] = table[to]
-        out[1] = table[to ^ 1]
+        out[0] = pick(to)
+        out[1] = pick(to ^ 1)
 
 
 def sum_kernel(*refs):
@@ -336,9 +340,8 @@
             [VMEM] * len(inputs),
             "sketch",
             8,
-            [pltpu.VMEM((cols,) + block, f32)],
         )(*inputs)
-        received = [shift(blocks[s], "col", cols, s) for s in STEPS]
+        received = [shift(blocks[s], "col", cols, s) for s in (2, 3, 1)]
         own, pair = call(sum_kernel, [shape] * 2, [VMEM] * cols, "own", 2)(blocks[0], *received)
         other = crossed(pair, exs, cols)
         line = jax.ShapeDtypeStruct((8, lanes), f32)

time: 29.5 us -> 29.5 us (level)
    ppermute x10, waiting for transfers between devices: 4.59 us -> 4.19 us  [shift(): lax.ppermute(x, axis, [(i, partner(i, step, count)) for i in range(count)])]
  transfers between devices with their start and end apart: 12 -> 12, of which waited for: 7 -> 7; matrix products, arithmetic and copies ran while one was open for 0% -> 0% of each run, Pallas kernels for 19% -> 20%
where the time goes in v8:
time: 29.5 us; the launch traced here: 29.3 us
  starting transfers between devices  14 us (47%)
  waiting for transfers between devices  7.21 us (24%)
  Pallas kernels  6.68 us (23%)
  between operations  1.39 us (5%)
    ppermute x10, starting transfers between devices, shift(): lax.ppermute(x, axis, [(i, partner(i, step, count)) for i in range(count)])  9.39 us
    ppermute x2, starting transfers between devices, crossed(): return lax.ppermute(x, ('ex', 'col'), pairs)  4.62 us
    ppermute x10, waiting for transfers between devices, shift(): lax.ppermute(x, axis, [(i, partner(i, step, count)) for i in range(count)])  4.19 us
    pallas_call x1, Pallas kernels, on_device(): call(mix_kernel, [jax.ShapeDtypeStruct((layers * 2 * m, seq), f32), rows,...  3.03 us
    ppermute x2, waiting for transfers between devices, crossed(): return lax.ppermute(x, ('ex', 'col'), pairs)  3.02 us
    pallas_call x1, Pallas kernels, on_device(): call(sign_kernel, [signed, signed], [VMEM] * 3, 'sign', 8, [pltpu.VMEM((2...  1.88 us
    pallas_call x1, Pallas kernels, on_device(): call(last, results, [VMEM] * (1 + len(parts)), 'last', 2)(own, *parts)  0.66 us
  transfers between devices with their start and end apart: 12, of which 7 were waited for; matrix products, arithmetic and copies ran while one was open for 0% of the time, Pallas kernels for 20%

profile of v8, /device:TPU:0, one launch (start us, length us, event | category | flops | bytes accessed | tf_op | source)
XLA Modules:
  0.0 29.3 jit_solution(7795861125387975838)
XLA Ops:
  0.6 3.1 %collective-permute-start.7 = (f32[64,2048]{1,0:T(8,128)}, f32[64,2048]{1,0:T(8,128)S(1)}, u32[]{:S(2)}, u32[]{:S(2)}) collective-permute-start(f32[64,2048]{1,0:T(8,128)} %refs_0_.1), channel_id=1, source_target_pairs={{0,4},{4,0},{8,12},{12,8},{1,5},{5,1},{9,13},{13,9},{2,6},{6,2},{1... | collective-permute-start | bytes 1572872 | tf_op jit(solution)/shard_map/ppermute | solution.py:45
  3.7 0.0 copy-start.1
  3.8 3.0 %mix.1 = (f32[16,256]{1,0:T(8,128)S(1)}, bf16[1,2,256,1280]{3,2,1,0:T(8,128)(2,1)S(1)}, bf16[1,2,256,1280]{3,2,1,0:T(8,128)(2,1)S(1)}) custom-call(s32[2,2,4,128]{3,2,1,0:T(4,128)} %bitcast.3, bf16[1,2,256,1280]{3,2,1,0:T(8,128)(2,1)} %hidden.1, bf16[1,2,256,1280]{3,2,1,0:T(8,128)(2,1)} %grad.1, bf16[2,128,1280]{2,1,0:T(8,128)(2,1)} %down.1, ...), custom_call_target="tpu_custom_call" | custom-call | flops 335544320 | bytes 4194304 | tf_op jit(solution)/shard_map/mix/pallas_call | solution.py:284
  6.8 0.7 %collective-permute-start = (f32[16,256]{1,0:T(8,128)S(1)}, f32[16,256]{1,0:T(8,128)S(1)}, u32[]{:S(2)}, u32[]{:S(2)}) collective-permute-start(f32[16,256]{1,0:T(8,128)S(1)} %get-tuple-element.21.own), channel_id=1, source_target_pairs={{0,3},{1,2},{2,1},{3,0},{4,7},{5,6},{6,5},{7,4},{8,11},{9,10},{10,... | collective-permute-start | bytes 49160 | tf_op jit(solution)/shard_map/ppermute | solution.py:45
  7.5 0.9 %collective-permute-start.1 = (f32[16,256]{1,0:T(8,128)S(1)}, f32[16,256]{1,0:T(8,128)S(1)}, u32[]{:S(2)}, u32[]{:S(2)}) collective-permute-start(f32[16,256]{1,0:T(8,128)S(1)} %get-tuple-element.21.own), channel_id=1, source_target_pairs={{0,2},{1,3},{2,0},{3,1},{4,6},{5,7},{6,4},{7,5},{8,10},{9,11},{10,... | collective-permute-start | bytes 49160 | tf_op jit(solution)/shard_map/ppermute | solution.py:45
  8.4 0.3 collective-permute-start.2
  8.7 0.0 copy-done.1
  8.7 1.9 %sign.1 = (bf16[2,2,256,512]{3,2,1,0:T(8,128)(2,1)S(1)}, bf16[2,2,256,512]{3,2,1,0:T(8,128)(2,1)S(1)}) custom-call(s32[2,2,32,1280]{3,2,1,0:T(8,128)S(1)} %copy-done.1, bf16[1,2,256,1280]{3,2,1,0:T(8,128)(2,1)S(1)} %get-tuple-element.22.hidden, bf16[1,2,256,1280]{3,2,1,0:T(8,128)(2,1)S(1)} %get-tuple-element.23.grad), custom_call_target="tpu_custom_call" | custom-call | flops 1342177280 | bytes 6291456 | tf_op jit(solution)/shard_map/sign/pallas_call | solution.py:301
  10.6 0.0 copy-start
  11.3 0.0 collective-permute-done.refs_0_
  11.3 0.1 collective-permute-done.1.refs_1_
  11.4 0.0 collective-permute-done.2.refs_2_
  11.4 0.4 %sketch.1 = (f32[2,16,128]{2,1,0:T(8,128)S(1)}, f32[2,16,128]{2,1,0:T(8,128)S(1)}, f32[2,16,128]{2,1,0:T(8,128)S(1)}, f32[2,16,128]{2,1,0:T(8,128)S(1)}) custom-call(s32[1,1]{1,0:T(1,128)} %bitcast.2.length, f32[16,256]{1,0:T(8,128)S(1)} %get-tuple-element.21.own, f32[16,256]{1,0:T(8,128)S(1)} %collective-permute-done.refs_0_, ...), custom_call_target="tpu_custom_call" | custom-call | tf_op jit(solution)/shard_map/sketch/pallas_call | solution.py:337
  11.9 1.5 %collective-permute-start.3 = (f32[2,16,128]{2,1,0:T(8,128)S(1)}, f32[2,16,128]{2,1,0:T(8,128)S(1)}, u32[]{:S(2)}, u32[]{:S(2)}) collective-permute-start(f32[2,16,128]{2,1,0:T(8,128)S(1)} %get-tuple-element.27), channel_id=1, source_target_pairs={{0,2},{1,3},{2,0},{3,1},{4,6},{5,7},{6,4},{7,5},{8,10},{9,11},{10,... | collective-permute-start | bytes 49160 | tf_op jit(solution)/shard_map/ppermute | solution.py:45
  13.4 0.1 collective-permute-start.4
  13.4 0.6 %collective-permute-start.5 = (f32[2,16,128]{2,1,0:T(8,128)S(1)}, f32[2,16,128]{2,1,0:T(8,128)S(1)}, u32[]{:S(2)}, u32[]{:S(2)}) collective-permute-start(f32[2,16,128]{2,1,0:T(8,128)S(1)} %get-tuple-element.29), channel_id=1, source_target_pairs={{0,1},{1,0},{2,3},{3,2},{4,5},{5,4},{6,7},{7,6},{8,9},{9,8},{10,11... | collective-permute-start | bytes 49160 | tf_op jit(solution)/shard_map/ppermute | solution.py:45
  14.1 1.6 %collective-permute-done.3.refs_1_ = f32[2,16,128]{2,1,0:T(8,128)S(1)} collective-permute-done((f32[2,16,128]{2,1,0:T(8,128)S(1)}, f32[2,16,128]{2,1,0:T(8,128)S(1)}, u32[]{:S(2)}, u32[]{:S(2)}) %collective-permute-start.3) | collective-permute-done | bytes 16416 | tf_op jit(solution)/shard_map/ppermute | solution.py:45
  15.7 0.9 %collective-permute-done.4.refs_2_ = f32[2,16,128]{2,1,0:T(8,128)S(1)} collective-permute-done((f32[2,16,128]{2,1,0:T(8,128)S(1)}, f32[2,16,128]{2,1,0:T(8,128)S(1)}, u32[]{:S(2)}, u32[]{:S(2)}) %collective-permute-start.4) | collective-permute-done | bytes 16416 | tf_op jit(solution)/shard_map/ppermute | solution.py:45
  16.6 0.0 collective-permute-done.5.refs_3_
  16.6 2.3 %collective-permute-start.6 = (f32[16,128]{1,0:T(8,128)S(1)}, f32[16,128]{1,0:T(8,128)S(1)}, u32[]{:S(2)}, u32[]{:S(2)}) collective-permute-start(f32[16,128]{1,0:T(8,128)S(1)} %get-tuple-element.31), channel_id=1, source_target_pairs={{0,9},{1,8},{2,11},{3,10},{4,13},{5,12},{6,15},{7,14},{8,1},{9,0},... | collective-permute-start | bytes 24584 | tf_op jit(solution)/shard_map/ppermute | solution.py:20
  18.9 0.0 collective-permute-done.7.refs_1_
  18.9 0.0 copy-done
  18.9 0.4 %split.1 = (bf16[2048,256]{1,0:T(8,128)(2,1)S(1)}, f32[1,128]{1,0:T(1,128)S(1)}) custom-call(f32[64,2048]{1,0:T(8,128)S(1)} %copy-done, f32[64,2048]{1,0:T(8,128)S(1)} %collective-permute-done.7.refs_1_), custom_call_target="tpu_custom_call" | custom-call | bytes 1048576 | tf_op jit(solution)/shard_map/split/pallas_call | solution.py:314
  19.3 1.4 %collective-permute-done.6.other = f32[16,128]{1,0:T(8,128)S(1)} collective-permute-done((f32[16,128]{1,0:T(8,128)S(1)}, f32[16,128]{1,0:T(8,128)S(1)}, u32[]{:S(2)}, u32[]{:S(2)}) %collective-permute-start.6) | collective-permute-done | bytes 8224 | tf_op jit(solution)/shard_map/ppermute | solution.py:20
  20.7 0.3 score.1
  21.0 2.3 %collective-permute-start.8 = (f32[8,128]{1,0:T(8,128)S(1)}, f32[8,128]{1,0:T(8,128)S(1)}, u32[]{:S(2)}, u32[]{:S(2)}) collective-permute-start(f32[8,128]{1,0:T(8,128)S(1)} %get-tuple-element.35), channel_id=1, source_target_pairs={{0,9},{1,8},{2,11},{3,10},{4,13},{5,12},{6,15},{7,14},{8,1},{9,0},... | collective-permute-start | bytes 12296 | tf_op jit(solution)/shard_map/ppermute | solution.py:20
  23.3 1.6 %collective-permute-done.8.remote = f32[8,128]{1,0:T(8,128)S(1)} collective-permute-done((f32[8,128]{1,0:T(8,128)S(1)}, f32[8,128]{1,0:T(8,128)S(1)}, u32[]{:S(2)}, u32[]{:S(2)}) %collective-permute-start.8) | collective-permute-done | bytes 4128 | tf_op jit(solution)/shard_map/ppermute | solution.py:20
  24.9 0.7 %collective-permute-start.10 = (f32[8,128]{1,0:T(8,128)S(1)}, f32[8,128]{1,0:T(8,128)S(1)}, u32[]{:S(2)}, u32[]{:S(2)}) collective-permute-start(f32[8,128]{1,0:T(8,128)S(1)} %get-tuple-element.38), channel_id=1, source_target_pairs={{0,2},{1,3},{2,0},{3,1},{4,6},{5,7},{6,4},{7,5},{8,10},{9,11},{10,... | collective-permute-start | bytes 12296 | tf_op jit(solution)/shard_map/ppermute | solution.py:45
  25.6 0.8 %collective-permute-start.11 = (f32[8,128]{1,0:T(8,128)S(1)}, f32[8,128]{1,0:T(8,128)S(1)}, u32[]{:S(2)}, u32[]{:S(2)}) collective-permute-start(f32[8,128]{1,0:T(8,128)S(1)} %get-tuple-element.39), channel_id=1, source_target_pairs={{0,3},{1,2},{2,1},{3,0},{4,7},{5,6},{6,5},{7,4},{8,11},{9,10},{10,... | collective-permute-start | bytes 12296 | tf_op jit(solution)/shard_map/ppermute | solution.py:45
  26.4 0.7 %collective-permute-start.9 = (f32[8,128]{1,0:T(8,128)S(1)}, f32[8,128]{1,0:T(8,128)S(1)}, u32[]{:S(2)}, u32[]{:S(2)}) collective-permute-start(f32[8,128]{1,0:T(8,128)S(1)} %get-tuple-element.37), channel_id=1, source_target_pairs={{0,1},{1,0},{2,3},{3,2},{4,5},{5,4},{6,7},{7,6},{8,9},{9,8},{10,11... | collective-permute-start | bytes 12296 | tf_op jit(solution)/shard_map/ppermute | solution.py:45
  27.1 1.5 %collective-permute-done.10.refs_2_ = f32[8,128]{1,0:T(8,128)S(1)} collective-permute-done((f32[8,128]{1,0:T(8,128)S(1)}, f32[8,128]{1,0:T(8,128)S(1)}, u32[]{:S(2)}, u32[]{:S(2)}) %collective-permute-start.10) | collective-permute-done | bytes 4128 | tf_op jit(solution)/shard_map/ppermute | solution.py:45
  28.5 0.1 collective-permute-done.11.refs_3_
  28.6 0.0 collective-permute-done.9.refs_1_
  28.6 0.7 %last.1 = (f32[1,2048]{1,0:T(1,128)}, f32[1,64]{1,0:T(1,128)}) custom-call(f32[16,128]{1,0:T(8,128)S(1)} %get-tuple-element.30.own, f32[8,128]{1,0:T(8,128)S(1)} %get-tuple-element.36.refs_0_, f32[8,128]{1,0:T(8,128)S(1)} %collective-permute-done.9.refs_1_, f32[8,128]{1,0:T(8,128)S(1)} %collective-permute-done.10.refs_2_, ...), custom_call_target="tpu_custom_call" | custom-call | tf_op jit(solution)/shard_map/last/pallas_call | solution.py:356
  (2 shorter events, 0.0 us)
Async XLA Ops:
  0.6 18.3 %collective-permute-start.7 = (f32[64,2048]{1,0:T(8,128)}, f32[64,2048]{1,0:T(8,128)S(1)}, u32[]{:S(2)}, u32[]{:S(2)}) collective-permute-start(f32[64,2048]{1,0:T(8,128)} %refs_0_.1), channel_id=1, source_target_pairs={{0,4},{4,0},{8,12},{12,8},{1,5},{5,1},{9,13},{13,9},{2,6},{6,2},{1... | collective-permute-start | bytes 1572872 | tf_op jit(solution)/shard_map/ppermute | solution.py:45
  3.7 5.0 %copy-start.1 = (s32[2,2,32,1280]{3,2,1,0:T(8,128)S(1)}, s32[2,2,32,1280]{3,2,1,0:T(8,128)}, u32[]{:S(2)}) copy-start(s32[2,2,32,1280]{3,2,1,0:T(8,128)} %words.1) | copy-start | bytes 1966084
  6.8 4.5 %collective-permute-start = (f32[16,256]{1,0:T(8,128)S(1)}, f32[16,256]{1,0:T(8,128)S(1)}, u32[]{:S(2)}, u32[]{:S(2)}) collective-permute-start(f32[16,256]{1,0:T(8,128)S(1)} %get-tuple-element.21.own), channel_id=1, source_target_pairs={{0,3},{1,2},{2,1},{3,0},{4,7},{5,6},{6,5},{7,4},{8,11},{9,10},{10,... | collective-permute-start | bytes 49160 | tf_op jit(solution)/shard_map/ppermute | solution.py:45
  7.5 3.9 %collective-permute-start.1 = (f32[16,256]{1,0:T(8,128)S(1)}, f32[16,256]{1,0:T(8,128)S(1)}, u32[]{:S(2)}, u32[]{:S(2)}) collective-permute-start(f32[16,256]{1,0:T(8,128)S(1)} %get-tuple-element.21.own), channel_id=1, source_target_pairs={{0,2},{1,3},{2,0},{3,1},{4,6},{5,7},{6,4},{7,5},{8,10},{9,11},{10,... | collective-permute-start | bytes 49160 | tf_op jit(solution)/shard_map/ppermute | solution.py:45
  8.4 3.0 %collective-permute-start.2 = (f32[16,256]{1,0:T(8,128)S(1)}, f32[16,256]{1,0:T(8,128)S(1)}, u32[]{:S(2)}, u32[]{:S(2)}) collective-permute-start(f32[16,256]{1,0:T(8,128)S(1)} %get-tuple-element.21.own), channel_id=1, source_target_pairs={{0,1},{1,0},{2,3},{3,2},{4,5},{5,4},{6,7},{7,6},{8,9},{9,8},{10,11... | collective-permute-start | bytes 49160 | tf_op jit(solution)/shard_map/ppermute | solution.py:45
  10.6 8.3 %copy-start = (f32[64,2048]{1,0:T(8,128)S(1)}, f32[64,2048]{1,0:T(8,128)}, u32[]{:S(2)}) copy-start(f32[64,2048]{1,0:T(8,128)} %refs_0_.1) | copy-start | bytes 1572868
  11.9 3.8 %collective-permute-start.3 = (f32[2,16,128]{2,1,0:T(8,128)S(1)}, f32[2,16,128]{2,1,0:T(8,128)S(1)}, u32[]{:S(2)}, u32[]{:S(2)}) collective-permute-start(f32[2,16,128]{2,1,0:T(8,128)S(1)} %get-tuple-element.27), channel_id=1, source_target_pairs={{0,2},{1,3},{2,0},{3,1},{4,6},{5,7},{6,4},{7,5},{8,10},{9,11},{10,... | collective-permute-start | bytes 49160 | tf_op jit(solution)/shard_map/ppermute | solution.py:45
  13.4 3.2 %collective-permute-start.4 = (f32[2,16,128]{2,1,0:T(8,128)S(1)}, f32[2,16,128]{2,1,0:T(8,128)S(1)}, u32[]{:S(2)}, u32[]{:S(2)}) collective-permute-start(f32[2,16,128]{2,1,0:T(8,128)S(1)} %get-tuple-element.28), channel_id=1, source_target_pairs={{0,3},{1,2},{2,1},{3,0},{4,7},{5,6},{6,5},{7,4},{8,11},{9,10},{10,... | collective-permute-start | bytes 49160 | tf_op jit(solution)/shard_map/ppermute | solution.py:45
  13.4 3.2 %collective-permute-start.5 = (f32[2,16,128]{2,1,0:T(8,128)S(1)}, f32[2,16,128]{2,1,0:T(8,128)S(1)}, u32[]{:S(2)}, u32[]{:S(2)}) collective-permute-start(f32[2,16,128]{2,1,0:T(8,128)S(1)} %get-tuple-element.29), channel_id=1, source_target_pairs={{0,1},{1,0},{2,3},{3,2},{4,5},{5,4},{6,7},{7,6},{8,9},{9,8},{10,11... | collective-permute-start | bytes 49160 | tf_op jit(solution)/shard_map/ppermute | solution.py:45
  16.6 4.0 %collective-permute-start.6 = (f32[16,128]{1,0:T(8,128)S(1)}, f32[16,128]{1,0:T(8,128)S(1)}, u32[]{:S(2)}, u32[]{:S(2)}) collective-permute-start(f32[16,128]{1,0:T(8,128)S(1)} %get-tuple-element.31), channel_id=1, source_target_pairs={{0,9},{1,8},{2,11},{3,10},{4,13},{5,12},{6,15},{7,14},{8,1},{9,0},... | collective-permute-start | bytes 24584 | tf_op jit(solution)/shard_map/ppermute | solution.py:20
  21.0 4.0 %collective-permute-start.8 = (f32[8,128]{1,0:T(8,128)S(1)}, f32[8,128]{1,0:T(8,128)S(1)}, u32[]{:S(2)}, u32[]{:S(2)}) collective-permute-start(f32[8,128]{1,0:T(8,128)S(1)} %get-tuple-element.35), channel_id=1, source_target_pairs={{0,9},{1,8},{2,11},{3,10},{4,13},{5,12},{6,15},{7,14},{8,1},{9,0},... | collective-permute-start | bytes 12296 | tf_op jit(solution)/shard_map/ppermute | solution.py:20
  24.9 3.6 %collective-permute-start.10 = (f32[8,128]{1,0:T(8,128)S(1)}, f32[8,128]{1,0:T(8,128)S(1)}, u32[]{:S(2)}, u32[]{:S(2)}) collective-permute-start(f32[8,128]{1,0:T(8,128)S(1)} %get-tuple-element.38), channel_id=1, source_target_pairs={{0,2},{1,3},{2,0},{3,1},{4,6},{5,7},{6,4},{7,5},{8,10},{9,11},{10,... | collective-permute-start | bytes 12296 | tf_op jit(solution)/shard_map/ppermute | solution.py:45
  25.6 3.0 %collective-permute-start.11 = (f32[8,128]{1,0:T(8,128)S(1)}, f32[8,128]{1,0:T(8,128)S(1)}, u32[]{:S(2)}, u32[]{:S(2)}) collective-permute-start(f32[8,128]{1,0:T(8,128)S(1)} %get-tuple-element.39), channel_id=1, source_target_pairs={{0,3},{1,2},{2,1},{3,0},{4,7},{5,6},{6,5},{7,4},{8,11},{9,10},{10,... | collective-permute-start | bytes 12296 | tf_op jit(solution)/shard_map/ppermute | solution.py:45
  26.4 2.2 %collective-permute-start.9 = (f32[8,128]{1,0:T(8,128)S(1)}, f32[8,128]{1,0:T(8,128)S(1)}, u32[]{:S(2)}, u32[]{:S(2)}) collective-permute-start(f32[8,128]{1,0:T(8,128)S(1)} %get-tuple-element.37), channel_id=1, source_target_pairs={{0,1},{1,0},{2,3},{3,2},{4,5},{5,4},{6,7},{7,6},{8,9},{9,8},{10,11... | collective-permute-start | bytes 12296 | tf_op jit(solution)/shard_map/ppermute | solution.py:45

commit v9 on v8

--- a/solution.py
+++ b/solution.py
@@ -341,7 +341,7 @@
             "sketch",
             8,
         )(*inputs)
-        received = [shift(blocks[s], "col", cols, s) for s in (2, 3, 1)]
+        received = [shift(blocks[s], "col", cols, s) for s in STEPS]
         own, pair = call(sum_kernel, [shape] * 2, [VMEM] * cols, "own", 2)(blocks[0], *received)
         other = crossed(pair, exs, cols)
         line = jax.ShapeDtypeStruct((8, lanes), f32)

time: 29.5 us -> 29.5 us (level)
    ppermute x10, waiting for transfers between devices: 4.19 us -> 4.59 us  [shift(): lax.ppermute(x, axis, [(i, partner(i, step, count)) for i in range(count)])]
  transfers between devices with their start and end apart: 12 -> 12, of which waited for: 7 -> 7; matrix products, arithmetic and copies ran while one was open for 0% -> 0% of each run, Pallas kernels for 20% -> 19%
where the time goes in v9:
time: 29.5 us; the launch traced here: 29.4 us
  starting transfers between devices  13.8 us (47%)
  waiting for transfers between devices  7.44 us (25%)
  Pallas kernels  6.68 us (23%)
  between operations  1.39 us (5%)
    ppermute x10, starting transfers between devices, shift(): lax.ppermute(x, axis, [(i, partner(i, step, count)) for i in range(count)])  9.11 us
    ppermute x2, starting transfers between devices, crossed(): return lax.ppermute(x, ('ex', 'col'), pairs)  4.73 us
    ppermute x10, waiting for transfers between devices, shift(): lax.ppermute(x, axis, [(i, partner(i, step, count)) for i in range(count)])  4.59 us
    pallas_call x1, Pallas kernels, on_device(): call(mix_kernel, [jax.ShapeDtypeStruct((layers * 2 * m, seq), f32), rows,...  3.03 us
    ppermute x2, waiting for transfers between devices, crossed(): return lax.ppermute(x, ('ex', 'col'), pairs)  2.85 us
    pallas_call x1, Pallas kernels, on_device(): call(sign_kernel, [signed, signed], [VMEM] * 3, 'sign', 8, [pltpu.VMEM((2...  1.88 us
    pallas_call x1, Pallas kernels, on_device(): call(last, results, [VMEM] * (1 + len(parts)), 'last', 2)(own, *parts)  0.66 us
  transfers between devices with their start and end apart: 12, of which 7 were waited for; matrix products, arithmetic and copies ran while one was open for 0% of the time, Pallas kernels for 19%

profile of v9, /device:TPU:0, one launch (start us, length us, event | category | flops | bytes accessed | tf_op | source)
XLA Modules:
  0.0 29.4 jit_solution(10352774592783089264)
XLA Ops:
  0.6 3.1 %collective-permute-start.7 = (f32[64,2048]{1,0:T(8,128)}, f32[64,2048]{1,0:T(8,128)S(1)}, u32[]{:S(2)}, u32[]{:S(2)}) collective-permute-start(f32[64,2048]{1,0:T(8,128)} %refs_0_.1), channel_id=1, source_target_pairs={{0,4},{4,0},{8,12},{12,8},{1,5},{5,1},{9,13},{13,9},{2,6},{6,2},{1... | collective-permute-start | bytes 1572872 | tf_op jit(solution)/shard_map/ppermute | solution.py:45
  3.7 0.0 copy-start.1
  3.8 3.0 %mix.1 = (f32[16,256]{1,0:T(8,128)S(1)}, bf16[1,2,256,1280]{3,2,1,0:T(8,128)(2,1)S(1)}, bf16[1,2,256,1280]{3,2,1,0:T(8,128)(2,1)S(1)}) custom-call(s32[2,2,4,128]{3,2,1,0:T(4,128)} %bitcast.3, bf16[1,2,256,1280]{3,2,1,0:T(8,128)(2,1)} %hidden.1, bf16[1,2,256,1280]{3,2,1,0:T(8,128)(2,1)} %grad.1, bf16[2,128,1280]{2,1,0:T(8,128)(2,1)} %down.1, ...), custom_call_target="tpu_custom_call" | custom-call | flops 335544320 | bytes 4194304 | tf_op jit(solution)/shard_map/mix/pallas_call | solution.py:284
  6.8 0.7 %collective-permute-start = (f32[16,256]{1,0:T(8,128)S(1)}, f32[16,256]{1,0:T(8,128)S(1)}, u32[]{:S(2)}, u32[]{:S(2)}) collective-permute-start(f32[16,256]{1,0:T(8,128)S(1)} %get-tuple-element.21.own), channel_id=1, source_target_pairs={{0,3},{1,2},{2,1},{3,0},{4,7},{5,6},{6,5},{7,4},{8,11},{9,10},{10,... | collective-permute-start | bytes 49160 | tf_op jit(solution)/shard_map/ppermute | solution.py:45
  7.5 0.9 %collective-permute-start.1 = (f32[16,256]{1,0:T(8,128)S(1)}, f32[16,256]{1,0:T(8,128)S(1)}, u32[]{:S(2)}, u32[]{:S(2)}) collective-permute-start(f32[16,256]{1,0:T(8,128)S(1)} %get-tuple-element.21.own), channel_id=1, source_target_pairs={{0,2},{1,3},{2,0},{3,1},{4,6},{5,7},{6,4},{7,5},{8,10},{9,11},{10,... | collective-permute-start | bytes 49160 | tf_op jit(solution)/shard_map/ppermute | solution.py:45
  8.4 0.3 collective-permute-start.2
  8.7 0.0 copy-done.1
  8.7 1.9 %sign.1 = (bf16[2,2,256,512]{3,2,1,0:T(8,128)(2,1)S(1)}, bf16[2,2,256,512]{3,2,1,0:T(8,128)(2,1)S(1)}) custom-call(s32[2,2,32,1280]{3,2,1,0:T(8,128)S(1)} %copy-done.1, bf16[1,2,256,1280]{3,2,1,0:T(8,128)(2,1)S(1)} %get-tuple-element.22.hidden, bf16[1,2,256,1280]{3,2,1,0:T(8,128)(2,1)S(1)} %get-tuple-element.23.grad), custom_call_target="tpu_custom_call" | custom-call | flops 1342177280 | bytes 6291456 | tf_op jit(solution)/shard_map/sign/pallas_call | solution.py:301
  10.6 0.0 copy-start
  11.3 0.0 collective-permute-done.refs_0_
  11.3 0.1 collective-permute-done.1.refs_1_
  11.4 0.0 collective-permute-done.2.refs_2_
  11.4 0.4 %sketch.1 = (f32[2,16,128]{2,1,0:T(8,128)S(1)}, f32[2,16,128]{2,1,0:T(8,128)S(1)}, f32[2,16,128]{2,1,0:T(8,128)S(1)}, f32[2,16,128]{2,1,0:T(8,128)S(1)}) custom-call(s32[1,1]{1,0:T(1,128)} %bitcast.2.length, f32[16,256]{1,0:T(8,128)S(1)} %get-tuple-element.21.own, f32[16,256]{1,0:T(8,128)S(1)} %collective-permute-done.refs_0_, ...), custom_call_target="tpu_custom_call" | custom-call | tf_op jit(solution)/shard_map/sketch/pallas_call | solution.py:337
  11.9 0.2 collective-permute-start.3
  12.1 1.4 %collective-permute-start.4 = (f32[2,16,128]{2,1,0:T(8,128)S(1)}, f32[2,16,128]{2,1,0:T(8,128)S(1)}, u32[]{:S(2)}, u32[]{:S(2)}) collective-permute-start(f32[2,16,128]{2,1,0:T(8,128)S(1)} %get-tuple-element.28), channel_id=1, source_target_pairs={{0,2},{1,3},{2,0},{3,1},{4,6},{5,7},{6,4},{7,5},{8,10},{9,11},{10,... | collective-permute-start | bytes 49160 | tf_op jit(solution)/shard_map/ppermute | solution.py:45
  13.4 0.3 %collective-permute-start.5 = (f32[2,16,128]{2,1,0:T(8,128)S(1)}, f32[2,16,128]{2,1,0:T(8,128)S(1)}, u32[]{:S(2)}, u32[]{:S(2)}) collective-permute-start(f32[2,16,128]{2,1,0:T(8,128)S(1)} %get-tuple-element.29), channel_id=1, source_target_pairs={{0,3},{1,2},{2,1},{3,0},{4,7},{5,6},{6,5},{7,4},{8,11},{9,10},{10,... | collective-permute-start | bytes 49160 | tf_op jit(solution)/shard_map/ppermute | solution.py:45
  13.8 0.0 collective-permute-done.3.refs_1_
  13.8 2.0 %collective-permute-done.4.refs_2_ = f32[2,16,128]{2,1,0:T(8,128)S(1)} collective-permute-done((f32[2,16,128]{2,1,0:T(8,128)S(1)}, f32[2,16,128]{2,1,0:T(8,128)S(1)}, u32[]{:S(2)}, u32[]{:S(2)}) %collective-permute-start.4) | collective-permute-done | bytes 16416 | tf_op jit(solution)/shard_map/ppermute | solution.py:45
  15.8 0.8 %collective-permute-done.5.refs_3_ = f32[2,16,128]{2,1,0:T(8,128)S(1)} collective-permute-done((f32[2,16,128]{2,1,0:T(8,128)S(1)}, f32[2,16,128]{2,1,0:T(8,128)S(1)}, u32[]{:S(2)}, u32[]{:S(2)}) %collective-permute-start.5) | collective-permute-done | bytes 16416 | tf_op jit(solution)/shard_map/ppermute | solution.py:45
  16.6 2.3 %collective-permute-start.6 = (f32[16,128]{1,0:T(8,128)S(1)}, f32[16,128]{1,0:T(8,128)S(1)}, u32[]{:S(2)}, u32[]{:S(2)}) collective-permute-start(f32[16,128]{1,0:T(8,128)S(1)} %get-tuple-element.31), channel_id=1, source_target_pairs={{0,9},{1,8},{2,11},{3,10},{4,13},{5,12},{6,15},{7,14},{8,1},{9,0},... | collective-permute-start | bytes 24584 | tf_op jit(solution)/shard_map/ppermute | solution.py:20
  19.0 0.0 collective-permute-done.7.refs_1_
  19.0 0.0 copy-done
  19.0 0.4 %split.1 = (bf16[2048,256]{1,0:T(8,128)(2,1)S(1)}, f32[1,128]{1,0:T(1,128)S(1)}) custom-call(f32[64,2048]{1,0:T(8,128)S(1)} %copy-done, f32[64,2048]{1,0:T(8,128)S(1)} %collective-permute-done.7.refs_1_), custom_call_target="tpu_custom_call" | custom-call | bytes 1048576 | tf_op jit(solution)/shard_map/split/pallas_call | solution.py:314
  19.3 1.3 %collective-permute-done.6.other = f32[16,128]{1,0:T(8,128)S(1)} collective-permute-done((f32[16,128]{1,0:T(8,128)S(1)}, f32[16,128]{1,0:T(8,128)S(1)}, u32[]{:S(2)}, u32[]{:S(2)}) %collective-permute-start.6) | collective-permute-done | bytes 8224 | tf_op jit(solution)/shard_map/ppermute | solution.py:20
  20.6 0.3 score.1
  20.9 2.4 %collective-permute-start.8 = (f32[8,128]{1,0:T(8,128)S(1)}, f32[8,128]{1,0:T(8,128)S(1)}, u32[]{:S(2)}, u32[]{:S(2)}) collective-permute-start(f32[8,128]{1,0:T(8,128)S(1)} %get-tuple-element.35), channel_id=1, source_target_pairs={{0,9},{1,8},{2,11},{3,10},{4,13},{5,12},{6,15},{7,14},{8,1},{9,0},... | collective-permute-start | bytes 12296 | tf_op jit(solution)/shard_map/ppermute | solution.py:20
  23.3 1.6 %collective-permute-done.8.remote = f32[8,128]{1,0:T(8,128)S(1)} collective-permute-done((f32[8,128]{1,0:T(8,128)S(1)}, f32[8,128]{1,0:T(8,128)S(1)}, u32[]{:S(2)}, u32[]{:S(2)}) %collective-permute-start.8) | collective-permute-done | bytes 4128 | tf_op jit(solution)/shard_map/ppermute | solution.py:20
  24.9 0.8 %collective-permute-start.10 = (f32[8,128]{1,0:T(8,128)S(1)}, f32[8,128]{1,0:T(8,128)S(1)}, u32[]{:S(2)}, u32[]{:S(2)}) collective-permute-start(f32[8,128]{1,0:T(8,128)S(1)} %get-tuple-element.38), channel_id=1, source_target_pairs={{0,2},{1,3},{2,0},{3,1},{4,6},{5,7},{6,4},{7,5},{8,10},{9,11},{10,... | collective-permute-start | bytes 12296 | tf_op jit(solution)/shard_map/ppermute | solution.py:45
  25.7 0.7 %collective-permute-start.11 = (f32[8,128]{1,0:T(8,128)S(1)}, f32[8,128]{1,0:T(8,128)S(1)}, u32[]{:S(2)}, u32[]{:S(2)}) collective-permute-start(f32[8,128]{1,0:T(8,128)S(1)} %get-tuple-element.39), channel_id=1, source_target_pairs={{0,3},{1,2},{2,1},{3,0},{4,7},{5,6},{6,5},{7,4},{8,11},{9,10},{10,... | collective-permute-start | bytes 12296 | tf_op jit(solution)/shard_map/ppermute | solution.py:45
  26.4 0.6 %collective-permute-start.9 = (f32[8,128]{1,0:T(8,128)S(1)}, f32[8,128]{1,0:T(8,128)S(1)}, u32[]{:S(2)}, u32[]{:S(2)}) collective-permute-start(f32[8,128]{1,0:T(8,128)S(1)} %get-tuple-element.37), channel_id=1, source_target_pairs={{0,1},{1,0},{2,3},{3,2},{4,5},{5,4},{6,7},{7,6},{8,9},{9,8},{10,11... | collective-permute-start | bytes 12296 | tf_op jit(solution)/shard_map/ppermute | solution.py:45
  27.0 1.5 %collective-permute-done.10.refs_2_ = f32[8,128]{1,0:T(8,128)S(1)} collective-permute-done((f32[8,128]{1,0:T(8,128)S(1)}, f32[8,128]{1,0:T(8,128)S(1)}, u32[]{:S(2)}, u32[]{:S(2)}) %collective-permute-start.10) | collective-permute-done | bytes 4128 | tf_op jit(solution)/shard_map/ppermute | solution.py:45
  28.5 0.2 collective-permute-done.11.refs_3_
  28.7 0.0 collective-permute-done.9.refs_1_
  28.7 0.7 %last.1 = (f32[1,2048]{1,0:T(1,128)}, f32[1,64]{1,0:T(1,128)}) custom-call(f32[16,128]{1,0:T(8,128)S(1)} %get-tuple-element.30.own, f32[8,128]{1,0:T(8,128)S(1)} %get-tuple-element.36.refs_0_, f32[8,128]{1,0:T(8,128)S(1)} %collective-permute-done.9.refs_1_, f32[8,128]{1,0:T(8,128)S(1)} %collective-permute-done.10.refs_2_, ...), custom_call_target="tpu_custom_call" | custom-call | tf_op jit(solution)/shard_map/last/pallas_call | solution.py:356
  (2 shorter events, 0.0 us)
Async XLA Ops:
  0.6 18.3 %collective-permute-start.7 = (f32[64,2048]{1,0:T(8,128)}, f32[64,2048]{1,0:T(8,128)S(1)}, u32[]{:S(2)}, u32[]{:S(2)}) collective-permute-start(f32[64,2048]{1,0:T(8,128)} %refs_0_.1), channel_id=1, source_target_pairs={{0,4},{4,0},{8,12},{12,8},{1,5},{5,1},{9,13},{13,9},{2,6},{6,2},{1... | collective-permute-start | bytes 1572872 | tf_op jit(solution)/shard_map/ppermute | solution.py:45
  3.7 5.0 %copy-start.1 = (s32[2,2,32,1280]{3,2,1,0:T(8,128)S(1)}, s32[2,2,32,1280]{3,2,1,0:T(8,128)}, u32[]{:S(2)}) copy-start(s32[2,2,32,1280]{3,2,1,0:T(8,128)} %words.1) | copy-start | bytes 1966084
  6.8 4.5 %collective-permute-start = (f32[16,256]{1,0:T(8,128)S(1)}, f32[16,256]{1,0:T(8,128)S(1)}, u32[]{:S(2)}, u32[]{:S(2)}) collective-permute-start(f32[16,256]{1,0:T(8,128)S(1)} %get-tuple-element.21.own), channel_id=1, source_target_pairs={{0,3},{1,2},{2,1},{3,0},{4,7},{5,6},{6,5},{7,4},{8,11},{9,10},{10,... | collective-permute-start | bytes 49160 | tf_op jit(solution)/shard_map/ppermute | solution.py:45
  7.5 3.9 %collective-permute-start.1 = (f32[16,256]{1,0:T(8,128)S(1)}, f32[16,256]{1,0:T(8,128)S(1)}, u32[]{:S(2)}, u32[]{:S(2)}) collective-permute-start(f32[16,256]{1,0:T(8,128)S(1)} %get-tuple-element.21.own), channel_id=1, source_target_pairs={{0,2},{1,3},{2,0},{3,1},{4,6},{5,7},{6,4},{7,5},{8,10},{9,11},{10,... | collective-permute-start | bytes 49160 | tf_op jit(solution)/shard_map/ppermute | solution.py:45
  8.4 3.0 %collective-permute-start.2 = (f32[16,256]{1,0:T(8,128)S(1)}, f32[16,256]{1,0:T(8,128)S(1)}, u32[]{:S(2)}, u32[]{:S(2)}) collective-permute-start(f32[16,256]{1,0:T(8,128)S(1)} %get-tuple-element.21.own), channel_id=1, source_target_pairs={{0,1},{1,0},{2,3},{3,2},{4,5},{5,4},{6,7},{7,6},{8,9},{9,8},{10,11... | collective-permute-start | bytes 49160 | tf_op jit(solution)/shard_map/ppermute | solution.py:45
  10.6 8.4 %copy-start = (f32[64,2048]{1,0:T(8,128)S(1)}, f32[64,2048]{1,0:T(8,128)}, u32[]{:S(2)}) copy-start(f32[64,2048]{1,0:T(8,128)} %refs_0_.1) | copy-start | bytes 1572868
  11.9 1.9 %collective-permute-start.3 = (f32[2,16,128]{2,1,0:T(8,128)S(1)}, f32[2,16,128]{2,1,0:T(8,128)S(1)}, u32[]{:S(2)}, u32[]{:S(2)}) collective-permute-start(f32[2,16,128]{2,1,0:T(8,128)S(1)} %get-tuple-element.27), channel_id=1, source_target_pairs={{0,1},{1,0},{2,3},{3,2},{4,5},{5,4},{6,7},{7,6},{8,9},{9,8},{10,11... | collective-permute-start | bytes 49160 | tf_op jit(solution)/shard_map/ppermute | solution.py:45
  12.1 3.7 %collective-permute-start.4 = (f32[2,16,128]{2,1,0:T(8,128)S(1)}, f32[2,16,128]{2,1,0:T(8,128)S(1)}, u32[]{:S(2)}, u32[]{:S(2)}) collective-permute-start(f32[2,16,128]{2,1,0:T(8,128)S(1)} %get-tuple-element.28), channel_id=1, source_target_pairs={{0,2},{1,3},{2,0},{3,1},{4,6},{5,7},{6,4},{7,5},{8,10},{9,11},{10,... | collective-permute-start | bytes 49160 | tf_op jit(solution)/shard_map/ppermute | solution.py:45
  13.4 3.2 %collective-permute-start.5 = (f32[2,16,128]{2,1,0:T(8,128)S(1)}, f32[2,16,128]{2,1,0:T(8,128)S(1)}, u32[]{:S(2)}, u32[]{:S(2)}) collective-permute-start(f32[2,16,128]{2,1,0:T(8,128)S(1)} %get-tuple-element.29), channel_id=1, source_target_pairs={{0,3},{1,2},{2,1},{3,0},{4,7},{5,6},{6,5},{7,4},{8,11},{9,10},{10,... | collective-permute-start | bytes 49160 | tf_op jit(solution)/shard_map/ppermute | solution.py:45
  16.6 4.0 %collective-permute-start.6 = (f32[16,128]{1,0:T(8,128)S(1)}, f32[16,128]{1,0:T(8,128)S(1)}, u32[]{:S(2)}, u32[]{:S(2)}) collective-permute-start(f32[16,128]{1,0:T(8,128)S(1)} %get-tuple-element.31), channel_id=1, source_target_pairs={{0,9},{1,8},{2,11},{3,10},{4,13},{5,12},{6,15},{7,14},{8,1},{9,0},... | collective-permute-start | bytes 24584 | tf_op jit(solution)/shard_map/ppermute | solution.py:20
  20.9 4.0 %collective-permute-start.8 = (f32[8,128]{1,0:T(8,128)S(1)}, f32[8,128]{1,0:T(8,128)S(1)}, u32[]{:S(2)}, u32[]{:S(2)}) collective-permute-start(f32[8,128]{1,0:T(8,128)S(1)} %get-tuple-element.35), channel_id=1, source_target_pairs={{0,9},{1,8},{2,11},{3,10},{4,13},{5,12},{6,15},{7,14},{8,1},{9,0},... | collective-permute-start | bytes 12296 | tf_op jit(solution)/shard_map/ppermute | solution.py:20
  24.9 3.6 %collective-permute-start.10 = (f32[8,128]{1,0:T(8,128)S(1)}, f32[8,128]{1,0:T(8,128)S(1)}, u32[]{:S(2)}, u32[]{:S(2)}) collective-permute-start(f32[8,128]{1,0:T(8,128)S(1)} %get-tuple-element.38), channel_id=1, source_target_pairs={{0,2},{1,3},{2,0},{3,1},{4,6},{5,7},{6,4},{7,5},{8,10},{9,11},{10,... | collective-permute-start | bytes 12296 | tf_op jit(solution)/shard_map/ppermute | solution.py:45
  25.7 3.0 %collective-permute-start.11 = (f32[8,128]{1,0:T(8,128)S(1)}, f32[8,128]{1,0:T(8,128)S(1)}, u32[]{:S(2)}, u32[]{:S(2)}) collective-permute-start(f32[8,128]{1,0:T(8,128)S(1)} %get-tuple-element.39), channel_id=1, source_target_pairs={{0,3},{1,2},{2,1},{3,0},{4,7},{5,6},{6,5},{7,4},{8,11},{9,10},{10,... | collective-permute-start | bytes 12296 | tf_op jit(solution)/shard_map/ppermute | solution.py:45
  26.4 2.3 %collective-permute-start.9 = (f32[8,128]{1,0:T(8,128)S(1)}, f32[8,128]{1,0:T(8,128)S(1)}, u32[]{:S(2)}, u32[]{:S(2)}) collective-permute-start(f32[8,128]{1,0:T(8,128)S(1)} %get-tuple-element.37), channel_id=1, source_target_pairs={{0,1},{1,0},{2,3},{3,2},{4,5},{5,4},{6,7},{7,6},{8,9},{9,8},{10,11... | collective-permute-start | bytes 12296 | tf_op jit(solution)/shard_map/ppermute | solution.py:45
